TPU v7x, 512 devices: a whole 4x4x16 slice. The times are simulated.
512 devices in a mesh: seq: 16 (over x, y_hi, core), shard: 32 (over y_lo, z).
Axes of the slice: x: 4, y: 4 (y_hi: 2, y_lo: 2; y = y_hi * 2 + y_lo), z: 16, core: 2. Of those that a mesh axis runs over, the one named last changes fastest.
Arguments:
- features: bfloat16 [4096, 4096], P('seq', 'shard'), may hold values from -6 to 6
- in_proj: bfloat16 [4096, 3, 4096], P(None, None, 'shard'), may hold values from -0.09375 to 0.09375
- short_filter: float32 [3, 3, 4096], replicated, may hold values from -3.5 to 3.5
- residue: float32 [16, 4096], P(None, 'shard'), may hold values from -1.5 to 1.5
- decay_rate: float32 [16, 4096], P(None, 'shard'), may hold values from 0.05 to 1000
- skip_gain: float32 [4096], P('shard'), may hold values from -4 to 4
Outputs:
- gated: bfloat16 [4096, 4096], P('seq', 'shard')
All inputs are finite; a program needn't handle non-finite values.
Results may differ from a plain program's by a relative error of at most 0.0063.
Values may be sent and summed in bfloat16 or wider, within the bound.
No kernel may reach another device: no remote copies, remote signals or barrier semaphores. Data moves between devices by JAX's collectives and lax.ppermute only.
A program may use at most 64 MiB of HBM per device.

v0:
```python
import math

import jax
import jax.numpy as jnp
from jax import lax
from jax.sharding import PartitionSpec as P


def shifted(value, axis, steps):
    count = lax.axis_size(axis)
    initial, last = (max(0, -steps), min(count, count - steps))
    return lax.ppermute(value, axis, [(source, source + steps) for source in range(initial, last)])


def mode_tables(residue, decay_rate, total_len, block_len):
    step_rate = decay_rate / total_len
    mode_gain = residue * jnp.sqrt(jnp.expm1(-2.0 * step_rate) / jnp.expm1(-2.0 * decay_rate))
    steps = jnp.arange(block_len, dtype=jnp.float32)[:, None, None]
    lagged = jnp.exp(-step_rate * steps)
    kernel = jnp.sum(mode_gain * lagged, axis=1)
    offsets = jnp.arange(block_len)[:, None] - jnp.arange(block_len)[None, :]
    toeplitz = jnp.where(
        (offsets >= 0)[:, :, None], kernel[jnp.clip(offsets, 0, block_len - 1)], 0.0
    )
    head_table = mode_gain * jnp.exp(-step_rate * (steps + 1.0))
    tail_table = jnp.exp(-step_rate * (block_len - 1.0 - steps))
    step_decay = jnp.exp(-step_rate * block_len)
    return (toeplitz, head_table, tail_table, step_decay)


def project_rows(row_block, w_flat):
    return jnp.dot(
        lax.all_gather(row_block, "shard", axis=1, tiled=True),
        w_flat,
        preferred_element_type=jnp.float32,
    )


def shards(features, in_proj, short_filter, residue, decay_rate, skip_gain):
    length = features.shape[0]
    channels = in_proj.shape[2]
    tap_count = short_filter.shape[0]
    rim_count = tap_count - 1
    seq_count = lax.axis_size("seq")
    total_len = length * seq_count
    w_flat = in_proj.reshape(in_proj.shape[0], 3 * channels)
    proj = project_rows(features, w_flat).astype(jnp.bfloat16).reshape(length, 3, channels)
    rim_rows = shifted(proj[length - rim_count :], "seq", 1)
    extended = jnp.concatenate([rim_rows, proj], 0)
    extended = extended.astype(jnp.float32)
    own_taps = lax.dynamic_slice_in_dim(
        short_filter, lax.axis_index("shard") * channels, channels, 2
    )
    filtered = jnp.zeros((length, 3, channels), jnp.float32)
    for tap_index in range(tap_count):
        start_row = rim_count - tap_index
        filtered = filtered + own_taps[tap_index] * extended[start_row : start_row + length]
    drive_term = filtered[:, 1, :] * filtered[:, 2, :]
    block_len = math.gcd(length, 128)
    block_count = length // block_len
    toeplitz, head_table, tail_table, step_decay = mode_tables(
        residue, decay_rate, total_len, block_len
    )
    highest = lax.Precision.HIGHEST
    blocks = drive_term.reshape(block_count, block_len, channels)
    intra = jnp.einsum("tsc,bsc->btc", toeplitz, blocks, precision=highest)
    states = jnp.einsum("bsc,smc->bmc", blocks, tail_table, precision=highest)

    def accumulate(carried, state_in):
        return (carried * step_decay + state_in, carried)

    total_state, carries = lax.scan(accumulate, jnp.zeros(residue.shape, jnp.float32), states)
    device_decay = jnp.exp(-(decay_rate / total_len) * length)

    def relay(turn, incoming):
        return shifted(incoming * device_decay + total_state, "seq", 1)

    incoming = lax.fori_loop(0, seq_count - 1, relay, jnp.zeros_like(total_state))
    block_starts = (block_len * jnp.arange(block_count, dtype=jnp.float32))[:, None, None]
    entering = carries + jnp.exp(-(decay_rate / total_len)[None] * block_starts) * incoming[None]
    correction = jnp.einsum("tmc,bmc->btc", head_table, entering, precision=highest)
    longconv = (intra + correction).reshape(length, channels)
    return (filtered[:, 0, :] * (longconv + skip_gain * drive_term)).astype(jnp.bfloat16)


def solution(mesh):
    placed = (
        P("seq", "shard"),
        P(None, None, "shard"),
        P(),
        P(None, "shard"),
        P(None, "shard"),
        P("shard"),
    )
    return jax.shard_map(
        shards, mesh=mesh, in_specs=placed, out_specs=P("seq", "shard"), check_vma=False
    )
```

profile of v0, /device:TPU:6, one launch (start us, length us, event | category | flops | bytes accessed | tf_op | source)
XLA Modules:
  0.0 349.9 jit_solution(4702001722327481454)
XLA Ops:
  7.3 3.2 copy.26
  13.5 128.4 %all-gather.2.cloned.1.call-done = bf16[256,4096]{1,0:T(8,128)(2,1)} async-done(((bf16[256,128]{1,0:T(8,128)(2,1)}), bf16[256,4096]{1,0:T(8,128)(2,1)}) %all-gather.2.cloned.1.call-update) | async-done | bytes 2097168 | tf_op jit(solution)/shard_map/all_gather | solution.py:33
  141.9 2.9 convolution_convert_fusion
  144.8 1.9 collective-permute-start.1
  147.7 54.5 %gather_fusion = f32[16384,128]{1,0:T(8,128)} fusion(f32[128,128]{1,0:T(8,128)S(1)} %copy.31, s32[16384]{0:T(1024)S(1)} %fusion.23), kind=kCustom, calls=%fused_computation | custom fusion | bytes 16842752 | tf_op jit(solution)/shard_map/gather | solution.py:23
  202.2 9.4 %copy.32 = f32[128,128,128]{1,0,2:T(8,128)} copy(f32[128,128,128]{2,1,0:T(8,128)} %bitcast.48) | data formatting | bytes 16777216 | tf_op jit(solution)/shard_map/gather | solution.py:23
  214.6 110.5 %while.23 = (s32[]{:T(128)}, f32[16,128]{1,0:T(8,128)S(1)}, f32[16,128]{1,0:T(8,128)S(1)}, f32[16,128]{1,0:T(8,128)S(1)}, s32[]{:T(128)}) while((s32[]{:T(128)}, f32[16,128]{1,0:T(8,128)S(1)}, f32[16,128]{1,0:T(8,128)S(1)}, f32[16,128]{1,0:T(8,128)S(1)}, s32[]{:T(128)}) %tuple.46), condition=%wide.region_4.5_spmd, body=%wide.region_3.4_spmd.sunk | while | flops 4098 | bytes 65637 | solution.py:78
  214.7 5.1 %collective-permute-start = (f32[16,128]{1,0:T(8,128)S(1)}, f32[16,128]{1,0:T(8,128)S(1)}, u32[]{:S(2)}, u32[]{:S(2)}) collective-permute-start(f32[16,128]{1,0:T(8,128)S(1)} %multiply_add_fusion.3), channel_id=1, source_target_pairs={{0,32},{32,64},{64,96},{96,128},{128,160},{160,192},{192,224},{224... | collective-permute-start | bytes 24584 | tf_op jit(solution)/shard_map/while/body/eval_jaxpr/ppermute | solution.py:12
  219.8 2.2 collective-permute-done
  222.0 1.9 collective-permute-start
  224.0 5.4 %collective-permute-done = f32[16,128]{1,0:T(8,128)S(1)} collective-permute-done((f32[16,128]{1,0:T(8,128)S(1)}, f32[16,128]{1,0:T(8,128)S(1)}, u32[]{:S(2)}, u32[]{:S(2)}) %collective-permute-start) | collective-permute-done | bytes 8224 | tf_op jit(solution)/shard_map/while/body/eval_jaxpr/ppermute | solution.py:12
  229.4 1.9 collective-permute-start
  231.3 5.4 %collective-permute-done = f32[16,128]{1,0:T(8,128)S(1)} collective-permute-done((f32[16,128]{1,0:T(8,128)S(1)}, f32[16,128]{1,0:T(8,128)S(1)}, u32[]{:S(2)}, u32[]{:S(2)}) %collective-permute-start) | collective-permute-done | bytes 8224 | tf_op jit(solution)/shard_map/while/body/eval_jaxpr/ppermute | solution.py:12
  236.8 1.9 collective-permute-start
  238.7 5.4 %collective-permute-done = f32[16,128]{1,0:T(8,128)S(1)} collective-permute-done((f32[16,128]{1,0:T(8,128)S(1)}, f32[16,128]{1,0:T(8,128)S(1)}, u32[]{:S(2)}, u32[]{:S(2)}) %collective-permute-start) | collective-permute-done | bytes 8224 | tf_op jit(solution)/shard_map/while/body/eval_jaxpr/ppermute | solution.py:12
  244.1 1.9 collective-permute-start
  246.1 5.4 %collective-permute-done = f32[16,128]{1,0:T(8,128)S(1)} collective-permute-done((f32[16,128]{1,0:T(8,128)S(1)}, f32[16,128]{1,0:T(8,128)S(1)}, u32[]{:S(2)}, u32[]{:S(2)}) %collective-permute-start) | collective-permute-done | bytes 8224 | tf_op jit(solution)/shard_map/while/body/eval_jaxpr/ppermute | solution.py:12
  253.4 5.4 %collective-permute-done = f32[16,128]{1,0:T(8,128)S(1)} collective-permute-done((f32[16,128]{1,0:T(8,128)S(1)}, f32[16,128]{1,0:T(8,128)S(1)}, u32[]{:S(2)}, u32[]{:S(2)}) %collective-permute-start) | collective-permute-done | bytes 8224 | tf_op jit(solution)/shard_map/while/body/eval_jaxpr/ppermute | solution.py:12
  260.8 5.4 %collective-permute-done = f32[16,128]{1,0:T(8,128)S(1)} collective-permute-done((f32[16,128]{1,0:T(8,128)S(1)}, f32[16,128]{1,0:T(8,128)S(1)}, u32[]{:S(2)}, u32[]{:S(2)}) %collective-permute-start) | collective-permute-done | bytes 8224 | tf_op jit(solution)/shard_map/while/body/eval_jaxpr/ppermute | solution.py:12
  268.2 5.4 %collective-permute-done = f32[16,128]{1,0:T(8,128)S(1)} collective-permute-done((f32[16,128]{1,0:T(8,128)S(1)}, f32[16,128]{1,0:T(8,128)S(1)}, u32[]{:S(2)}, u32[]{:S(2)}) %collective-permute-start) | collective-permute-done | bytes 8224 | tf_op jit(solution)/shard_map/while/body/eval_jaxpr/ppermute | solution.py:12
  275.5 5.4 %collective-permute-done = f32[16,128]{1,0:T(8,128)S(1)} collective-permute-done((f32[16,128]{1,0:T(8,128)S(1)}, f32[16,128]{1,0:T(8,128)S(1)}, u32[]{:S(2)}, u32[]{:S(2)}) %collective-permute-start) | collective-permute-done | bytes 8224 | tf_op jit(solution)/shard_map/while/body/eval_jaxpr/ppermute | solution.py:12
  282.9 5.4 %collective-permute-done = f32[16,128]{1,0:T(8,128)S(1)} collective-permute-done((f32[16,128]{1,0:T(8,128)S(1)}, f32[16,128]{1,0:T(8,128)S(1)}, u32[]{:S(2)}, u32[]{:S(2)}) %collective-permute-start) | collective-permute-done | bytes 8224 | tf_op jit(solution)/shard_map/while/body/eval_jaxpr/ppermute | solution.py:12
  290.3 5.4 %collective-permute-done = f32[16,128]{1,0:T(8,128)S(1)} collective-permute-done((f32[16,128]{1,0:T(8,128)S(1)}, f32[16,128]{1,0:T(8,128)S(1)}, u32[]{:S(2)}, u32[]{:S(2)}) %collective-permute-start) | collective-permute-done | bytes 8224 | tf_op jit(solution)/shard_map/while/body/eval_jaxpr/ppermute | solution.py:12
  295.7 1.9 collective-permute-start
  297.6 5.4 %collective-permute-done = f32[16,128]{1,0:T(8,128)S(1)} collective-permute-done((f32[16,128]{1,0:T(8,128)S(1)}, f32[16,128]{1,0:T(8,128)S(1)}, u32[]{:S(2)}, u32[]{:S(2)}) %collective-permute-start) | collective-permute-done | bytes 8224 | tf_op jit(solution)/shard_map/while/body/eval_jaxpr/ppermute | solution.py:12
  303.1 1.9 collective-permute-start
  305.0 5.4 %collective-permute-done = f32[16,128]{1,0:T(8,128)S(1)} collective-permute-done((f32[16,128]{1,0:T(8,128)S(1)}, f32[16,128]{1,0:T(8,128)S(1)}, u32[]{:S(2)}, u32[]{:S(2)}) %collective-permute-start) | collective-permute-done | bytes 8224 | tf_op jit(solution)/shard_map/while/body/eval_jaxpr/ppermute | solution.py:12
  310.4 1.9 collective-permute-start
  312.4 5.4 %collective-permute-done = f32[16,128]{1,0:T(8,128)S(1)} collective-permute-done((f32[16,128]{1,0:T(8,128)S(1)}, f32[16,128]{1,0:T(8,128)S(1)}, u32[]{:S(2)}, u32[]{:S(2)}) %collective-permute-start) | collective-permute-done | bytes 8224 | tf_op jit(solution)/shard_map/while/body/eval_jaxpr/ppermute | solution.py:12
  317.8 1.9 collective-permute-start
  319.7 5.4 %collective-permute-done = f32[16,128]{1,0:T(8,128)S(1)} collective-permute-done((f32[16,128]{1,0:T(8,128)S(1)}, f32[16,128]{1,0:T(8,128)S(1)}, u32[]{:S(2)}, u32[]{:S(2)}) %collective-permute-start) | collective-permute-done | bytes 8224 | tf_op jit(solution)/shard_map/while/body/eval_jaxpr/ppermute | solution.py:12
  326.8 15.4 %fusion.4 = f32[128,2,128]{2,1,0:T(2,128)S(1)} fusion(f32[128,2,128]{2,1,0:T(2,128)S(1)} %fusion.7, f32[2,128,128]{1,0,2:T(2,128)S(1)} %mul.171, f32[128,128,128]{1,0,2:T(8,128)} %copy.32, pred[128,128]{1,0:T(8,128)(4,1)S(1)} %subtract_compare_fusion), kind=kOutput, calls=%fused_computation.9 | convolution fusion | flops 52461568 | bytes 8798208 | tf_op jit(solution)/shard_map/tsc,bsc->btc/dot_general | solution.py:66
  (64 shorter events, 21.7 us)
Async XLA Ops:
  6.5 135.4 %all-gather.2.cloned.1.call-start = ((), (), s32[]{:S(2)}) async-start(), calls=%async_computation | async-start | bytes 2162688 | tf_op jit(solution)/shard_map/all_gather | solution.py:33
  11.4 0.8 copy-start
  144.8 66.9 %collective-permute-start.1 = (bf16[2,3,128]{2,1,0:T(4,128)(2,1)S(1)}, bf16[2,3,128]{2,1,0:T(4,128)(2,1)S(1)}, u32[]{:S(2)}, u32[]{:S(2)}) collective-permute-start(bf16[2,3,128]{2,1,0:T(4,128)(2,1)S(1)} %slice.35), channel_id=1, source_target_pairs={{0,32},{32,64},{64,96},{96,128},{128,160},{160,192},{192,224},{224... | collective-permute-start | bytes 4616 | tf_op jit(solution)/shard_map/ppermute | solution.py:12
  202.2 123.2 %copy-start.1 = (f32[16,128]{0,1:T(8,128)S(1)}, f32[16,128]{0,1:T(8,128)}, u32[]{:S(2)}) copy-start(f32[16,128]{0,1:T(8,128)} %copy-done) | copy-start | bytes 24580
  211.6 130.6 %copy-start.2 = (f32[128]{0:T(128)S(1)}, f32[128]{0:T(128)}, u32[]{:S(2)}) copy-start(f32[128]{0:T(128)} %param.15) | copy-start | bytes 1540
  214.7 7.4 %collective-permute-start = (f32[16,128]{1,0:T(8,128)S(1)}, f32[16,128]{1,0:T(8,128)S(1)}, u32[]{:S(2)}, u32[]{:S(2)}) collective-permute-start(f32[16,128]{1,0:T(8,128)S(1)} %multiply_add_fusion.3), channel_id=1, source_target_pairs={{0,32},{32,64},{64,96},{96,128},{128,160},{160,192},{192,224},{224... | collective-permute-start | bytes 24584 | tf_op jit(solution)/shard_map/while/body/eval_jaxpr/ppermute | solution.py:12
  222.0 7.4 %collective-permute-start = (f32[16,128]{1,0:T(8,128)S(1)}, f32[16,128]{1,0:T(8,128)S(1)}, u32[]{:S(2)}, u32[]{:S(2)}) collective-permute-start(f32[16,128]{1,0:T(8,128)S(1)} %multiply_add_fusion.3), channel_id=1, source_target_pairs={{0,32},{32,64},{64,96},{96,128},{128,160},{160,192},{192,224},{224... | collective-permute-start | bytes 24584 | tf_op jit(solution)/shard_map/while/body/eval_jaxpr/ppermute | solution.py:12
  229.4 7.4 %collective-permute-start = (f32[16,128]{1,0:T(8,128)S(1)}, f32[16,128]{1,0:T(8,128)S(1)}, u32[]{:S(2)}, u32[]{:S(2)}) collective-permute-start(f32[16,128]{1,0:T(8,128)S(1)} %multiply_add_fusion.3), channel_id=1, source_target_pairs={{0,32},{32,64},{64,96},{96,128},{128,160},{160,192},{192,224},{224... | collective-permute-start | bytes 24584 | tf_op jit(solution)/shard_map/while/body/eval_jaxpr/ppermute | solution.py:12
  236.8 7.4 %collective-permute-start = (f32[16,128]{1,0:T(8,128)S(1)}, f32[16,128]{1,0:T(8,128)S(1)}, u32[]{:S(2)}, u32[]{:S(2)}) collective-permute-start(f32[16,128]{1,0:T(8,128)S(1)} %multiply_add_fusion.3), channel_id=1, source_target_pairs={{0,32},{32,64},{64,96},{96,128},{128,160},{160,192},{192,224},{224... | collective-permute-start | bytes 24584 | tf_op jit(solution)/shard_map/while/body/eval_jaxpr/ppermute | solution.py:12
  244.1 7.4 %collective-permute-start = (f32[16,128]{1,0:T(8,128)S(1)}, f32[16,128]{1,0:T(8,128)S(1)}, u32[]{:S(2)}, u32[]{:S(2)}) collective-permute-start(f32[16,128]{1,0:T(8,128)S(1)} %multiply_add_fusion.3), channel_id=1, source_target_pairs={{0,32},{32,64},{64,96},{96,128},{128,160},{160,192},{192,224},{224... | collective-permute-start | bytes 24584 | tf_op jit(solution)/shard_map/while/body/eval_jaxpr/ppermute | solution.py:12
  251.5 7.4 %collective-permute-start = (f32[16,128]{1,0:T(8,128)S(1)}, f32[16,128]{1,0:T(8,128)S(1)}, u32[]{:S(2)}, u32[]{:S(2)}) collective-permute-start(f32[16,128]{1,0:T(8,128)S(1)} %multiply_add_fusion.3), channel_id=1, source_target_pairs={{0,32},{32,64},{64,96},{96,128},{128,160},{160,192},{192,224},{224... | collective-permute-start | bytes 24584 | tf_op jit(solution)/shard_map/while/body/eval_jaxpr/ppermute | solution.py:12
  258.9 7.4 %collective-permute-start = (f32[16,128]{1,0:T(8,128)S(1)}, f32[16,128]{1,0:T(8,128)S(1)}, u32[]{:S(2)}, u32[]{:S(2)}) collective-permute-start(f32[16,128]{1,0:T(8,128)S(1)} %multiply_add_fusion.3), channel_id=1, source_target_pairs={{0,32},{32,64},{64,96},{96,128},{128,160},{160,192},{192,224},{224... | collective-permute-start | bytes 24584 | tf_op jit(solution)/shard_map/while/body/eval_jaxpr/ppermute | solution.py:12
  266.2 7.4 %collective-permute-start = (f32[16,128]{1,0:T(8,128)S(1)}, f32[16,128]{1,0:T(8,128)S(1)}, u32[]{:S(2)}, u32[]{:S(2)}) collective-permute-start(f32[16,128]{1,0:T(8,128)S(1)} %multiply_add_fusion.3), channel_id=1, source_target_pairs={{0,32},{32,64},{64,96},{96,128},{128,160},{160,192},{192,224},{224... | collective-permute-start | bytes 24584 | tf_op jit(solution)/shard_map/while/body/eval_jaxpr/ppermute | solution.py:12
  273.6 7.4 %collective-permute-start = (f32[16,128]{1,0:T(8,128)S(1)}, f32[16,128]{1,0:T(8,128)S(1)}, u32[]{:S(2)}, u32[]{:S(2)}) collective-permute-start(f32[16,128]{1,0:T(8,128)S(1)} %multiply_add_fusion.3), channel_id=1, source_target_pairs={{0,32},{32,64},{64,96},{96,128},{128,160},{160,192},{192,224},{224... | collective-permute-start | bytes 24584 | tf_op jit(solution)/shard_map/while/body/eval_jaxpr/ppermute | solution.py:12
  281.0 7.4 %collective-permute-start = (f32[16,128]{1,0:T(8,128)S(1)}, f32[16,128]{1,0:T(8,128)S(1)}, u32[]{:S(2)}, u32[]{:S(2)}) collective-permute-start(f32[16,128]{1,0:T(8,128)S(1)} %multiply_add_fusion.3), channel_id=1, source_target_pairs={{0,32},{32,64},{64,96},{96,128},{128,160},{160,192},{192,224},{224... | collective-permute-start | bytes 24584 | tf_op jit(solution)/shard_map/while/body/eval_jaxpr/ppermute | solution.py:12
  288.3 7.4 %collective-permute-start = (f32[16,128]{1,0:T(8,128)S(1)}, f32[16,128]{1,0:T(8,128)S(1)}, u32[]{:S(2)}, u32[]{:S(2)}) collective-permute-start(f32[16,128]{1,0:T(8,128)S(1)} %multiply_add_fusion.3), channel_id=1, source_target_pairs={{0,32},{32,64},{64,96},{96,128},{128,160},{160,192},{192,224},{224... | collective-permute-start | bytes 24584 | tf_op jit(solution)/shard_map/while/body/eval_jaxpr/ppermute | solution.py:12
  295.7 7.4 %collective-permute-start = (f32[16,128]{1,0:T(8,128)S(1)}, f32[16,128]{1,0:T(8,128)S(1)}, u32[]{:S(2)}, u32[]{:S(2)}) collective-permute-start(f32[16,128]{1,0:T(8,128)S(1)} %multiply_add_fusion.3), channel_id=1, source_target_pairs={{0,32},{32,64},{64,96},{96,128},{128,160},{160,192},{192,224},{224... | collective-permute-start | bytes 24584 | tf_op jit(solution)/shard_map/while/body/eval_jaxpr/ppermute | solution.py:12
  303.1 7.4 %collective-permute-start = (f32[16,128]{1,0:T(8,128)S(1)}, f32[16,128]{1,0:T(8,128)S(1)}, u32[]{:S(2)}, u32[]{:S(2)}) collective-permute-start(f32[16,128]{1,0:T(8,128)S(1)} %multiply_add_fusion.3), channel_id=1, source_target_pairs={{0,32},{32,64},{64,96},{96,128},{128,160},{160,192},{192,224},{224... | collective-permute-start | bytes 24584 | tf_op jit(solution)/shard_map/while/body/eval_jaxpr/ppermute | solution.py:12
  310.4 7.4 %collective-permute-start = (f32[16,128]{1,0:T(8,128)S(1)}, f32[16,128]{1,0:T(8,128)S(1)}, u32[]{:S(2)}, u32[]{:S(2)}) collective-permute-start(f32[16,128]{1,0:T(8,128)S(1)} %multiply_add_fusion.3), channel_id=1, source_target_pairs={{0,32},{32,64},{64,96},{96,128},{128,160},{160,192},{192,224},{224... | collective-permute-start | bytes 24584 | tf_op jit(solution)/shard_map/while/body/eval_jaxpr/ppermute | solution.py:12
  317.8 7.4 %collective-permute-start = (f32[16,128]{1,0:T(8,128)S(1)}, f32[16,128]{1,0:T(8,128)S(1)}, u32[]{:S(2)}, u32[]{:S(2)}) collective-permute-start(f32[16,128]{1,0:T(8,128)S(1)} %multiply_add_fusion.3), channel_id=1, source_target_pairs={{0,32},{32,64},{64,96},{96,128},{128,160},{160,192},{192,224},{224... | collective-permute-start | bytes 24584 | tf_op jit(solution)/shard_map/while/body/eval_jaxpr/ppermute | solution.py:12
Sparse Core Ops, SparseCore 0:
  9.4 132.5 all-gather.1
where the time goes:
time: 351 us; the launch traced here: 350 us
  waiting for transfers between devices  208 us (59%)
  local copies, waits for them, and re-layouts  70.3 us (20%)
  starting transfers between devices  33.8 us (10%)
  matrix products  21.5 us (6%)
  between operations  13.6 us (4%)
    all_gather x1, waiting for transfers between devices, project_rows(): lax.all_gather(row_block, 'shard', axis=1, tiled=True)  128 us
    ppermute x16, waiting for transfers between devices, shifted(): lax.ppermute(value, axis, [(source, source + steps) for source in range(i...  78.4 us
    gather x2, local copies, waits for them, and re-layouts, mode_tables(): kernel[jnp.clip(offsets, 0, block_len - 1)]  63.9 us
    ppermute x16, starting transfers between devices, shifted(): lax.ppermute(value, axis, [(source, source + steps) for source in range(i...  33.8 us
    dot_general x1, matrix products, shards(): intra = jnp.einsum('tsc,bsc->btc', toeplitz, blocks, precision=highest)  15.4 us
  transfers between devices with their start and end apart: 17, of which 16 were waited for; matrix products, arithmetic and copies ran while one was open for 20% of the time, Pallas kernels for 0%

commit v1 on v0

v1 whole, which is shorter than its diff:
```python
import functools

import jax
import jax.numpy as jnp
from jax import lax
from jax.experimental import pallas as pl
from jax.experimental.pallas import tpu as pltpu
from jax.sharding import PartitionSpec as P

TILE = 8
ROWS = 32


def row_tile(ref, row):
    return jnp.broadcast_to(ref[row : row + 1, :], (TILE, ref.shape[1]))


def tables_kernel(modes, length, total, rate_ref, gain_ref, h_ref, e_ref):
    tiles = length // TILE
    step = rate_ref[...] * (1.0 / total)
    lane = jax.lax.broadcasted_iota(jnp.int32, (TILE, step.shape[1]), 0).astype(jnp.float32)
    for q in range(tiles):
        e_ref[q * modes : (q + 1) * modes, :] = jnp.exp(-step * float(TILE * q))
    scaled = [gain_ref[m : m + 1, :] * jnp.exp(-step[m : m + 1, :] * lane) for m in range(modes)]
    for q in range(tiles):
        total_tile = row_tile(e_ref, q * modes) * scaled[0]
        for m in range(1, modes):
            total_tile = total_tile + row_tile(e_ref, q * modes + m) * scaled[m]
        h_ref[q * TILE : (q + 1) * TILE, :] = total_tile


def project_kernel(
    modes, length, total, per_step, x_ref, w_ref, taps_ref, rate_ref, e_ref,
    first_ref, drive_ref, message_ref, acc_ref, proj_ref, filt_ref,
):
    at = pl.program_id(0)
    block = x_ref.shape[2]
    channels = drive_ref.shape[1]

    @pl.when(at == 0)
    def _():
        acc_ref[...] = jnp.zeros_like(acc_ref)

    part = acc_ref[...]
    for i in range(0, per_step, 2):
        left = jnp.concatenate([x_ref[i], x_ref[i + 1]], axis=1)
        part = part + jnp.dot(
            left, w_ref[i * block : (i + 2) * block, :], preferred_element_type=jnp.float32
        )
    acc_ref[...] = part

    @pl.when(at == pl.num_programs(0) - 1)
    def _():
        pad = TILE
        proj_ref[0:pad, :] = jnp.zeros((pad, 3 * channels), jnp.float32)
        proj_ref[pad:, :] = acc_ref[...].astype(jnp.bfloat16).astype(jnp.float32)
        for b in range(3):
            cols = slice(b * channels, (b + 1) * channels)
            value = taps_ref[b : b + 1, :] * proj_ref[pad : pad + length, cols]
            value = value + taps_ref[3 + b : 4 + b, :] * proj_ref[pad - 1 : pad - 1 + length, cols]
            value = value + taps_ref[6 + b : 7 + b, :] * proj_ref[pad - 2 : pad - 2 + length, cols]
            if b == 0:
                first_ref[...] = value
            else:
                filt_ref[b - 1] = value
        drive = filt_ref[0] * filt_ref[1]
        drive_ref[...] = drive
        row = jax.lax.broadcasted_iota(jnp.int32, (TILE, channels), 0)
        lag = (TILE - 1 - row).astype(jnp.float32)
        tiles = length // TILE
        pieces = [drive_ref[q * TILE : (q + 1) * TILE, :] for q in range(tiles)]
        pieces[0] = jnp.where(row < 2, 0.0, pieces[0])
        step = rate_ref[...] * (1.0 / total)
        for m in range(modes):
            state = row_tile(e_ref, (tiles - 1) * modes + m) * pieces[0]
            for q in range(1, tiles):
                state = state + row_tile(e_ref, (tiles - 1 - q) * modes + m) * pieces[q]
            state = state * jnp.exp(-step[m : m + 1, :] * lag)
            message_ref[m : m + 1, :] = jnp.sum(state, axis=0, keepdims=True)
        one, two, three = channels, 2 * channels, 3 * channels
        head, tail = pad, pad + length - 2
        spots = [
            (head, one, two), (head, two, three), (head + 1, one, two), (head + 1, two, three),
            (tail, one, two), (tail, two, three), (tail + 1, one, two), (tail + 1, two, three),
            (tail, 0, one), (tail + 1, 0, one),
        ]
        for k, (r, lo, hi) in enumerate(spots):
            message_ref[modes + k : modes + k + 1, :] = proj_ref[r : r + 1, lo:hi]
        used = modes + len(spots)
        message_ref[used:ROWS, :] = jnp.zeros((ROWS - used, channels), jnp.float32)


def finish_kernel(
    modes, length, total, seq_count, me_ref, all_ref, first_ref, drive_ref, taps_ref, rate_ref,
    gain_ref, skip_ref, h_ref, e_ref, out_ref, pad_ref, lag_ref, conv_ref,
):
    me = me_ref[0]
    channels = drive_ref.shape[1]
    tiles = length // TILE
    step = rate_ref[...] * (1.0 / total)

    def tap(j, b):
        return taps_ref[3 * j + b : 3 * j + b + 1, :]

    def rows(k):
        return all_ref[pl.ds(modes + k, seq_count, stride=ROWS), :]

    order = jax.lax.broadcasted_iota(jnp.int32, (seq_count, channels), 0)

    def before(k):
        return jnp.where(order == 0, 0.0, pltpu.roll(rows(k), 1, 0))

    starts = [None, None]
    for b in (1, 2):
        head0, head1 = rows(b - 1), rows(2 + b - 1)
        rim0, rim1 = before(4 + b - 1), before(6 + b - 1)
        row0 = tap(0, b) * head0 + tap(1, b) * rim1 + tap(2, b) * rim0
        row1 = tap(0, b) * head1 + tap(1, b) * head0 + tap(2, b) * rim1
        starts = [row0, row1] if b == 1 else [starts[0] * row0, starts[1] * row1]
    start0, start1 = starts
    late0 = jnp.exp(-step * float(length - 1))
    late1 = jnp.exp(-step * float(length - 2))
    fade = jnp.exp(-step * float(length))
    incoming = jnp.zeros((modes, channels), jnp.float32)
    for j in range(seq_count):
        state = all_ref[j * ROWS : j * ROWS + modes, :]
        state = state + late0 * start0[j : j + 1, :] + late1 * start1[j : j + 1, :]
        incoming = jnp.where(j < me, incoming * fade + state, incoming)

    row = jax.lax.broadcasted_iota(jnp.int32, (TILE, channels), 0)
    mine0 = jnp.sum(jnp.where(order == me, start0, 0.0), axis=0, keepdims=True)
    mine1 = jnp.sum(jnp.where(order == me, start1, 0.0), axis=0, keepdims=True)
    rim0 = jnp.sum(jnp.where(order == me - 1, rows(8), 0.0), axis=0, keepdims=True)
    rim1 = jnp.sum(jnp.where(order == me - 1, rows(9), 0.0), axis=0, keepdims=True)
    extra0 = tap(1, 0) * rim1 + tap(2, 0) * rim0
    extra1 = tap(2, 0) * rim1

    pad_ref[0:TILE, :] = jnp.zeros((TILE, channels), jnp.float32)
    pad_ref[TILE:, :] = drive_ref[...]
    head = drive_ref[0:TILE, :]
    head = jnp.where(row == 0, mine0, jnp.where(row == 1, mine1, head))
    pad_ref[TILE : 2 * TILE, :] = head
    for j in range(TILE):
        lag_ref[j] = pad_ref[TILE - j : TILE - j + length, :]

    group = 8
    for g in range(tiles // group):
        low = g * group

        def over_lags(j, accs):
            accs = list(accs)
            window = [lag_ref[j, pl.ds((low + i) * TILE, TILE), :] for i in range(group)]
            for p in range(low + group):
                weight = jnp.broadcast_to(h_ref[pl.ds(TILE * p + j, 1), :], (TILE, channels))
                for i in range(group):
                    if low + i - p >= 0:
                        accs[i] = accs[i] + weight * window[i]
                below = low - p - 1
                fresh = lag_ref[j, pl.ds(below * TILE, TILE), :] if below >= 0 else None
                window = [fresh] + window[:-1]
            return tuple(accs)

        zero = jnp.zeros((TILE, channels), jnp.float32)
        accs = lax.fori_loop(0, TILE, over_lags, (zero,) * group)
        for i in range(group):
            conv_ref[(low + i) * TILE : (low + i + 1) * TILE, :] = accs[i]

    lead = (row + 1).astype(jnp.float32)
    heads = []
    for m in range(modes):
        scale = gain_ref[m : m + 1, :] * incoming[m : m + 1, :]
        heads.append(scale * jnp.exp(-step[m : m + 1, :] * lead))
    skip = skip_ref[...]
    for q in range(tiles):
        at = slice(q * TILE, (q + 1) * TILE)
        value = conv_ref[at, :] + skip * pad_ref[(q + 1) * TILE : (q + 2) * TILE, :]
        for m in range(modes):
            value = value + row_tile(e_ref, q * modes + m) * heads[m]
        gate = first_ref[at, :]
        if q == 0:
            gate = gate + jnp.where(row == 0, extra0, jnp.where(row == 1, extra1, 0.0))
        conv_ref[at, :] = gate * value
    out_ref[...] = conv_ref[...].astype(out_ref.dtype)


def gather_features(features):
    return lax.all_gather(features, "shard", axis=0)


def shards(features, in_proj, short_filter, residue, decay_rate, skip_gain):
    length = features.shape[0]
    channels = in_proj.shape[2]
    modes = residue.shape[0]
    seq_count = lax.axis_size("seq")
    shard_count = lax.axis_size("shard")
    total = length * seq_count
    tiles = length // TILE
    f32 = jnp.float32
    params = pltpu.CompilerParams(vmem_limit_bytes=48 << 20)

    gathered = gather_features(features)
    w_flat = in_proj.reshape(in_proj.shape[0], 3 * channels)
    taps = lax.dynamic_slice_in_dim(
        short_filter, lax.axis_index("shard") * channels, channels, 2
    ).reshape(-1, channels)
    step_rate = decay_rate / total
    gain = residue * jnp.sqrt(jnp.expm1(-2.0 * step_rate) / jnp.expm1(-2.0 * decay_rate))
    h, e = pl.pallas_call(
        functools.partial(tables_kernel, modes, length, total),
        out_shape=(
            jax.ShapeDtypeStruct((length, channels), f32),
            jax.ShapeDtypeStruct((tiles * modes, channels), f32),
        ),
        compiler_params=params,
        name="tables",
    )(decay_rate, gain)

    per_step = 4
    block = features.shape[1]
    whole = lambda shape: pl.BlockSpec(shape, lambda i: (0,) * len(shape))
    first, drive, message = pl.pallas_call(
        functools.partial(project_kernel, modes, length, total, per_step),
        grid=(shard_count // per_step,),
        in_specs=[
            pl.BlockSpec((per_step, length, block), lambda i: (i, 0, 0)),
            pl.BlockSpec((per_step * block, 3 * channels), lambda i: (i, 0)),
            whole(taps.shape),
            whole(decay_rate.shape),
            whole(e.shape),
        ],
        out_specs=(whole((length, channels)), whole((length, channels)), whole((ROWS, channels))),
        out_shape=(
            jax.ShapeDtypeStruct((length, channels), f32),
            jax.ShapeDtypeStruct((length, channels), f32),
            jax.ShapeDtypeStruct((ROWS, channels), f32),
        ),
        scratch_shapes=[
            pltpu.VMEM((length, 3 * channels), f32),
            pltpu.VMEM((length + TILE, 3 * channels), f32),
            pltpu.VMEM((2, length, channels), f32),
        ],
        compiler_params=params,
        name="project",
    )(gathered, w_flat, taps, decay_rate, e)

    spread = jnp.broadcast_to(message[None], (seq_count,) + message.shape)
    everyone = lax.all_to_all(spread, "seq", 0, 0).reshape(seq_count * ROWS, channels)

    me = lax.axis_index("seq").astype(jnp.int32).reshape(1)
    vmem = pl.BlockSpec(memory_space=pltpu.VMEM)
    return pl.pallas_call(
        functools.partial(finish_kernel, modes, length, total, seq_count),
        in_specs=[pl.BlockSpec(memory_space=pltpu.SMEM)] + [vmem] * 9,
        out_specs=vmem,
        out_shape=jax.ShapeDtypeStruct((length, channels), features.dtype),
        scratch_shapes=[
            pltpu.VMEM((length + TILE, channels), f32),
            pltpu.VMEM((TILE, length, channels), f32),
            pltpu.VMEM((length, channels), f32),
        ],
        compiler_params=params,
        name="finish",
    )(me, everyone, first, drive, taps, decay_rate, gain, skip_gain.reshape(1, channels), h, e)


def solution(mesh):
    placed = (
        P("seq", "shard"),
        P(None, None, "shard"),
        P(),
        P(None, "shard"),
        P(None, "shard"),
        P("shard"),
    )
    return jax.shard_map(
        shards, mesh=mesh, in_specs=placed, out_specs=P("seq", "shard"), check_vma=False
    )
```

time: 351 us -> 184 us (0.52)
  the two profiles are of different devices: /device:TPU:6 before, /device:TPU:1 now
where the time goes in v1:
time: 184 us
  waiting for transfers between devices  119 us (65%)
  starting transfers between devices  27.7 us (15%)
  local copies, waits for them, and re-layouts  17.1 us (9%)
  between operations  13.4 us (7%)
  Pallas kernels  5.28 us (3%)
    all_gather x1, waiting for transfers between devices, gather_features(): return lax.all_gather(features, 'shard', axis=0)  110 us
    all_to_all x1, starting transfers between devices, shards(): lax.all_to_all(spread, 'seq', 0, 0).reshape(seq_count * ROWS, channels)  27.7 us
    unnamed x25, local copies, waits for them, and re-layouts  12.9 us
    all_to_all x1, waiting for transfers between devices, shards(): lax.all_to_all(spread, 'seq', 0, 0).reshape(seq_count * ROWS, channels)  8.91 us
  transfers between devices with their start and end apart: 2, of which 2 were waited for; matrix products, arithmetic and copies ran while one was open for 5% of the time, Pallas kernels for 0%

profile of v1, /device:TPU:1, one launch (start us, length us, event | category | flops | bytes accessed | tf_op | source)
XLA Modules:
  0.0 183.7 jit_solution(1126493834072275821)
XLA Ops:
  6.5 0.0 copy-start
  6.5 0.0 all-gather.3.cloned.1.call-start
  6.5 0.7 all-gather.3.cloned.1.call-update
  7.3 0.2 copy-done
  7.5 0.7 sqrt_multiply_fusion.gain_ref
  8.2 0.0 copy-start.5
  8.2 0.7 copy-done.5
  8.9 0.2 tables.1
  9.1 0.0 copy-start.2
  9.1 0.7 copy-done.2
  9.8 4.7 %copy.8 = bf16[4096,3,128]{0,2,1:T(8,128)(2,1)} copy(bf16[4096,3,128]{2,0,1:T(8,128)(2,1)} %param.7) | data formatting | bytes 6291456 | tf_op args[1]
  14.5 0.0 copy-start.6
  14.5 3.5 %copy.9.w_ref = bf16[4096,384]{1,0:T(8,128)(2,1)S(1)} copy(bf16[4096,384]{0,1:T(8,128)(2,1)} %bitcast.8) | data formatting | bytes 6291456 | tf_op jit(solution)/shard_map/reshape | solution.py:202
  18.0 109.7 %all-gather.3.cloned.1.call-done = bf16[8192,128]{1,0:T(8,128)(2,1)} async-done(((bf16[256,128]{1,0:T(8,128)(2,1)}), bf16[8192,128]{1,0:T(8,128)(2,1)}) %all-gather.3.cloned.1.call-update) | async-done | bytes 2097168 | tf_op jit(solution)/shard_map/all_gather | solution.py:187
  127.7 0.0 copy-done.6
  127.7 0.0 copy-start.1
  127.7 1.6 copy-done.1
  129.3 0.0 copy-start.3
  129.3 0.9 copy-done.3
  130.3 0.0 copy-start.11
  130.3 2.8 %project.1 = (f32[256,128]{1,0:T(8,128)S(1)}, f32[256,128]{1,0:T(8,128)S(1)}, f32[32,128]{1,0:T(8,128)S(1)}) custom-call(bf16[32,256,128]{2,1,0:T(8,128)(2,1)S(1)} %bitcast.5, bf16[4096,384]{1,0:T(8,128)(2,1)S(1)} %copy.9.w_ref, f32[9,128]{1,0:T(8,128)S(1)} %reshape.18.taps_ref, f32[16,128]{1,0:T(8,128)S(1)} %copy-done.6, f32[512,128]{1,0:T(8,128)S(1)} %copy-done.3), custom_call_target="tpu_custom_call" | custom-call | tf_op jit(solution)/shard_map/project/pallas_call | solution.py:221
  133.1 0.0 copy-start.7
  133.1 0.6 copy-done.7
  133.8 0.6 copy-done.9
  134.4 0.7 broadcast_in_dim.2
  135.1 27.7 %all-to-all-start = ((f32[16,32,128]{2,1,0:T(8,128)}), f32[16,32,128]{2,1,0:T(8,128)S(1)}, u32[]{:S(2)}, u32[]{:S(2)}) async-start(f32[16,32,128]{2,1,0:T(8,128)} %broadcast_in_dim.2), calls=%async_computation | async-start | bytes 524288 | tf_op jit(solution)/shard_map/all_to_all | solution.py:247
  162.9 8.9 %all-to-all-done = f32[16,32,128]{2,1,0:T(8,128)S(1)} async-done(((f32[16,32,128]{2,1,0:T(8,128)}), f32[16,32,128]{2,1,0:T(8,128)S(1)}, u32[]{:S(2)}, u32[]{:S(2)}) %all-to-all-start) | async-done | bytes 262176 | tf_op jit(solution)/shard_map/all_to_all | solution.py:247
  171.8 0.0 copy-done.11
  171.8 0.9 copy-done.4
  172.7 0.9 copy-done.8
  173.7 0.9 copy-done.10
  174.6 2.3 %finish.1 = bf16[256,128]{1,0:T(8,128)(2,1)} custom-call(s32[1]{0:T(128)} %bitcast.me_ref, f32[512,128]{1,0:T(8,128)S(1)} %bitcast.6, f32[256,128]{1,0:T(8,128)S(1)} %copy-done.8, f32[256,128]{1,0:T(8,128)S(1)} %copy-done.10, f32[9,128]{1,0:T(8,128)S(1)} %reshape.18.taps_ref, f32[16,128]{1,0:T(8,128)S(1)} %copy-done.6, ...), custom_call_target="tpu_custom_call" | custom-call | tf_op jit(solution)/shard_map/finish/pallas_call | solution.py:251
  (6 shorter events, 0.0 us)
Async XLA Ops:
  6.5 0.9 copy-start
  6.5 121.2 %all-gather.3.cloned.1.call-start = ((), (), s32[]{:S(2)}) async-start(), calls=%async_computation.1 | async-start | bytes 2162688 | tf_op jit(solution)/shard_map/all_gather | solution.py:187
  8.2 0.7 copy-start.5
  9.1 0.7 copy-start.2
  14.5 113.2 %copy-start.6 = (f32[16,128]{1,0:T(8,128)S(1)}, f32[16,128]{1,0:T(8,128)}, u32[]{:S(2)}) copy-start(f32[16,128]{1,0:T(8,128)} %rate_ref.5) | copy-start | bytes 24580
  127.7 1.6 copy-start.1
  129.3 0.9 copy-start.3
  130.3 41.5 %copy-start.11 = (f32[128]{0:T(128)S(1)}, f32[128]{0:T(128)}, u32[]{:S(2)}) copy-start(f32[128]{0:T(128)} %param.11) | copy-start | bytes 1540
  133.1 0.6 copy-start.7
  133.8 0.6 copy-start.9
  135.1 36.7 %all-to-all-start = ((f32[16,32,128]{2,1,0:T(8,128)}), f32[16,32,128]{2,1,0:T(8,128)S(1)}, u32[]{:S(2)}, u32[]{:S(2)}) async-start(f32[16,32,128]{2,1,0:T(8,128)} %broadcast_in_dim.2), calls=%async_computation | async-start | bytes 524288 | tf_op jit(solution)/shard_map/all_to_all | solution.py:247
  171.8 1.0 copy-start.4
  172.7 0.9 copy-start.8
  173.6 0.9 copy-start.10
Sparse Core Ops, SparseCore 0:
  9.4 118.2 all-gather.2

commit v2 on v1

--- a/solution.py
+++ b/solution.py
@@ -30,64 +30,69 @@
 
 
 def project_kernel(
-    modes, length, total, per_step, x_ref, w_ref, taps_ref, rate_ref, e_ref,
-    first_ref, drive_ref, message_ref, acc_ref, proj_ref, filt_ref,
+    modes, length, total, place_ref, near_ref, near_up_ref, near_down_ref, far_ref, far_up_ref,
+    far_down_ref, w_ref, taps_ref, rate_ref, e_ref,
+    first_ref, drive_ref, message_ref, acc_ref, proj_ref, filt_ref, state_ref,
 ):
-    at = pl.program_id(0)
-    block = x_ref.shape[2]
+    line, parity = place_ref[0], place_ref[1]
+    pairs, _, block = near_ref.shape
     channels = drive_ref.shape[1]
-
-    @pl.when(at == 0)
-    def _():
-        acc_ref[...] = jnp.zeros_like(acc_ref)
-
-    part = acc_ref[...]
-    for i in range(0, per_step, 2):
-        left = jnp.concatenate([x_ref[i], x_ref[i + 1]], axis=1)
-        part = part + jnp.dot(
-            left, w_ref[i * block : (i + 2) * block, :], preferred_element_type=jnp.float32
+    split = near_up_ref.shape[0]
+
+    def weight(owner):
+        at = pl.ds(pl.multiple_of(owner * block, block), block)
+        return jnp.concatenate([w_ref[b, at, :] for b in range(3)], axis=1)
+
+    for k in range(pairs):
+        near_odd = near_up_ref[k] if k < split else near_down_ref[k - split]
+        far_odd = far_up_ref[k] if k < split else far_down_ref[k - split]
+        left = jnp.concatenate([near_ref[k], near_odd, far_ref[k], far_odd], axis=1)
+        own, other = 2 * pairs * line + 2 * k, 2 * pairs * (1 - line) + 2 * k
+        right = jnp.concatenate(
+            [weight(own + parity), weight(own + 1 - parity), weight(other + parity), weight(other + 1 - parity)],
+            axis=0,
         )
-    acc_ref[...] = part
-
-    @pl.when(at == pl.num_programs(0) - 1)
-    def _():
-        pad = TILE
-        proj_ref[0:pad, :] = jnp.zeros((pad, 3 * channels), jnp.float32)
-        proj_ref[pad:, :] = acc_ref[...].astype(jnp.bfloat16).astype(jnp.float32)
-        for b in range(3):
-            cols = slice(b * channels, (b + 1) * channels)
-            value = taps_ref[b : b + 1, :] * proj_ref[pad : pad + length, cols]
-            value = value + taps_ref[3 + b : 4 + b, :] * proj_ref[pad - 1 : pad - 1 + length, cols]
-            value = value + taps_ref[6 + b : 7 + b, :] * proj_ref[pad - 2 : pad - 2 + length, cols]
-            if b == 0:
-                first_ref[...] = value
-            else:
-                filt_ref[b - 1] = value
-        drive = filt_ref[0] * filt_ref[1]
-        drive_ref[...] = drive
-        row = jax.lax.broadcasted_iota(jnp.int32, (TILE, channels), 0)
-        lag = (TILE - 1 - row).astype(jnp.float32)
-        tiles = length // TILE
-        pieces = [drive_ref[q * TILE : (q + 1) * TILE, :] for q in range(tiles)]
-        pieces[0] = jnp.where(row < 2, 0.0, pieces[0])
-        step = rate_ref[...] * (1.0 / total)
-        for m in range(modes):
-            state = row_tile(e_ref, (tiles - 1) * modes + m) * pieces[0]
-            for q in range(1, tiles):
-                state = state + row_tile(e_ref, (tiles - 1 - q) * modes + m) * pieces[q]
-            state = state * jnp.exp(-step[m : m + 1, :] * lag)
-            message_ref[m : m + 1, :] = jnp.sum(state, axis=0, keepdims=True)
-        one, two, three = channels, 2 * channels, 3 * channels
-        head, tail = pad, pad + length - 2
-        spots = [
-            (head, one, two), (head, two, three), (head + 1, one, two), (head + 1, two, three),
-            (tail, one, two), (tail, two, three), (tail + 1, one, two), (tail + 1, two, three),
-            (tail, 0, one), (tail + 1, 0, one),
-        ]
-        for k, (r, lo, hi) in enumerate(spots):
-            message_ref[modes + k : modes + k + 1, :] = proj_ref[r : r + 1, lo:hi]
-        used = modes + len(spots)
-        message_ref[used:ROWS, :] = jnp.zeros((ROWS - used, channels), jnp.float32)
+        part = jnp.dot(left, right, preferred_element_type=jnp.float32)
+        acc_ref[...] = part if k == 0 else acc_ref[...] + part
+
+    pad = TILE
+    proj_ref[0:pad, :] = jnp.zeros((pad, 3 * channels), jnp.float32)
+    proj_ref[pad:, :] = acc_ref[...].astype(jnp.bfloat16).astype(jnp.float32)
+    for b in range(3):
+        cols = slice(b * channels, (b + 1) * channels)
+        value = taps_ref[b : b + 1, :] * proj_ref[pad : pad + length, cols]
+        value = value + taps_ref[3 + b : 4 + b, :] * proj_ref[pad - 1 : pad - 1 + length, cols]
+        value = value + taps_ref[6 + b : 7 + b, :] * proj_ref[pad - 2 : pad - 2 + length, cols]
+        if b == 0:
+            first_ref[...] = value
+        else:
+            filt_ref[b - 1] = value
+    drive_ref[...] = filt_ref[0] * filt_ref[1]
+    row = jax.lax.broadcasted_iota(jnp.int32, (TILE, channels), 0)
+    lag = (TILE - 1 - row).astype(jnp.float32)
+    tiles = length // TILE
+    pieces = [drive_ref[q * TILE : (q + 1) * TILE, :] for q in range(tiles)]
+    pieces[0] = jnp.where(row < 2, 0.0, pieces[0])
+    step = rate_ref[...] * (1.0 / total)
+    for m in range(modes):
+        state = row_tile(e_ref, (tiles - 1) * modes + m) * pieces[0]
+        for q in range(1, tiles):
+            state = state + row_tile(e_ref, (tiles - 1 - q) * modes + m) * pieces[q]
+        state = state * jnp.exp(-step[m : m + 1, :] * lag)
+        state_ref[m : m + 1, :] = jnp.sum(state, axis=0, keepdims=True)
+    one, two, three = channels, 2 * channels, 3 * channels
+    head, tail = pad, pad + length - 2
+    spots = [
+        (head, one, two), (head, two, three), (head + 1, one, two), (head + 1, two, three),
+        (tail, one, two), (tail, two, three), (tail + 1, one, two), (tail + 1, two, three),
+        (tail, 0, one), (tail + 1, 0, one),
+    ]
+    for k, (r, lo, hi) in enumerate(spots):
+        state_ref[modes + k : modes + k + 1, :] = proj_ref[r : r + 1, lo:hi]
+    used = modes + len(spots)
+    state_ref[used:ROWS, :] = jnp.zeros((ROWS - used, channels), jnp.float32)
+    for s in range(message_ref.shape[0]):
+        message_ref[s] = state_ref[...]
 
 
 def finish_kernel(
@@ -184,7 +189,22 @@
 
 
 def gather_features(features):
-    return lax.all_gather(features, "shard", axis=0)
+    shard_count = lax.axis_size("shard")
+    line = shard_count // 2
+    pairs = line // 2
+    groups = [[l * line + 2 * q + p for q in range(pairs)] for l in range(2) for p in range(2)]
+    across = [(i, (i + line) % shard_count) for i in range(shard_count)]
+    up = [(l * line + z, l * line + (z - 1) % line) for l in range(2) for z in range(line)]
+    down = [(l * line + z, l * line + (z + 1) % line) for l in range(2) for z in range(line)]
+    half = pairs // 2
+
+    near = lax.all_gather(features, "shard", axis=0, axis_index_groups=groups)
+    far = lax.ppermute(near, "shard", across)
+    near_up = lax.ppermute(near[:half], "shard", up)
+    near_down = lax.ppermute(near[half:], "shard", down)
+    far_up = lax.ppermute(far[:half], "shard", up)
+    far_down = lax.ppermute(far[half:], "shard", down)
+    return near, near_up, near_down, far, far_up, far_down
 
 
 def shards(features, in_proj, short_filter, residue, decay_rate, skip_gain):
@@ -192,17 +212,20 @@
     channels = in_proj.shape[2]
     modes = residue.shape[0]
     seq_count = lax.axis_size("seq")
-    shard_count = lax.axis_size("shard")
+    line = lax.axis_size("shard") // 2
     total = length * seq_count
     tiles = length // TILE
     f32 = jnp.float32
-    params = pltpu.CompilerParams(vmem_limit_bytes=48 << 20)
-
-    gathered = gather_features(features)
-    w_flat = in_proj.reshape(in_proj.shape[0], 3 * channels)
-    taps = lax.dynamic_slice_in_dim(
-        short_filter, lax.axis_index("shard") * channels, channels, 2
-    ).reshape(-1, channels)
+    vmem = pl.BlockSpec(memory_space=pltpu.VMEM)
+    smem = pl.BlockSpec(memory_space=pltpu.SMEM)
+
+    def params(mebibytes):
+        return pltpu.CompilerParams(vmem_limit_bytes=mebibytes << 20)
+
+    pieces = gather_features(features)
+    w_branch = in_proj.transpose(1, 0, 2)
+    at = lax.axis_index("shard")
+    taps = lax.dynamic_slice_in_dim(short_filter, at * channels, channels, 2).reshape(-1, channels)
     step_rate = decay_rate / total
     gain = residue * jnp.sqrt(jnp.expm1(-2.0 * step_rate) / jnp.expm1(-2.0 * decay_rate))
     h, e = pl.pallas_call(
@@ -211,46 +234,36 @@
             jax.ShapeDtypeStruct((length, channels), f32),
             jax.ShapeDtypeStruct((tiles * modes, channels), f32),
         ),
-        compiler_params=params,
+        compiler_params=params(4),
         name="tables",
     )(decay_rate, gain)
 
-    per_step = 4
-    block = features.shape[1]
-    whole = lambda shape: pl.BlockSpec(shape, lambda i: (0,) * len(shape))
+    place = jnp.stack([at // line, at % 2]).astype(jnp.int32)
     first, drive, message = pl.pallas_call(
-        functools.partial(project_kernel, modes, length, total, per_step),
-        grid=(shard_count // per_step,),
-        in_specs=[
-            pl.BlockSpec((per_step, length, block), lambda i: (i, 0, 0)),
-            pl.BlockSpec((per_step * block, 3 * channels), lambda i: (i, 0)),
-            whole(taps.shape),
-            whole(decay_rate.shape),
-            whole(e.shape),
-        ],
-        out_specs=(whole((length, channels)), whole((length, channels)), whole((ROWS, channels))),
+        functools.partial(project_kernel, modes, length, total),
+        in_specs=[smem] + [vmem] * 10,
+        out_specs=(vmem,) * 3,
         out_shape=(
             jax.ShapeDtypeStruct((length, channels), f32),
             jax.ShapeDtypeStruct((length, channels), f32),
-            jax.ShapeDtypeStruct((ROWS, channels), f32),
+            jax.ShapeDtypeStruct((seq_count, ROWS, channels), f32),
         ),
         scratch_shapes=[
             pltpu.VMEM((length, 3 * channels), f32),
             pltpu.VMEM((length + TILE, 3 * channels), f32),
             pltpu.VMEM((2, length, channels), f32),
+            pltpu.VMEM((ROWS, channels), f32),
         ],
-        compiler_params=params,
+        compiler_params=params(16),
         name="project",
-    )(gathered, w_flat, taps, decay_rate, e)
-
-    spread = jnp.broadcast_to(message[None], (seq_count,) + message.shape)
-    everyone = lax.all_to_all(spread, "seq", 0, 0).reshape(seq_count * ROWS, channels)
+    )(place, *pieces, w_branch, taps, decay_rate, e)
+
+    everyone = lax.all_to_all(message, "seq", 0, 0).reshape(seq_count * ROWS, channels)
 
     me = lax.axis_index("seq").astype(jnp.int32).reshape(1)
-    vmem = pl.BlockSpec(memory_space=pltpu.VMEM)
     return pl.pallas_call(
         functools.partial(finish_kernel, modes, length, total, seq_count),
-        in_specs=[pl.BlockSpec(memory_space=pltpu.SMEM)] + [vmem] * 9,
+        in_specs=[smem] + [vmem] * 9,
         out_specs=vmem,
         out_shape=jax.ShapeDtypeStruct((length, channels), features.dtype),
         scratch_shapes=[
@@ -258,7 +271,7 @@
             pltpu.VMEM((TILE, length, channels), f32),
             pltpu.VMEM((length, channels), f32),
         ],
-        compiler_params=params,
+        compiler_params=params(8),
         name="finish",
     )(me, everyone, first, drive, taps, decay_rate, gain, skip_gain.reshape(1, channels), h, e)
 

time: 184 us -> 86.3 us (0.47)
  waiting for transfers between devices: 119 us -> 11.8 us
  blocking collectives: 0 us -> 33.4 us
  between operations: 13.4 us -> 0.12 us
  local copies, waits for them, and re-layouts: 17.1 us -> 4.07 us
  starting transfers between devices: 27.7 us -> 30.2 us
    all_gather x1 -> x0, waiting for transfers between devices: 110 us -> none  [gather_features(): return lax.all_gather(features, 'shard', axis=0)]
    all_gather x0 -> x1, blocking collectives: none -> 33.4 us  [gather_features(): near = lax.all_gather(features, 'shard', axis=0, axis_index_groups=groups)]
    ppermute x0 -> x5, starting transfers between devices: none -> 15.1 us  [the longest x1 4.43 us: gather_features(): far_up = lax.ppermute(far[:half], 'shard', up)]
    all_to_all x1, starting transfers between devices: 27.7 us -> 15.1 us  [shards(): lax.all_to_all(message, 'seq', 0, 0).reshape(seq_count * ROWS, channels)]
    unnamed x25 -> x12, local copies, waits for them, and re-layouts: 12.9 us -> 3.29 us
    reshape x2 -> x1, local copies, waits for them, and re-layouts: 3.49 us -> 0.01 us  [shards(): lax.dynamic_slice_in_dim(short_filter, at * channels, channels, 2)]
    ppermute x0 -> x5, waiting for transfers between devices: none -> 2.88 us  [the longest x1 1.31 us: gather_features(): far = lax.ppermute(near, 'shard', across)]
  transfers between devices with their start and end apart: 2 -> 6, of which waited for: 2 -> 4; matrix products, arithmetic and copies ran while one was open for 5% -> 2% of each run, Pallas kernels for 0% -> 0%
where the time goes in v2:
time: 86.3 us; the launch traced here: 85.7 us
  blocking collectives  33.4 us (39%)
  starting transfers between devices  30.2 us (35%)
  waiting for transfers between devices  11.8 us (14%)
  Pallas kernels  5.26 us (6%)
  local copies, waits for them, and re-layouts  4.07 us (5%)
    all_gather x1, blocking collectives, gather_features(): near = lax.all_gather(features, 'shard', axis=0, axis_index_groups=groups)  33.4 us
    all_to_all x1, starting transfers between devices, shards(): lax.all_to_all(message, 'seq', 0, 0).reshape(seq_count * ROWS, channels)  15.1 us
    all_to_all x1, waiting for transfers between devices, shards(): lax.all_to_all(message, 'seq', 0, 0).reshape(seq_count * ROWS, channels)  8.91 us
    ppermute x1, starting transfers between devices, gather_features(): far_up = lax.ppermute(far[:half], 'shard', up)  4.43 us
    unnamed x12, local copies, waits for them, and re-layouts  3.29 us
    ppermute x1, starting transfers between devices, gather_features(): near_up = lax.ppermute(near[:half], 'shard', up)  3.28 us
    ppermute x1, starting transfers between devices, gather_features(): far = lax.ppermute(near, 'shard', across)  3.19 us
    pallas_call x1, Pallas kernels, shards(): pl.pallas_call(functools.partial(project_kernel, modes, length, total), i...  2.81 us
  transfers between devices with their start and end apart: 6, of which 4 were waited for; matrix products, arithmetic and copies ran while one was open for 2% of the time, Pallas kernels for 0%

profile of v2, /device:TPU:1, one launch (start us, length us, event | category | flops | bytes accessed | tf_op | source)
XLA Modules:
  0.0 85.7 jit_solution(14914826242372431965)
XLA Ops:
  0.0 0.0 copy-start
  0.0 33.4 %all-gather = bf16[2048,128]{1,0:T(8,128)(2,1)S(1)} all-gather(bf16[256,128]{1,0:T(8,128)(2,1)} %param.6), channel_id=2, replica_groups={{0,2,4,6,8,10,12,14},{1,3,5,7,9,11,13,15},{16,18,20,22,24,26,28,30},{17..., dimensions={0}, use_global_device_ids=true | all-gather | bytes 589824 | tf_op jit(solution)/shard_map/all_gather | solution.py:201
  33.5 3.2 %collective-permute-start.2 = (bf16[8,256,128]{2,1,0:T(8,128)(2,1)S(1)}, bf16[8,256,128]{2,1,0:T(8,128)(2,1)S(1)}, u32[]{:S(2)}, u32[]{:S(2)}) collective-permute-start(bf16[8,256,128]{2,1,0:T(8,128)(2,1)S(1)} %bitcast.9), channel_id=1, source_target_pairs={{0,16},{1,17},{2,18},{3,19},{4,20},{5,21},{6,22},{7,23},{8,24},{9,... | collective-permute-start | bytes 1572872 | tf_op jit(solution)/shard_map/ppermute | solution.py:202
  36.7 3.3 %collective-permute-start = (bf16[4,256,128]{2,1,0:T(8,128)(2,1)S(1)}, bf16[4,256,128]{2,1,0:T(8,128)(2,1)S(1)}, u32[]{:S(2)}, u32[]{:S(2)}) collective-permute-start(bf16[4,256,128]{2,1,0:T(8,128)(2,1)S(1)} %bitcast.15), channel_id=1, source_target_pairs={{0,15},{1,0},{2,1},{3,2},{4,3},{5,4},{6,5},{7,6},{8,7},{9,8},{10,9... | collective-permute-start | bytes 786440 | tf_op jit(solution)/shard_map/ppermute | solution.py:203
  40.0 2.0 %collective-permute-start.1 = (bf16[4,256,128]{2,1,0:T(8,128)(2,1)S(1)}, bf16[4,256,128]{2,1,0:T(8,128)(2,1)S(1)}, u32[]{:S(2)}, u32[]{:S(2)}) collective-permute-start(bf16[4,256,128]{2,1,0:T(8,128)(2,1)S(1)} %bitcast.14), channel_id=1, source_target_pairs={{0,1},{1,2},{2,3},{3,4},{4,5},{5,6},{6,7},{7,8},{8,9},{9,10},{10,1... | collective-permute-start | bytes 786440 | tf_op jit(solution)/shard_map/ppermute | solution.py:204
  42.0 0.0 copy-done
  42.1 1.3 %collective-permute-done.2.far_ref = bf16[8,256,128]{2,1,0:T(8,128)(2,1)S(1)} collective-permute-done((bf16[8,256,128]{2,1,0:T(8,128)(2,1)S(1)}, bf16[8,256,128]{2,1,0:T(8,128)(2,1)S(1)}, u32[]{:S(2)}, u32[]{:S(2)}) %collective-permute-start.2) | collective-permute-done | bytes 524320 | tf_op jit(solution)/shard_map/ppermute | solution.py:202
  43.4 0.7 fusion
  44.1 0.0 copy-start.4
  44.1 0.0 copy-start.5
  44.1 2.2 %collective-permute-start.4 = (bf16[4,256,128]{2,1,0:T(8,128)(2,1)}, bf16[4,256,128]{2,1,0:T(8,128)(2,1)S(1)}, u32[]{:S(2)}, u32[]{:S(2)}) collective-permute-start(bf16[4,256,128]{2,1,0:T(8,128)(2,1)} %get-tuple-element.15), channel_id=1, source_target_pairs={{0,1},{1,2},{2,3},{3,4},{4,5},{5,6},{6,7},{7,8},{8,9},{9,10},{10,1... | collective-permute-start | bytes 786440 | tf_op jit(solution)/shard_map/ppermute | solution.py:206
  46.3 4.4 %collective-permute-start.3 = (bf16[4,256,128]{2,1,0:T(8,128)(2,1)S(1)}, bf16[4,256,128]{2,1,0:T(8,128)(2,1)S(1)}, u32[]{:S(2)}, u32[]{:S(2)}) collective-permute-start(bf16[4,256,128]{2,1,0:T(8,128)(2,1)S(1)} %get-tuple-element.16), channel_id=1, source_target_pairs={{0,15},{1,0},{2,1},{3,2},{4,3},{5,4},{6,5},{7,6},{8,7},{9,8},{10,9... | collective-permute-start | bytes 786440 | tf_op jit(solution)/shard_map/ppermute | solution.py:205
  50.7 0.7 sqrt_multiply_fusion.gain_ref
  51.5 0.0 copy-start.2
  51.5 0.7 copy-done.2
  52.2 0.2 tables.1
  52.4 0.1 pad_add_fusion.place_ref
  52.5 0.0 collective-permute-done.near_up_ref
  52.5 0.0 collective-permute-done.1.near_down_ref
  52.5 0.7 collective-permute-done.4.far_down_ref
  53.2 0.8 collective-permute-done.3.far_up_ref
  54.0 0.0 copy-start.1
  54.0 1.9 %copy-done.1 = bf16[4096,3,128]{2,0,1:T(8,128)(2,1)S(1)} copy-done((bf16[4096,3,128]{2,0,1:T(8,128)(2,1)S(1)}, bf16[4096,3,128]{2,0,1:T(8,128)(2,1)}, u32[]{:S(2)}) %copy-start.1) | copy-done | bytes 3145752
  55.9 0.0 copy-start.3
  55.9 0.7 copy-done.3
  56.6 2.8 %project.1 = (f32[256,128]{1,0:T(8,128)S(1)}, f32[256,128]{1,0:T(8,128)S(1)}, f32[16,32,128]{2,1,0:T(8,128)}) custom-call(s32[2]{0:T(128)S(1)} %pad_add_fusion.place_ref, bf16[8,256,128]{2,1,0:T(8,128)(2,1)S(1)} %bitcast.10, bf16[4,256,128]{2,1,0:T(8,128)(2,1)S(1)} %collective-permute-done.near_up_ref, ...), custom_call_target="tpu_custom_call" | custom-call | tf_op jit(solution)/shard_map/project/pallas_call | solution.py:242
  59.4 15.1 %all-to-all-start = ((f32[16,32,128]{2,1,0:T(8,128)}), f32[16,32,128]{2,1,0:T(8,128)S(1)}, u32[]{:S(2)}, u32[]{:S(2)}) async-start(f32[16,32,128]{2,1,0:T(8,128)} %get-tuple-element.11), calls=%async_computation | async-start | bytes 524288 | tf_op jit(solution)/shard_map/all_to_all | solution.py:261
  74.5 8.9 %all-to-all-done = f32[16,32,128]{2,1,0:T(8,128)S(1)} async-done(((f32[16,32,128]{2,1,0:T(8,128)}), f32[16,32,128]{2,1,0:T(8,128)S(1)}, u32[]{:S(2)}, u32[]{:S(2)}) %all-to-all-start) | async-done | bytes 262176 | tf_op jit(solution)/shard_map/all_to_all | solution.py:261
  83.4 0.0 copy-done.4
  83.4 0.0 copy-done.5
  83.4 2.3 %finish.1 = bf16[256,128]{1,0:T(8,128)(2,1)} custom-call(s32[1]{0:T(128)} %bitcast.me_ref, f32[512,128]{1,0:T(8,128)S(1)} %bitcast.12, f32[256,128]{1,0:T(8,128)S(1)} %get-tuple-element.12.first_ref, f32[256,128]{1,0:T(8,128)S(1)} %get-tuple-element.13.drive_ref, f32[9,128]{1,0:T(8,128)S(1)} %reshape.13.taps_ref, f32[16,128]{1,0:T(8,128)S(1)} %copy-done.4, ...), custom_call_target="tpu_custom_call" | custom-call | tf_op jit(solution)/shard_map/finish/pallas_call | solution.py:264
  (3 shorter events, 0.1 us)
Async XLA Ops:
  0.0 42.0 %copy-start = (f32[3,3,4096]{2,1,0:T(4,128)S(1)}, f32[3,3,4096]{2,1,0:T(4,128)}, u32[]{:S(2)}) copy-start(f32[3,3,4096]{2,1,0:T(4,128)} %param.8) | copy-start | bytes 442372
  33.5 9.9 %collective-permute-start.2 = (bf16[8,256,128]{2,1,0:T(8,128)(2,1)S(1)}, bf16[8,256,128]{2,1,0:T(8,128)(2,1)S(1)}, u32[]{:S(2)}, u32[]{:S(2)}) collective-permute-start(bf16[8,256,128]{2,1,0:T(8,128)(2,1)S(1)} %bitcast.9), channel_id=1, source_target_pairs={{0,16},{1,17},{2,18},{3,19},{4,20},{5,21},{6,22},{7,23},{8,24},{9,... | collective-permute-start | bytes 1572872 | tf_op jit(solution)/shard_map/ppermute | solution.py:202
  36.7 15.8 %collective-permute-start = (bf16[4,256,128]{2,1,0:T(8,128)(2,1)S(1)}, bf16[4,256,128]{2,1,0:T(8,128)(2,1)S(1)}, u32[]{:S(2)}, u32[]{:S(2)}) collective-permute-start(bf16[4,256,128]{2,1,0:T(8,128)(2,1)S(1)} %bitcast.15), channel_id=1, source_target_pairs={{0,15},{1,0},{2,1},{3,2},{4,3},{5,4},{6,5},{7,6},{8,7},{9,8},{10,9... | collective-permute-start | bytes 786440 | tf_op jit(solution)/shard_map/ppermute | solution.py:203
  40.0 12.5 %collective-permute-start.1 = (bf16[4,256,128]{2,1,0:T(8,128)(2,1)S(1)}, bf16[4,256,128]{2,1,0:T(8,128)(2,1)S(1)}, u32[]{:S(2)}, u32[]{:S(2)}) collective-permute-start(bf16[4,256,128]{2,1,0:T(8,128)(2,1)S(1)} %bitcast.14), channel_id=1, source_target_pairs={{0,1},{1,2},{2,3},{3,4},{4,5},{5,6},{6,7},{7,8},{8,9},{9,10},{10,1... | collective-permute-start | bytes 786440 | tf_op jit(solution)/shard_map/ppermute | solution.py:204
  44.1 39.3 %copy-start.4 = (f32[16,128]{1,0:T(8,128)S(1)}, f32[16,128]{1,0:T(8,128)}, u32[]{:S(2)}) copy-start(f32[16,128]{1,0:T(8,128)} %rate_ref.5) | copy-start | bytes 24580
  44.1 39.3 %copy-start.5 = (f32[128]{0:T(128)S(1)}, f32[128]{0:T(128)}, u32[]{:S(2)}) copy-start(f32[128]{0:T(128)} %param.11) | copy-start | bytes 1540
  44.1 9.1 %collective-permute-start.4 = (bf16[4,256,128]{2,1,0:T(8,128)(2,1)}, bf16[4,256,128]{2,1,0:T(8,128)(2,1)S(1)}, u32[]{:S(2)}, u32[]{:S(2)}) collective-permute-start(bf16[4,256,128]{2,1,0:T(8,128)(2,1)} %get-tuple-element.15), channel_id=1, source_target_pairs={{0,1},{1,2},{2,3},{3,4},{4,5},{5,6},{6,7},{7,8},{8,9},{9,10},{10,1... | collective-permute-start | bytes 786440 | tf_op jit(solution)/shard_map/ppermute | solution.py:206
  46.3 7.7 %collective-permute-start.3 = (bf16[4,256,128]{2,1,0:T(8,128)(2,1)S(1)}, bf16[4,256,128]{2,1,0:T(8,128)(2,1)S(1)}, u32[]{:S(2)}, u32[]{:S(2)}) collective-permute-start(bf16[4,256,128]{2,1,0:T(8,128)(2,1)S(1)} %get-tuple-element.16), channel_id=1, source_target_pairs={{0,15},{1,0},{2,1},{3,2},{4,3},{5,4},{6,5},{7,6},{8,7},{9,8},{10,9... | collective-permute-start | bytes 786440 | tf_op jit(solution)/shard_map/ppermute | solution.py:205
  51.5 0.7 copy-start.2
  54.0 1.9 %copy-start.1 = (bf16[4096,3,128]{2,0,1:T(8,128)(2,1)S(1)}, bf16[4096,3,128]{2,0,1:T(8,128)(2,1)}, u32[]{:S(2)}) copy-start(bf16[4096,3,128]{2,0,1:T(8,128)(2,1)} %param.7) | copy-start | bytes 9437188
  55.9 0.7 copy-start.3
  59.4 24.0 %all-to-all-start = ((f32[16,32,128]{2,1,0:T(8,128)}), f32[16,32,128]{2,1,0:T(8,128)S(1)}, u32[]{:S(2)}, u32[]{:S(2)}) async-start(f32[16,32,128]{2,1,0:T(8,128)} %get-tuple-element.11), calls=%async_computation | async-start | bytes 524288 | tf_op jit(solution)/shard_map/all_to_all | solution.py:261

commit v3 on v2

--- a/solution.py
+++ b/solution.py
@@ -22,42 +22,60 @@
     for q in range(tiles):
         e_ref[q * modes : (q + 1) * modes, :] = jnp.exp(-step * float(TILE * q))
     scaled = [gain_ref[m : m + 1, :] * jnp.exp(-step[m : m + 1, :] * lane) for m in range(modes)]
+    h_ref[0:TILE, :] = jnp.zeros((TILE, step.shape[1]), jnp.float32)
     for q in range(tiles):
         total_tile = row_tile(e_ref, q * modes) * scaled[0]
         for m in range(1, modes):
             total_tile = total_tile + row_tile(e_ref, q * modes + m) * scaled[m]
-        h_ref[q * TILE : (q + 1) * TILE, :] = total_tile
+        h_ref[(q + 1) * TILE : (q + 2) * TILE, :] = total_tile
+
+
+def weight_rows(w_ref, owners, block):
+    rows = []
+    for owner in owners:
+        at = pl.ds(pl.multiple_of(owner * block, block), block)
+        rows.append(jnp.concatenate([w_ref[b, at, :] for b in range(3)], axis=1))
+    return jnp.concatenate(rows, axis=0)
+
+
+def early_kernel(place_ref, near_ref, near_up_ref, near_down_ref, far_ref, w_ref, acc_ref):
+    line, parity = place_ref[0], place_ref[1]
+    pairs, _, block = near_ref.shape
+    split = near_up_ref.shape[0]
+    for k in range(0, pairs, 2):
+        lefts, owners = [], []
+        for i in (k, k + 1):
+            odd = near_up_ref[i] if i < split else near_down_ref[i - split]
+            lefts += [near_ref[i], odd, far_ref[i]]
+            own, other = 2 * pairs * line + 2 * i, 2 * pairs * (1 - line) + 2 * i
+            owners += [own + parity, own + 1 - parity, other + parity]
+        part = jnp.dot(
+            jnp.concatenate(lefts, axis=1),
+            weight_rows(w_ref, owners, block),
+            preferred_element_type=jnp.float32,
+        )
+        acc_ref[...] = part if k == 0 else acc_ref[...] + part
 
 
 def project_kernel(
-    modes, length, total, place_ref, near_ref, near_up_ref, near_down_ref, far_ref, far_up_ref,
-    far_down_ref, w_ref, taps_ref, rate_ref, e_ref,
-    first_ref, drive_ref, message_ref, acc_ref, proj_ref, filt_ref, state_ref,
+    modes, length, total, place_ref, early_ref, far_up_ref, far_down_ref, w_ref, taps_ref, rate_ref,
+    e_ref, first_ref, drive_ref, message_ref, proj_ref, filt_ref, state_ref,
 ):
     line, parity = place_ref[0], place_ref[1]
-    pairs, _, block = near_ref.shape
+    split, _, block = far_up_ref.shape
+    pairs = 2 * split
     channels = drive_ref.shape[1]
-    split = near_up_ref.shape[0]
-
-    def weight(owner):
-        at = pl.ds(pl.multiple_of(owner * block, block), block)
-        return jnp.concatenate([w_ref[b, at, :] for b in range(3)], axis=1)
-
-    for k in range(pairs):
-        near_odd = near_up_ref[k] if k < split else near_down_ref[k - split]
-        far_odd = far_up_ref[k] if k < split else far_down_ref[k - split]
-        left = jnp.concatenate([near_ref[k], near_odd, far_ref[k], far_odd], axis=1)
-        own, other = 2 * pairs * line + 2 * k, 2 * pairs * (1 - line) + 2 * k
-        right = jnp.concatenate(
-            [weight(own + parity), weight(own + 1 - parity), weight(other + parity), weight(other + 1 - parity)],
-            axis=0,
+    acc = early_ref[...]
+    for ref, start in ((far_up_ref, 0), (far_down_ref, split)):
+        owners = [2 * pairs * (1 - line) + 2 * (start + k) + 1 - parity for k in range(split)]
+        left = jnp.concatenate([ref[k] for k in range(split)], axis=1)
+        acc = acc + jnp.dot(
+            left, weight_rows(w_ref, owners, block), preferred_element_type=jnp.float32
         )
-        part = jnp.dot(left, right, preferred_element_type=jnp.float32)
-        acc_ref[...] = part if k == 0 else acc_ref[...] + part
 
     pad = TILE
     proj_ref[0:pad, :] = jnp.zeros((pad, 3 * channels), jnp.float32)
-    proj_ref[pad:, :] = acc_ref[...].astype(jnp.bfloat16).astype(jnp.float32)
+    proj_ref[pad:, :] = acc.astype(jnp.bfloat16).astype(jnp.float32)
     for b in range(3):
         cols = slice(b * channels, (b + 1) * channels)
         value = taps_ref[b : b + 1, :] * proj_ref[pad : pad + length, cols]
@@ -69,10 +87,10 @@
             filt_ref[b - 1] = value
     drive_ref[...] = filt_ref[0] * filt_ref[1]
     row = jax.lax.broadcasted_iota(jnp.int32, (TILE, channels), 0)
+    drive_ref[0:TILE, :] = jnp.where(row < 2, 0.0, drive_ref[0:TILE, :])
     lag = (TILE - 1 - row).astype(jnp.float32)
     tiles = length // TILE
     pieces = [drive_ref[q * TILE : (q + 1) * TILE, :] for q in range(tiles)]
-    pieces[0] = jnp.where(row < 2, 0.0, pieces[0])
     step = rate_ref[...] * (1.0 / total)
     for m in range(modes):
         state = row_tile(e_ref, (tiles - 1) * modes + m) * pieces[0]
@@ -95,12 +113,43 @@
         message_ref[s] = state_ref[...]
 
 
+def conv_kernel(length, drive_ref, h_ref, skip_ref, conv_ref, pad_ref, lag_ref):
+    channels = drive_ref.shape[1]
+    tiles = length // TILE
+    pad_ref[0:TILE, :] = jnp.zeros((TILE, channels), jnp.float32)
+    pad_ref[TILE:, :] = drive_ref[...]
+    for j in range(TILE):
+        lag_ref[j] = pad_ref[TILE - j : TILE - j + length, :]
+
+    group = 8
+    for g in range(tiles // group):
+        low = g * group
+
+        def over_lags(j, accs):
+            accs = list(accs)
+            window = [lag_ref[j, pl.ds((low + i) * TILE, TILE), :] for i in range(group)]
+            for p in range(low + group):
+                weight = jnp.broadcast_to(h_ref[pl.ds(TILE * (p + 1) + j, 1), :], (TILE, channels))
+                for i in range(group):
+                    if low + i - p >= 0:
+                        accs[i] = accs[i] + weight * window[i]
+                below = low - p - 1
+                fresh = lag_ref[j, pl.ds(below * TILE, TILE), :] if below >= 0 else None
+                window = [fresh] + window[:-1]
+            return tuple(accs)
+
+        accs = tuple(skip_ref[...] * drive_ref[(low + i) * TILE : (low + i + 1) * TILE, :] for i in range(group))
+        accs = lax.fori_loop(0, TILE, over_lags, accs)
+        for i in range(group):
+            conv_ref[(low + i) * TILE : (low + i + 1) * TILE, :] = accs[i]
+
+
 def finish_kernel(
-    modes, length, total, seq_count, me_ref, all_ref, first_ref, drive_ref, taps_ref, rate_ref,
-    gain_ref, skip_ref, h_ref, e_ref, out_ref, pad_ref, lag_ref, conv_ref,
+    modes, length, total, seq_count, me_ref, all_ref, first_ref, conv_ref, taps_ref, rate_ref,
+    gain_ref, skip_ref, h_ref, e_ref, out_ref, value_ref,
 ):
     me = me_ref[0]
-    channels = drive_ref.shape[1]
+    channels = conv_ref.shape[1]
     tiles = length // TILE
     step = rate_ref[...] * (1.0 / total)
 
@@ -140,36 +189,6 @@
     extra0 = tap(1, 0) * rim1 + tap(2, 0) * rim0
     extra1 = tap(2, 0) * rim1
 
-    pad_ref[0:TILE, :] = jnp.zeros((TILE, channels), jnp.float32)
-    pad_ref[TILE:, :] = drive_ref[...]
-    head = drive_ref[0:TILE, :]
-    head = jnp.where(row == 0, mine0, jnp.where(row == 1, mine1, head))
-    pad_ref[TILE : 2 * TILE, :] = head
-    for j in range(TILE):
-        lag_ref[j] = pad_ref[TILE - j : TILE - j + length, :]
-
-    group = 8
-    for g in range(tiles // group):
-        low = g * group
-
-        def over_lags(j, accs):
-            accs = list(accs)
-            window = [lag_ref[j, pl.ds((low + i) * TILE, TILE), :] for i in range(group)]
-            for p in range(low + group):
-                weight = jnp.broadcast_to(h_ref[pl.ds(TILE * p + j, 1), :], (TILE, channels))
-                for i in range(group):
-                    if low + i - p >= 0:
-                        accs[i] = accs[i] + weight * window[i]
-                below = low - p - 1
-                fresh = lag_ref[j, pl.ds(below * TILE, TILE), :] if below >= 0 else None
-                window = [fresh] + window[:-1]
-            return tuple(accs)
-
-        zero = jnp.zeros((TILE, channels), jnp.float32)
-        accs = lax.fori_loop(0, TILE, over_lags, (zero,) * group)
-        for i in range(group):
-            conv_ref[(low + i) * TILE : (low + i + 1) * TILE, :] = accs[i]
-
     lead = (row + 1).astype(jnp.float32)
     heads = []
     for m in range(modes):
@@ -178,14 +197,17 @@
     skip = skip_ref[...]
     for q in range(tiles):
         at = slice(q * TILE, (q + 1) * TILE)
-        value = conv_ref[at, :] + skip * pad_ref[(q + 1) * TILE : (q + 2) * TILE, :]
+        value = conv_ref[at, :]
+        value = value + mine0 * h_ref[(q + 1) * TILE : (q + 2) * TILE, :]
+        value = value + mine1 * h_ref[(q + 1) * TILE - 1 : (q + 2) * TILE - 1, :]
         for m in range(modes):
             value = value + row_tile(e_ref, q * modes + m) * heads[m]
         gate = first_ref[at, :]
         if q == 0:
+            value = value + jnp.where(row == 0, skip * mine0, jnp.where(row == 1, skip * mine1, 0.0))
             gate = gate + jnp.where(row == 0, extra0, jnp.where(row == 1, extra1, 0.0))
-        conv_ref[at, :] = gate * value
-    out_ref[...] = conv_ref[...].astype(out_ref.dtype)
+        value_ref[at, :] = gate * value
+    out_ref[...] = value_ref[...].astype(out_ref.dtype)
 
 
 def gather_features(features):
@@ -231,7 +253,7 @@
     h, e = pl.pallas_call(
         functools.partial(tables_kernel, modes, length, total),
         out_shape=(
-            jax.ShapeDtypeStruct((length, channels), f32),
+            jax.ShapeDtypeStruct((length + TILE, channels), f32),
             jax.ShapeDtypeStruct((tiles * modes, channels), f32),
         ),
         compiler_params=params(4),
@@ -239,9 +261,18 @@
     )(decay_rate, gain)
 
     place = jnp.stack([at // line, at % 2]).astype(jnp.int32)
+    near, near_up, near_down, far, far_up, far_down = pieces
+    early = pl.pallas_call(
+        early_kernel,
+        in_specs=[smem] + [vmem] * 5,
+        out_specs=vmem,
+        out_shape=jax.ShapeDtypeStruct((length, 3 * channels), f32),
+        compiler_params=params(12),
+        name="early",
+    )(place, near, near_up, near_down, far, w_branch)
     first, drive, message = pl.pallas_call(
         functools.partial(project_kernel, modes, length, total),
-        in_specs=[smem] + [vmem] * 10,
+        in_specs=[smem] + [vmem] * 7,
         out_specs=(vmem,) * 3,
         out_shape=(
             jax.ShapeDtypeStruct((length, channels), f32),
@@ -249,16 +280,28 @@
             jax.ShapeDtypeStruct((seq_count, ROWS, channels), f32),
         ),
         scratch_shapes=[
-            pltpu.VMEM((length, 3 * channels), f32),
             pltpu.VMEM((length + TILE, 3 * channels), f32),
             pltpu.VMEM((2, length, channels), f32),
             pltpu.VMEM((ROWS, channels), f32),
         ],
-        compiler_params=params(16),
+        compiler_params=params(12),
         name="project",
-    )(place, *pieces, w_branch, taps, decay_rate, e)
+    )(place, early, far_up, far_down, w_branch, taps, decay_rate, e)
 
     everyone = lax.all_to_all(message, "seq", 0, 0).reshape(seq_count * ROWS, channels)
+    skip = skip_gain.reshape(1, channels)
+    conv = pl.pallas_call(
+        functools.partial(conv_kernel, length),
+        in_specs=[vmem] * 3,
+        out_specs=vmem,
+        out_shape=jax.ShapeDtypeStruct((length, channels), f32),
+        scratch_shapes=[
+            pltpu.VMEM((length + TILE, channels), f32),
+            pltpu.VMEM((TILE, length, channels), f32),
+        ],
+        compiler_params=params(6),
+        name="conv",
+    )(drive, h, skip)
 
     me = lax.axis_index("seq").astype(jnp.int32).reshape(1)
     return pl.pallas_call(
@@ -266,14 +309,10 @@
         in_specs=[smem] + [vmem] * 9,
         out_specs=vmem,
         out_shape=jax.ShapeDtypeStruct((length, channels), features.dtype),
-        scratch_shapes=[
-            pltpu.VMEM((length + TILE, channels), f32),
-            pltpu.VMEM((TILE, length, channels), f32),
-            pltpu.VMEM((length, channels), f32),
-        ],
-        compiler_params=params(8),
+        scratch_shapes=[pltpu.VMEM((length, channels), f32)],
+        compiler_params=params(6),
         name="finish",
-    )(me, everyone, first, drive, taps, decay_rate, gain, skip_gain.reshape(1, channels), h, e)
+    )(me, everyone, first, conv, taps, decay_rate, gain, skip, h, e)
 
 
 def solution(mesh):

time: 86.3 us -> 83.6 us (0.969)
  starting transfers between devices: 30.2 us -> 26.8 us
    pallas_call x0 -> x2, Pallas kernels: none -> 2.91 us  [the longest x1 1.53 us: shards(): pl.pallas_call(early_kernel, in_specs=[smem] + [vmem] * 5, out_specs=vmem...]
    ppermute x1, waiting for transfers between devices: 0.72 us -> 3.6 us  [gather_features(): far_down = lax.ppermute(far[half:], 'shard', down)]
    all_to_all x1, starting transfers between devices: 15.1 us -> 13.1 us  [shards(): lax.all_to_all(message, 'seq', 0, 0).reshape(seq_count * ROWS, channels)]
    all_to_all x1, waiting for transfers between devices: 8.91 us -> 7.51 us  [shards(): lax.all_to_all(message, 'seq', 0, 0).reshape(seq_count * ROWS, channels)]
    pallas_call x1, Pallas kernels: 2.26 us -> 0.92 us  [shards(): pl.pallas_call(functools.partial(finish_kernel, modes, length, total, seq...]
    ppermute x1, starting transfers between devices: 4.43 us -> 3.27 us  [gather_features(): far_up = lax.ppermute(far[:half], 'shard', up)]
  transfers between devices with their start and end apart: 6 -> 6, of which waited for: 4 -> 3; matrix products, arithmetic and copies ran while one was open for 2% -> 2% of each run, Pallas kernels for 0% -> 4%
where the time goes in v3:
time: 83.6 us; the launch traced here: 83.1 us
  blocking collectives  33.4 us (40%)
  starting transfers between devices  26.8 us (32%)
  waiting for transfers between devices  12.4 us (15%)
  Pallas kernels  6.02 us (7%)
  local copies, waits for them, and re-layouts  3.39 us (4%)
    all_gather x1, blocking collectives, gather_features(): near = lax.all_gather(features, 'shard', axis=0, axis_index_groups=groups)  33.4 us
    all_to_all x1, starting transfers between devices, shards(): lax.all_to_all(message, 'seq', 0, 0).reshape(seq_count * ROWS, channels)  13.1 us
    all_to_all x1, waiting for transfers between devices, shards(): lax.all_to_all(message, 'seq', 0, 0).reshape(seq_count * ROWS, channels)  7.51 us
    ppermute x1, waiting for transfers between devices, gather_features(): far_down = lax.ppermute(far[half:], 'shard', down)  3.6 us
    ppermute x1, starting transfers between devices, gather_features(): near_up = lax.ppermute(near[:half], 'shard', up)  3.28 us
    ppermute x1, starting transfers between devices, gather_features(): far_up = lax.ppermute(far[:half], 'shard', up)  3.27 us
    ppermute x1, starting transfers between devices, gather_features(): far = lax.ppermute(near, 'shard', across)  3.19 us
    unnamed x12, local copies, waits for them, and re-layouts  2.6 us
  transfers between devices with their start and end apart: 6, of which 3 were waited for; matrix products, arithmetic and copies ran while one was open for 2% of the time, Pallas kernels for 4%

profile of v3, /device:TPU:1, one launch (start us, length us, event | category | flops | bytes accessed | tf_op | source)
XLA Modules:
  0.0 83.1 jit_solution(8104609956914297120)
XLA Ops:
  0.0 0.0 copy-start
  0.0 33.4 %all-gather = bf16[2048,128]{1,0:T(8,128)(2,1)S(1)} all-gather(bf16[256,128]{1,0:T(8,128)(2,1)} %param.6), channel_id=2, replica_groups={{0,2,4,6,8,10,12,14},{1,3,5,7,9,11,13,15},{16,18,20,22,24,26,28,30},{17..., dimensions={0}, use_global_device_ids=true | all-gather | bytes 589824 | tf_op jit(solution)/shard_map/all_gather | solution.py:223
  33.5 3.2 %collective-permute-start.2 = (bf16[8,256,128]{2,1,0:T(8,128)(2,1)S(1)}, bf16[8,256,128]{2,1,0:T(8,128)(2,1)S(1)}, u32[]{:S(2)}, u32[]{:S(2)}) collective-permute-start(bf16[8,256,128]{2,1,0:T(8,128)(2,1)S(1)} %bitcast.11), channel_id=1, source_target_pairs={{0,16},{1,17},{2,18},{3,19},{4,20},{5,21},{6,22},{7,23},{8,24},{9,... | collective-permute-start | bytes 1572872 | tf_op jit(solution)/shard_map/ppermute | solution.py:224
  36.7 3.3 %collective-permute-start = (bf16[4,256,128]{2,1,0:T(8,128)(2,1)S(1)}, bf16[4,256,128]{2,1,0:T(8,128)(2,1)S(1)}, u32[]{:S(2)}, u32[]{:S(2)}) collective-permute-start(bf16[4,256,128]{2,1,0:T(8,128)(2,1)S(1)} %bitcast.17), channel_id=1, source_target_pairs={{0,15},{1,0},{2,1},{3,2},{4,3},{5,4},{6,5},{7,6},{8,7},{9,8},{10,9... | collective-permute-start | bytes 786440 | tf_op jit(solution)/shard_map/ppermute | solution.py:225
  40.0 2.0 %collective-permute-start.1 = (bf16[4,256,128]{2,1,0:T(8,128)(2,1)S(1)}, bf16[4,256,128]{2,1,0:T(8,128)(2,1)S(1)}, u32[]{:S(2)}, u32[]{:S(2)}) collective-permute-start(bf16[4,256,128]{2,1,0:T(8,128)(2,1)S(1)} %bitcast.16), channel_id=1, source_target_pairs={{0,1},{1,2},{2,3},{3,4},{4,5},{5,6},{6,7},{7,8},{8,9},{9,10},{10,1... | collective-permute-start | bytes 786440 | tf_op jit(solution)/shard_map/ppermute | solution.py:226
  42.0 0.0 copy-start.4
  42.0 0.0 copy-done
  42.1 1.3 %collective-permute-done.2.far_ref = bf16[8,256,128]{2,1,0:T(8,128)(2,1)S(1)} collective-permute-done((bf16[8,256,128]{2,1,0:T(8,128)(2,1)S(1)}, bf16[8,256,128]{2,1,0:T(8,128)(2,1)S(1)}, u32[]{:S(2)}, u32[]{:S(2)}) %collective-permute-start.2) | collective-permute-done | bytes 524320 | tf_op jit(solution)/shard_map/ppermute | solution.py:224
  43.4 0.7 fusion
  44.1 3.3 %collective-permute-start.3 = (bf16[4,256,128]{2,1,0:T(8,128)(2,1)}, bf16[4,256,128]{2,1,0:T(8,128)(2,1)S(1)}, u32[]{:S(2)}, u32[]{:S(2)}) collective-permute-start(bf16[4,256,128]{2,1,0:T(8,128)(2,1)} %get-tuple-element.16), channel_id=1, source_target_pairs={{0,15},{1,0},{2,1},{3,2},{4,3},{5,4},{6,5},{7,6},{8,7},{9,8},{10,9... | collective-permute-start | bytes 786440 | tf_op jit(solution)/shard_map/ppermute | solution.py:227
  47.4 2.0 %collective-permute-start.4 = (bf16[4,256,128]{2,1,0:T(8,128)(2,1)S(1)}, bf16[4,256,128]{2,1,0:T(8,128)(2,1)S(1)}, u32[]{:S(2)}, u32[]{:S(2)}) collective-permute-start(bf16[4,256,128]{2,1,0:T(8,128)(2,1)S(1)} %get-tuple-element.15), channel_id=1, source_target_pairs={{0,1},{1,2},{2,3},{3,4},{4,5},{5,6},{6,7},{7,8},{8,9},{9,10},{10,1... | collective-permute-start | bytes 786440 | tf_op jit(solution)/shard_map/ppermute | solution.py:228
  49.4 0.7 sqrt_multiply_fusion.gain_ref
  50.1 0.0 copy-start.3
  50.1 0.7 copy-done.3
  50.8 0.2 tables.1
  51.0 0.1 pad_add_fusion.place_ref
  51.1 0.0 collective-permute-done.near_up_ref
  51.1 0.0 collective-permute-done.1.near_down_ref
  51.1 0.0 copy-start.1
  51.1 1.9 %copy-done.1 = bf16[4096,3,128]{2,0,1:T(8,128)(2,1)S(1)} copy-done((bf16[4096,3,128]{2,0,1:T(8,128)(2,1)S(1)}, bf16[4096,3,128]{2,0,1:T(8,128)(2,1)}, u32[]{:S(2)}) %copy-start.1) | copy-done | bytes 3145752
  53.0 1.5 %early.1.early_ref = f32[256,384]{1,0:T(8,128)S(1)} custom-call(s32[2]{0:T(128)S(1)} %pad_add_fusion.place_ref, bf16[8,256,128]{2,1,0:T(8,128)(2,1)S(1)} %bitcast.12, bf16[4,256,128]{2,1,0:T(8,128)(2,1)S(1)} %collective-permute-done.near_up_ref, bf16[4,256,128]{2,1,0:T(8,128)(2,1)S(1)} %collective-permute-done.1.near_down_ref, ...), custom_call_target="tpu_custom_call" | custom-call | tf_op jit(solution)/shard_map/early/pallas_call | solution.py:265
  54.5 0.0 copy-start.5
  54.6 0.0 collective-permute-done.3.far_up_ref
  54.6 3.6 %collective-permute-done.4.far_down_ref = bf16[4,256,128]{2,1,0:T(8,128)(2,1)S(1)} collective-permute-done((bf16[4,256,128]{2,1,0:T(8,128)(2,1)S(1)}, bf16[4,256,128]{2,1,0:T(8,128)(2,1)S(1)}, u32[]{:S(2)}, u32[]{:S(2)}) %collective-permute-start.4) | collective-permute-done | bytes 262176 | tf_op jit(solution)/shard_map/ppermute | solution.py:228
  58.2 0.0 copy-done.4
  58.2 0.0 copy-done.2
  58.2 2.0 %project.1 = (f32[256,128]{1,0:T(8,128)S(1)}, f32[256,128]{1,0:T(8,128)S(1)}, f32[16,32,128]{2,1,0:T(8,128)}) custom-call(s32[2]{0:T(128)S(1)} %pad_add_fusion.place_ref, f32[256,384]{1,0:T(8,128)S(1)} %early.1.early_ref, bf16[4,256,128]{2,1,0:T(8,128)(2,1)S(1)} %collective-permute-done.3.far_up_ref, ...), custom_call_target="tpu_custom_call" | custom-call | tf_op jit(solution)/shard_map/project/pallas_call | solution.py:273
  60.2 13.1 %all-to-all-start = ((f32[16,32,128]{2,1,0:T(8,128)}), f32[16,32,128]{2,1,0:T(8,128)S(1)}, u32[]{:S(2)}, u32[]{:S(2)}) async-start(f32[16,32,128]{2,1,0:T(8,128)} %get-tuple-element.11), calls=%async_computation | async-start | bytes 524288 | tf_op jit(solution)/shard_map/all_to_all | solution.py:291
  73.2 0.0 copy-done.5
  73.3 1.4 %conv.1.conv_ref = f32[256,128]{1,0:T(8,128)S(1)} custom-call(f32[256,128]{1,0:T(8,128)S(1)} %get-tuple-element.13.drive_ref, f32[264,128]{1,0:T(8,128)S(1)} %get-tuple-element.14.h_ref, f32[1,128]{1,0:T(1,128)S(1)} %bitcast.14), custom_call_target="tpu_custom_call" | custom-call | tf_op jit(solution)/shard_map/conv/pallas_call | solution.py:293
  74.6 7.5 %all-to-all-done = f32[16,32,128]{2,1,0:T(8,128)S(1)} async-done(((f32[16,32,128]{2,1,0:T(8,128)}), f32[16,32,128]{2,1,0:T(8,128)S(1)}, u32[]{:S(2)}, u32[]{:S(2)}) %all-to-all-start) | async-done | bytes 262176 | tf_op jit(solution)/shard_map/all_to_all | solution.py:291
  82.2 0.9 %finish.1 = bf16[256,128]{1,0:T(8,128)(2,1)} custom-call(s32[1]{0:T(128)} %bitcast.me_ref, f32[512,128]{1,0:T(8,128)S(1)} %bitcast.13, f32[256,128]{1,0:T(8,128)S(1)} %get-tuple-element.12.first_ref, f32[256,128]{1,0:T(8,128)S(1)} %conv.1.conv_ref, f32[9,128]{1,0:T(8,128)S(1)} %reshape.13.taps_ref, f32[16,128]{1,0:T(8,128)S(1)} %copy-done.4, ...), custom_call_target="tpu_custom_call" | custom-call | tf_op jit(solution)/shard_map/finish/pallas_call | solution.py:307
  (4 shorter events, 0.1 us)
Async XLA Ops:
  0.0 42.0 %copy-start = (f32[3,3,4096]{2,1,0:T(4,128)S(1)}, f32[3,3,4096]{2,1,0:T(4,128)}, u32[]{:S(2)}) copy-start(f32[3,3,4096]{2,1,0:T(4,128)} %param.8) | copy-start | bytes 442372
  33.5 9.9 %collective-permute-start.2 = (bf16[8,256,128]{2,1,0:T(8,128)(2,1)S(1)}, bf16[8,256,128]{2,1,0:T(8,128)(2,1)S(1)}, u32[]{:S(2)}, u32[]{:S(2)}) collective-permute-start(bf16[8,256,128]{2,1,0:T(8,128)(2,1)S(1)} %bitcast.11), channel_id=1, source_target_pairs={{0,16},{1,17},{2,18},{3,19},{4,20},{5,21},{6,22},{7,23},{8,24},{9,... | collective-permute-start | bytes 1572872 | tf_op jit(solution)/shard_map/ppermute | solution.py:224
  36.7 14.4 %collective-permute-start = (bf16[4,256,128]{2,1,0:T(8,128)(2,1)S(1)}, bf16[4,256,128]{2,1,0:T(8,128)(2,1)S(1)}, u32[]{:S(2)}, u32[]{:S(2)}) collective-permute-start(bf16[4,256,128]{2,1,0:T(8,128)(2,1)S(1)} %bitcast.17), channel_id=1, source_target_pairs={{0,15},{1,0},{2,1},{3,2},{4,3},{5,4},{6,5},{7,6},{8,7},{9,8},{10,9... | collective-permute-start | bytes 786440 | tf_op jit(solution)/shard_map/ppermute | solution.py:225
  40.0 11.1 %collective-permute-start.1 = (bf16[4,256,128]{2,1,0:T(8,128)(2,1)S(1)}, bf16[4,256,128]{2,1,0:T(8,128)(2,1)S(1)}, u32[]{:S(2)}, u32[]{:S(2)}) collective-permute-start(bf16[4,256,128]{2,1,0:T(8,128)(2,1)S(1)} %bitcast.16), channel_id=1, source_target_pairs={{0,1},{1,2},{2,3},{3,4},{4,5},{5,6},{6,7},{7,8},{8,9},{9,10},{10,1... | collective-permute-start | bytes 786440 | tf_op jit(solution)/shard_map/ppermute | solution.py:226
  42.0 16.2 %copy-start.4 = (f32[16,128]{1,0:T(8,128)S(1)}, f32[16,128]{1,0:T(8,128)}, u32[]{:S(2)}) copy-start(f32[16,128]{1,0:T(8,128)} %rate_ref.5) | copy-start | bytes 24580
  44.1 10.5 %collective-permute-start.3 = (bf16[4,256,128]{2,1,0:T(8,128)(2,1)}, bf16[4,256,128]{2,1,0:T(8,128)(2,1)S(1)}, u32[]{:S(2)}, u32[]{:S(2)}) collective-permute-start(bf16[4,256,128]{2,1,0:T(8,128)(2,1)} %get-tuple-element.16), channel_id=1, source_target_pairs={{0,15},{1,0},{2,1},{3,2},{4,3},{5,4},{6,5},{7,6},{8,7},{9,8},{10,9... | collective-permute-start | bytes 786440 | tf_op jit(solution)/shard_map/ppermute | solution.py:227
  47.4 10.8 %collective-permute-start.4 = (bf16[4,256,128]{2,1,0:T(8,128)(2,1)S(1)}, bf16[4,256,128]{2,1,0:T(8,128)(2,1)S(1)}, u32[]{:S(2)}, u32[]{:S(2)}) collective-permute-start(bf16[4,256,128]{2,1,0:T(8,128)(2,1)S(1)} %get-tuple-element.15), channel_id=1, source_target_pairs={{0,1},{1,2},{2,3},{3,4},{4,5},{5,6},{6,7},{7,8},{8,9},{9,10},{10,1... | collective-permute-start | bytes 786440 | tf_op jit(solution)/shard_map/ppermute | solution.py:228
  50.1 0.7 copy-start.3
  51.1 1.9 %copy-start.1 = (bf16[4096,3,128]{2,0,1:T(8,128)(2,1)S(1)}, bf16[4096,3,128]{2,0,1:T(8,128)(2,1)}, u32[]{:S(2)}) copy-start(bf16[4096,3,128]{2,0,1:T(8,128)(2,1)} %param.7) | copy-start | bytes 9437188
  53.0 5.2 %copy-start.2 = (bf16[4096,3,128]{2,0,1:T(8,128)(2,1)S(1)}, bf16[4096,3,128]{2,0,1:T(8,128)(2,1)}, u32[]{:S(2)}) copy-start(bf16[4096,3,128]{2,0,1:T(8,128)(2,1)} %param.7) | copy-start | bytes 9437188
  54.5 18.7 %copy-start.5 = (f32[128]{0:T(128)S(1)}, f32[128]{0:T(128)}, u32[]{:S(2)}) copy-start(f32[128]{0:T(128)} %param.11) | copy-start | bytes 1540
  60.2 22.0 %all-to-all-start = ((f32[16,32,128]{2,1,0:T(8,128)}), f32[16,32,128]{2,1,0:T(8,128)S(1)}, u32[]{:S(2)}, u32[]{:S(2)}) async-start(f32[16,32,128]{2,1,0:T(8,128)} %get-tuple-element.11), calls=%async_computation | async-start | bytes 524288 | tf_op jit(solution)/shard_map/all_to_all | solution.py:291

commit v4 on v3

--- a/solution.py
+++ b/solution.py
@@ -15,19 +15,32 @@
     return jnp.broadcast_to(ref[row : row + 1, :], (TILE, ref.shape[1]))
 
 
-def tables_kernel(modes, length, total, rate_ref, gain_ref, h_ref, e_ref):
-    tiles = length // TILE
-    step = rate_ref[...] * (1.0 / total)
-    lane = jax.lax.broadcasted_iota(jnp.int32, (TILE, step.shape[1]), 0).astype(jnp.float32)
+def rise(z):
+    value = jnp.full_like(z, 1.0 / 10.0)
+    for n in range(9, 1, -1):
+        value = (1.0 - z * value) * (1.0 / n)
+    return z * (1.0 - z * value)
+
+
+def prepare_kernel(modes, length, total, rate_ref, residue_ref, w_ref, h_ref, e_ref, gain_ref, held_ref, sem):
+    copy = pltpu.make_async_copy(w_ref, held_ref, sem)
+    copy.start()
+    tiles = length // TILE
+    rate = rate_ref[...]
+    step = rate * (1.0 / total)
+    gain = residue_ref[...] * jnp.sqrt(rise(2.0 * step) / (1.0 - jnp.exp(-2.0 * rate)))
+    gain_ref[...] = gain
+    lag = jax.lax.broadcasted_iota(jnp.int32, (TILE, step.shape[1]), 0).astype(jnp.float32)
     for q in range(tiles):
         e_ref[q * modes : (q + 1) * modes, :] = jnp.exp(-step * float(TILE * q))
-    scaled = [gain_ref[m : m + 1, :] * jnp.exp(-step[m : m + 1, :] * lane) for m in range(modes)]
+    scaled = [gain[m : m + 1, :] * jnp.exp(-step[m : m + 1, :] * lag) for m in range(modes)]
     h_ref[0:TILE, :] = jnp.zeros((TILE, step.shape[1]), jnp.float32)
     for q in range(tiles):
         total_tile = row_tile(e_ref, q * modes) * scaled[0]
         for m in range(1, modes):
             total_tile = total_tile + row_tile(e_ref, q * modes + m) * scaled[m]
         h_ref[(q + 1) * TILE : (q + 2) * TILE, :] = total_tile
+    copy.wait()
 
 
 def weight_rows(w_ref, owners, block):
@@ -38,7 +51,7 @@
     return jnp.concatenate(rows, axis=0)
 
 
-def early_kernel(place_ref, near_ref, near_up_ref, near_down_ref, far_ref, w_ref, acc_ref):
+def early_kernel(place_ref, near_ref, near_up_ref, near_down_ref, far_low_ref, far_high_ref, w_ref, acc_ref):
     line, parity = place_ref[0], place_ref[1]
     pairs, _, block = near_ref.shape
     split = near_up_ref.shape[0]
@@ -46,7 +59,8 @@
         lefts, owners = [], []
         for i in (k, k + 1):
             odd = near_up_ref[i] if i < split else near_down_ref[i - split]
-            lefts += [near_ref[i], odd, far_ref[i]]
+            far = far_low_ref[i] if i < split else far_high_ref[i - split]
+            lefts += [near_ref[i], odd, far]
             own, other = 2 * pairs * line + 2 * i, 2 * pairs * (1 - line) + 2 * i
             owners += [own + parity, own + 1 - parity, other + parity]
         part = jnp.dot(
@@ -221,12 +235,14 @@
     half = pairs // 2
 
     near = lax.all_gather(features, "shard", axis=0, axis_index_groups=groups)
-    far = lax.ppermute(near, "shard", across)
-    near_up = lax.ppermute(near[:half], "shard", up)
-    near_down = lax.ppermute(near[half:], "shard", down)
-    far_up = lax.ppermute(far[:half], "shard", up)
-    far_down = lax.ppermute(far[half:], "shard", down)
-    return near, near_up, near_down, far, far_up, far_down
+    low, high = near[:half], near[half:]
+    far_low = lax.ppermute(low, "shard", across)
+    far_high = lax.ppermute(high, "shard", across)
+    near_up = lax.ppermute(low, "shard", up)
+    near_down = lax.ppermute(high, "shard", down)
+    far_up = lax.ppermute(far_low, "shard", up)
+    far_down = lax.ppermute(far_high, "shard", down)
+    return near, near_up, near_down, far_low, far_high, far_up, far_down
 
 
 def shards(features, in_proj, short_filter, residue, decay_rate, skip_gain):
@@ -248,28 +264,32 @@
     w_branch = in_proj.transpose(1, 0, 2)
     at = lax.axis_index("shard")
     taps = lax.dynamic_slice_in_dim(short_filter, at * channels, channels, 2).reshape(-1, channels)
-    step_rate = decay_rate / total
-    gain = residue * jnp.sqrt(jnp.expm1(-2.0 * step_rate) / jnp.expm1(-2.0 * decay_rate))
-    h, e = pl.pallas_call(
-        functools.partial(tables_kernel, modes, length, total),
+    hbm = pl.BlockSpec(memory_space=pltpu.HBM)
+    h, e, gain, w_held = pl.pallas_call(
+        functools.partial(prepare_kernel, modes, length, total),
+        in_specs=[vmem, vmem, hbm],
+        out_specs=(vmem,) * 4,
         out_shape=(
             jax.ShapeDtypeStruct((length + TILE, channels), f32),
             jax.ShapeDtypeStruct((tiles * modes, channels), f32),
+            jax.ShapeDtypeStruct((modes, channels), f32),
+            jax.ShapeDtypeStruct(w_branch.shape, w_branch.dtype),
         ),
-        compiler_params=params(4),
-        name="tables",
-    )(decay_rate, gain)
+        scratch_shapes=[pltpu.SemaphoreType.DMA],
+        compiler_params=params(8),
+        name="prepare",
+    )(decay_rate, residue, w_branch)
 
     place = jnp.stack([at // line, at % 2]).astype(jnp.int32)
-    near, near_up, near_down, far, far_up, far_down = pieces
+    near, near_up, near_down, far_low, far_high, far_up, far_down = pieces
     early = pl.pallas_call(
         early_kernel,
-        in_specs=[smem] + [vmem] * 5,
+        in_specs=[smem] + [vmem] * 6,
         out_specs=vmem,
         out_shape=jax.ShapeDtypeStruct((length, 3 * channels), f32),
         compiler_params=params(12),
         name="early",
-    )(place, near, near_up, near_down, far, w_branch)
+    )(place, near, near_up, near_down, far_low, far_high, w_held)
     first, drive, message = pl.pallas_call(
         functools.partial(project_kernel, modes, length, total),
         in_specs=[smem] + [vmem] * 7,
@@ -286,7 +306,7 @@
         ],
         compiler_params=params(12),
         name="project",
-    )(place, early, far_up, far_down, w_branch, taps, decay_rate, e)
+    )(place, early, far_up, far_down, w_held, taps, decay_rate, e)
 
     everyone = lax.all_to_all(message, "seq", 0, 0).reshape(seq_count * ROWS, channels)
     skip = skip_gain.reshape(1, channels)

time: 83.6 us -> 84.8 us (1.014)
  starting transfers between devices: 26.8 us -> 30.2 us
  waiting for transfers between devices: 12.4 us -> 10.8 us
    ppermute x5 -> x6, starting transfers between devices: 13.7 us -> 17 us  [the longest x1 4.49 us: gather_features(): far_up = lax.ppermute(far_low, 'shard', up)]
    ppermute x5 -> x6, waiting for transfers between devices: 4.91 us -> 3.31 us  [the longest x1 3.29 us: gather_features(): far_down = lax.ppermute(far_high, 'shard', down)]
  transfers between devices with their start and end apart: 6 -> 7, of which waited for: 3 -> 2; matrix products, arithmetic and copies ran while one was open for 2% -> 0% of each run, Pallas kernels for 4% -> 4%
where the time goes in v4:
time: 84.8 us; the launch traced here: 84.3 us
  blocking collectives  33.4 us (39%)
  starting transfers between devices  30.2 us (36%)
  waiting for transfers between devices  10.8 us (13%)
  Pallas kernels  6.24 us (7%)
  local copies, waits for them, and re-layouts  3.35 us (4%)
    all_gather x1, blocking collectives, gather_features(): near = lax.all_gather(features, 'shard', axis=0, axis_index_groups=groups)  33.4 us
    all_to_all x1, starting transfers between devices, shards(): lax.all_to_all(message, 'seq', 0, 0).reshape(seq_count * ROWS, channels)  13.2 us
    all_to_all x1, waiting for transfers between devices, shards(): lax.all_to_all(message, 'seq', 0, 0).reshape(seq_count * ROWS, channels)  7.51 us
    ppermute x1, starting transfers between devices, gather_features(): far_up = lax.ppermute(far_low, 'shard', up)  4.49 us
    unnamed x12, local copies, waits for them, and re-layouts  3.29 us
    ppermute x1, waiting for transfers between devices, gather_features(): far_down = lax.ppermute(far_high, 'shard', down)  3.29 us
    ppermute x1, starting transfers between devices, gather_features(): near_up = lax.ppermute(low, 'shard', up)  3.28 us
    ppermute x1, starting transfers between devices, gather_features(): far_low = lax.ppermute(low, 'shard', across)  3.2 us
  transfers between devices with their start and end apart: 7, of which 2 were waited for; matrix products, arithmetic and copies ran while one was open for 0% of the time, Pallas kernels for 4%

profile of v4, /device:TPU:1, one launch (start us, length us, event | category | flops | bytes accessed | tf_op | source)
XLA Modules:
  0.0 84.3 jit_solution(17159112880202005016)
XLA Ops:
  0.0 0.0 copy-start
  0.0 33.4 %all-gather = bf16[2048,128]{1,0:T(8,128)(2,1)S(1)} all-gather(bf16[256,128]{1,0:T(8,128)(2,1)} %param.6), channel_id=2, replica_groups={{0,2,4,6,8,10,12,14},{1,3,5,7,9,11,13,15},{16,18,20,22,24,26,28,30},{17..., dimensions={0}, use_global_device_ids=true | all-gather | bytes 589824 | tf_op jit(solution)/shard_map/all_gather | solution.py:237
  33.5 3.2 %collective-permute-start.2 = (bf16[4,256,128]{2,1,0:T(8,128)(2,1)S(1)}, bf16[4,256,128]{2,1,0:T(8,128)(2,1)S(1)}, u32[]{:S(2)}, u32[]{:S(2)}) collective-permute-start(bf16[4,256,128]{2,1,0:T(8,128)(2,1)S(1)} %bitcast.16), channel_id=1, source_target_pairs={{0,16},{1,17},{2,18},{3,19},{4,20},{5,21},{6,22},{7,23},{8,24},{9,... | collective-permute-start | bytes 786440 | tf_op jit(solution)/shard_map/ppermute | solution.py:239
  36.7 2.1 %collective-permute-start.3 = (bf16[4,256,128]{2,1,0:T(8,128)(2,1)S(1)}, bf16[4,256,128]{2,1,0:T(8,128)(2,1)S(1)}, u32[]{:S(2)}, u32[]{:S(2)}) collective-permute-start(bf16[4,256,128]{2,1,0:T(8,128)(2,1)S(1)} %bitcast.14), channel_id=1, source_target_pairs={{0,16},{1,17},{2,18},{3,19},{4,20},{5,21},{6,22},{7,23},{8,24},{9,... | collective-permute-start | bytes 786440 | tf_op jit(solution)/shard_map/ppermute | solution.py:240
  38.8 3.3 %collective-permute-start = (bf16[4,256,128]{2,1,0:T(8,128)(2,1)S(1)}, bf16[4,256,128]{2,1,0:T(8,128)(2,1)S(1)}, u32[]{:S(2)}, u32[]{:S(2)}) collective-permute-start(bf16[4,256,128]{2,1,0:T(8,128)(2,1)S(1)} %bitcast.17), channel_id=1, source_target_pairs={{0,15},{1,0},{2,1},{3,2},{4,3},{5,4},{6,5},{7,6},{8,7},{9,8},{10,9... | collective-permute-start | bytes 786440 | tf_op jit(solution)/shard_map/ppermute | solution.py:241
  42.1 2.0 %collective-permute-start.1 = (bf16[4,256,128]{2,1,0:T(8,128)(2,1)S(1)}, bf16[4,256,128]{2,1,0:T(8,128)(2,1)S(1)}, u32[]{:S(2)}, u32[]{:S(2)}) collective-permute-start(bf16[4,256,128]{2,1,0:T(8,128)(2,1)S(1)} %bitcast.15), channel_id=1, source_target_pairs={{0,1},{1,2},{2,3},{3,4},{4,5},{5,6},{6,7},{7,8},{8,9},{9,10},{10,1... | collective-permute-start | bytes 786440 | tf_op jit(solution)/shard_map/ppermute | solution.py:242
  44.1 0.0 collective-permute-done.2.far_low_ref
  44.1 4.5 %collective-permute-start.4 = (bf16[4,256,128]{2,1,0:T(8,128)(2,1)S(1)}, bf16[4,256,128]{2,1,0:T(8,128)(2,1)S(1)}, u32[]{:S(2)}, u32[]{:S(2)}) collective-permute-start(bf16[4,256,128]{2,1,0:T(8,128)(2,1)S(1)} %collective-permute-done.2.far_low_ref), channel_id=1, source_target_pairs={{0,15},{1,0},{2,1},{3,2},{4,3},{5,4},{6,5},{7,6},{8,7},{9,8},{10,9... | collective-permute-start | bytes 786440 | tf_op jit(solution)/shard_map/ppermute | solution.py:243
  48.6 0.0 collective-permute-done.3.far_high_ref
  48.6 1.9 %collective-permute-start.5 = (bf16[4,256,128]{2,1,0:T(8,128)(2,1)S(1)}, bf16[4,256,128]{2,1,0:T(8,128)(2,1)S(1)}, u32[]{:S(2)}, u32[]{:S(2)}) collective-permute-start(bf16[4,256,128]{2,1,0:T(8,128)(2,1)S(1)} %collective-permute-done.3.far_high_ref), channel_id=1, source_target_pairs={{0,1},{1,2},{2,3},{3,4},{4,5},{5,6},{6,7},{7,8},{8,9},{9,10},{10,1... | collective-permute-start | bytes 786440 | tf_op jit(solution)/shard_map/ppermute | solution.py:244
  50.6 0.0 copy-done
  50.6 0.0 copy-start.1
  50.6 1.9 %copy-done.1 = bf16[4096,3,128]{2,0,1:T(8,128)(2,1)S(1)} copy-done((bf16[4096,3,128]{2,0,1:T(8,128)(2,1)S(1)}, bf16[4096,3,128]{2,0,1:T(8,128)(2,1)}, u32[]{:S(2)}) %copy-start.1) | copy-done | bytes 3145752
  52.5 0.0 copy-start.2
  52.5 0.7 copy-done.2
  53.2 0.7 copy-done.4
  53.9 0.4 prepare.1
  54.3 0.0 copy-start.3
  54.3 0.1 pad_add_fusion.place_ref
  54.4 0.0 collective-permute-done.near_up_ref
  54.4 0.0 collective-permute-done.1.near_down_ref
  54.4 1.5 %early.1.early_ref = f32[256,384]{1,0:T(8,128)S(1)} custom-call(s32[2]{0:T(128)S(1)} %pad_add_fusion.place_ref, bf16[8,256,128]{2,1,0:T(8,128)(2,1)S(1)} %bitcast.9, bf16[4,256,128]{2,1,0:T(8,128)(2,1)S(1)} %collective-permute-done.near_up_ref, bf16[4,256,128]{2,1,0:T(8,128)(2,1)S(1)} %collective-permute-done.1.near_down_ref, ...), custom_call_target="tpu_custom_call" | custom-call | tf_op jit(solution)/shard_map/early/pallas_call | solution.py:285
  56.0 0.0 copy-start.5
  56.0 0.0 collective-permute-done.4.far_up_ref
  56.0 3.3 %collective-permute-done.5.far_down_ref = bf16[4,256,128]{2,1,0:T(8,128)(2,1)S(1)} collective-permute-done((bf16[4,256,128]{2,1,0:T(8,128)(2,1)S(1)}, bf16[4,256,128]{2,1,0:T(8,128)(2,1)S(1)}, u32[]{:S(2)}, u32[]{:S(2)}) %collective-permute-start.5) | collective-permute-done | bytes 262176 | tf_op jit(solution)/shard_map/ppermute | solution.py:244
  59.3 0.0 copy-done.3
  59.3 2.0 %project.1 = (f32[256,128]{1,0:T(8,128)S(1)}, f32[256,128]{1,0:T(8,128)S(1)}, f32[16,32,128]{2,1,0:T(8,128)}) custom-call(s32[2]{0:T(128)S(1)} %pad_add_fusion.place_ref, f32[256,384]{1,0:T(8,128)S(1)} %early.1.early_ref, bf16[4,256,128]{2,1,0:T(8,128)(2,1)S(1)} %collective-permute-done.4.far_up_ref, ...), custom_call_target="tpu_custom_call" | custom-call | tf_op jit(solution)/shard_map/project/pallas_call | solution.py:293
  61.3 13.2 %all-to-all-start = ((f32[16,32,128]{2,1,0:T(8,128)}), f32[16,32,128]{2,1,0:T(8,128)S(1)}, u32[]{:S(2)}, u32[]{:S(2)}) async-start(f32[16,32,128]{2,1,0:T(8,128)} %get-tuple-element.14), calls=%async_computation | async-start | bytes 524288 | tf_op jit(solution)/shard_map/all_to_all | solution.py:311
  74.5 0.0 copy-done.5
  74.5 1.4 %conv.1.conv_ref = f32[256,128]{1,0:T(8,128)S(1)} custom-call(f32[256,128]{1,0:T(8,128)S(1)} %get-tuple-element.16.drive_ref, f32[264,128]{1,0:T(8,128)S(1)} %get-tuple-element.17.h_ref, f32[1,128]{1,0:T(1,128)S(1)} %bitcast.12), custom_call_target="tpu_custom_call" | custom-call | tf_op jit(solution)/shard_map/conv/pallas_call | solution.py:313
  75.8 7.5 %all-to-all-done = f32[16,32,128]{2,1,0:T(8,128)S(1)} async-done(((f32[16,32,128]{2,1,0:T(8,128)}), f32[16,32,128]{2,1,0:T(8,128)S(1)}, u32[]{:S(2)}, u32[]{:S(2)}) %all-to-all-start) | async-done | bytes 262176 | tf_op jit(solution)/shard_map/all_to_all | solution.py:311
  83.4 0.9 %finish.1 = bf16[256,128]{1,0:T(8,128)(2,1)} custom-call(s32[1]{0:T(128)} %bitcast.me_ref, f32[512,128]{1,0:T(8,128)S(1)} %bitcast.11, f32[256,128]{1,0:T(8,128)S(1)} %get-tuple-element.15.first_ref, f32[256,128]{1,0:T(8,128)S(1)} %conv.1.conv_ref, f32[9,128]{1,0:T(8,128)S(1)} %reshape.13.taps_ref, f32[16,128]{1,0:T(8,128)S(1)} %copy-done.3, ...), custom_call_target="tpu_custom_call" | custom-call | tf_op jit(solution)/shard_map/finish/pallas_call | solution.py:327
  (4 shorter events, 0.1 us)
Async XLA Ops:
  0.0 50.6 %copy-start = (f32[3,3,4096]{2,1,0:T(4,128)S(1)}, f32[3,3,4096]{2,1,0:T(4,128)}, u32[]{:S(2)}) copy-start(f32[3,3,4096]{2,1,0:T(4,128)} %param.8) | copy-start | bytes 442372
  33.5 10.6 %collective-permute-start.2 = (bf16[4,256,128]{2,1,0:T(8,128)(2,1)S(1)}, bf16[4,256,128]{2,1,0:T(8,128)(2,1)S(1)}, u32[]{:S(2)}, u32[]{:S(2)}) collective-permute-start(bf16[4,256,128]{2,1,0:T(8,128)(2,1)S(1)} %bitcast.16), channel_id=1, source_target_pairs={{0,16},{1,17},{2,18},{3,19},{4,20},{5,21},{6,22},{7,23},{8,24},{9,... | collective-permute-start | bytes 786440 | tf_op jit(solution)/shard_map/ppermute | solution.py:239
  36.7 11.9 %collective-permute-start.3 = (bf16[4,256,128]{2,1,0:T(8,128)(2,1)S(1)}, bf16[4,256,128]{2,1,0:T(8,128)(2,1)S(1)}, u32[]{:S(2)}, u32[]{:S(2)}) collective-permute-start(bf16[4,256,128]{2,1,0:T(8,128)(2,1)S(1)} %bitcast.14), channel_id=1, source_target_pairs={{0,16},{1,17},{2,18},{3,19},{4,20},{5,21},{6,22},{7,23},{8,24},{9,... | collective-permute-start | bytes 786440 | tf_op jit(solution)/shard_map/ppermute | solution.py:240
  38.8 15.6 %collective-permute-start = (bf16[4,256,128]{2,1,0:T(8,128)(2,1)S(1)}, bf16[4,256,128]{2,1,0:T(8,128)(2,1)S(1)}, u32[]{:S(2)}, u32[]{:S(2)}) collective-permute-start(bf16[4,256,128]{2,1,0:T(8,128)(2,1)S(1)} %bitcast.17), channel_id=1, source_target_pairs={{0,15},{1,0},{2,1},{3,2},{4,3},{5,4},{6,5},{7,6},{8,7},{9,8},{10,9... | collective-permute-start | bytes 786440 | tf_op jit(solution)/shard_map/ppermute | solution.py:241
  42.1 12.3 %collective-permute-start.1 = (bf16[4,256,128]{2,1,0:T(8,128)(2,1)S(1)}, bf16[4,256,128]{2,1,0:T(8,128)(2,1)S(1)}, u32[]{:S(2)}, u32[]{:S(2)}) collective-permute-start(bf16[4,256,128]{2,1,0:T(8,128)(2,1)S(1)} %bitcast.15), channel_id=1, source_target_pairs={{0,1},{1,2},{2,3},{3,4},{4,5},{5,6},{6,7},{7,8},{8,9},{9,10},{10,1... | collective-permute-start | bytes 786440 | tf_op jit(solution)/shard_map/ppermute | solution.py:242
  44.1 11.9 %collective-permute-start.4 = (bf16[4,256,128]{2,1,0:T(8,128)(2,1)S(1)}, bf16[4,256,128]{2,1,0:T(8,128)(2,1)S(1)}, u32[]{:S(2)}, u32[]{:S(2)}) collective-permute-start(bf16[4,256,128]{2,1,0:T(8,128)(2,1)S(1)} %collective-permute-done.2.far_low_ref), channel_id=1, source_target_pairs={{0,15},{1,0},{2,1},{3,2},{4,3},{5,4},{6,5},{7,6},{8,7},{9,8},{10,9... | collective-permute-start | bytes 786440 | tf_op jit(solution)/shard_map/ppermute | solution.py:243
  48.6 10.7 %collective-permute-start.5 = (bf16[4,256,128]{2,1,0:T(8,128)(2,1)S(1)}, bf16[4,256,128]{2,1,0:T(8,128)(2,1)S(1)}, u32[]{:S(2)}, u32[]{:S(2)}) collective-permute-start(bf16[4,256,128]{2,1,0:T(8,128)(2,1)S(1)} %collective-permute-done.3.far_high_ref), channel_id=1, source_target_pairs={{0,1},{1,2},{2,3},{3,4},{4,5},{5,6},{6,7},{7,8},{8,9},{9,10},{10,1... | collective-permute-start | bytes 786440 | tf_op jit(solution)/shard_map/ppermute | solution.py:244
  50.6 1.9 %copy-start.1 = (bf16[4096,3,128]{2,0,1:T(8,128)(2,1)S(1)}, bf16[4096,3,128]{2,0,1:T(8,128)(2,1)}, u32[]{:S(2)}) copy-start(bf16[4096,3,128]{2,0,1:T(8,128)(2,1)} %param.7) | copy-start | bytes 9437188
  52.5 0.7 copy-start.2
  53.2 0.7 copy-start.4
  54.3 4.9 %copy-start.3 = (f32[16,128]{1,0:T(8,128)S(1)}, f32[16,128]{1,0:T(8,128)}, u32[]{:S(2)}) copy-start(f32[16,128]{1,0:T(8,128)} %rate_ref.5) | copy-start | bytes 24580
  56.0 18.5 %copy-start.5 = (f32[128]{0:T(128)S(1)}, f32[128]{0:T(128)}, u32[]{:S(2)}) copy-start(f32[128]{0:T(128)} %param.11) | copy-start | bytes 1540
  61.3 22.1 %all-to-all-start = ((f32[16,32,128]{2,1,0:T(8,128)}), f32[16,32,128]{2,1,0:T(8,128)S(1)}, u32[]{:S(2)}, u32[]{:S(2)}) async-start(f32[16,32,128]{2,1,0:T(8,128)} %get-tuple-element.14), calls=%async_computation | async-start | bytes 524288 | tf_op jit(solution)/shard_map/all_to_all | solution.py:311

commit v5 on v3

--- a/solution.py
+++ b/solution.py
@@ -15,9 +15,18 @@
     return jnp.broadcast_to(ref[row : row + 1, :], (TILE, ref.shape[1]))
 
 
-def tables_kernel(modes, length, total, rate_ref, gain_ref, h_ref, e_ref):
-    tiles = length // TILE
-    step = rate_ref[...] * (1.0 / total)
+def rise(z):
+    value = jnp.full_like(z, 1.0 / 10.0)
+    for n in range(9, 1, -1):
+        value = (1.0 - z * value) * (1.0 / n)
+    return z * (1.0 - z * value)
+
+
+def tables_kernel(modes, length, total, rate_ref, residue_ref, h_ref, e_ref, gain_ref):
+    tiles = length // TILE
+    rate = rate_ref[...]
+    step = rate * (1.0 / total)
+    gain_ref[...] = residue_ref[...] * jnp.sqrt(rise(2.0 * step) / (1.0 - jnp.exp(-2.0 * rate)))
     lane = jax.lax.broadcasted_iota(jnp.int32, (TILE, step.shape[1]), 0).astype(jnp.float32)
     for q in range(tiles):
         e_ref[q * modes : (q + 1) * modes, :] = jnp.exp(-step * float(TILE * q))
@@ -59,67 +68,77 @@
 
 def project_kernel(
     modes, length, total, place_ref, early_ref, far_up_ref, far_down_ref, w_ref, taps_ref, rate_ref,
-    e_ref, first_ref, drive_ref, message_ref, proj_ref, filt_ref, state_ref,
+    e_ref, lead_ref, drive_ref, message_ref, pair_ref, state_ref,
 ):
     line, parity = place_ref[0], place_ref[1]
     split, _, block = far_up_ref.shape
-    pairs = 2 * split
+    pairs = split + far_down_ref.shape[0]
     channels = drive_ref.shape[1]
-    acc = early_ref[...]
-    for ref, start in ((far_up_ref, 0), (far_down_ref, split)):
-        owners = [2 * pairs * (1 - line) + 2 * (start + k) + 1 - parity for k in range(split)]
-        left = jnp.concatenate([ref[k] for k in range(split)], axis=1)
-        acc = acc + jnp.dot(
-            left, weight_rows(w_ref, owners, block), preferred_element_type=jnp.float32
-        )
-
+    owners = [2 * pairs * (1 - line) + 2 * k + 1 - parity for k in range(pairs)]
+    left = [far_up_ref[k] if k < split else far_down_ref[k - split] for k in range(pairs)]
+    acc = early_ref[...] + jnp.dot(
+        jnp.concatenate(left, axis=1),
+        weight_rows(w_ref, owners, block),
+        preferred_element_type=jnp.float32,
+    )
+    proj = acc.astype(jnp.bfloat16).astype(jnp.float32)
     pad = TILE
-    proj_ref[0:pad, :] = jnp.zeros((pad, 3 * channels), jnp.float32)
-    proj_ref[pad:, :] = acc.astype(jnp.bfloat16).astype(jnp.float32)
-    for b in range(3):
-        cols = slice(b * channels, (b + 1) * channels)
-        value = taps_ref[b : b + 1, :] * proj_ref[pad : pad + length, cols]
-        value = value + taps_ref[3 + b : 4 + b, :] * proj_ref[pad - 1 : pad - 1 + length, cols]
-        value = value + taps_ref[6 + b : 7 + b, :] * proj_ref[pad - 2 : pad - 2 + length, cols]
-        if b == 0:
-            first_ref[...] = value
-        else:
-            filt_ref[b - 1] = value
-    drive_ref[...] = filt_ref[0] * filt_ref[1]
+    one, two, three = channels, 2 * channels, 3 * channels
+    lead_ref[0:pad, :] = jnp.zeros((pad, channels), jnp.float32)
+    lead_ref[pad:, :] = proj[:, 0:one]
+    pair_ref[0:pad, :] = jnp.zeros((pad, two), jnp.float32)
+    pair_ref[pad:, :] = proj[:, one:three]
+
     row = jax.lax.broadcasted_iota(jnp.int32, (TILE, channels), 0)
-    drive_ref[0:TILE, :] = jnp.where(row < 2, 0.0, drive_ref[0:TILE, :])
+    taps = [[row_tile(taps_ref, 3 * j + b) for j in range(3)] for b in (1, 2)]
+    tiles = length // TILE
+    states = [None] * modes
+    for q in range(tiles):
+        drive = None
+        for b in range(2):
+            cols = slice(b * channels, (b + 1) * channels)
+            at = pad + q * TILE
+            value = taps[b][0] * pair_ref[at : at + TILE, cols]
+            value = value + taps[b][1] * pair_ref[at - 1 : at - 1 + TILE, cols]
+            value = value + taps[b][2] * pair_ref[at - 2 : at - 2 + TILE, cols]
+            drive = value if b == 0 else drive * value
+        if q == 0:
+            drive = jnp.where(row < 2, 0.0, drive)
+        drive_ref[q * TILE : (q + 1) * TILE, :] = drive
+        for m in range(modes):
+            term = row_tile(e_ref, (tiles - 1 - q) * modes + m) * drive
+            states[m] = term if q == 0 else states[m] + term
+    step = rate_ref[...] * (1.0 / total)
     lag = (TILE - 1 - row).astype(jnp.float32)
-    tiles = length // TILE
-    pieces = [drive_ref[q * TILE : (q + 1) * TILE, :] for q in range(tiles)]
-    step = rate_ref[...] * (1.0 / total)
     for m in range(modes):
-        state = row_tile(e_ref, (tiles - 1) * modes + m) * pieces[0]
-        for q in range(1, tiles):
-            state = state + row_tile(e_ref, (tiles - 1 - q) * modes + m) * pieces[q]
-        state = state * jnp.exp(-step[m : m + 1, :] * lag)
+        state = states[m] * jnp.exp(-step[m : m + 1, :] * lag)
         state_ref[m : m + 1, :] = jnp.sum(state, axis=0, keepdims=True)
-    one, two, three = channels, 2 * channels, 3 * channels
     head, tail = pad, pad + length - 2
-    spots = [
-        (head, one, two), (head, two, three), (head + 1, one, two), (head + 1, two, three),
-        (tail, one, two), (tail, two, three), (tail + 1, one, two), (tail + 1, two, three),
-        (tail, 0, one), (tail + 1, 0, one),
-    ]
-    for k, (r, lo, hi) in enumerate(spots):
-        state_ref[modes + k : modes + k + 1, :] = proj_ref[r : r + 1, lo:hi]
+    spots = [(r, b) for r in (head, head + 1, tail, tail + 1) for b in (0, 1)]
+    for k, (r, b) in enumerate(spots):
+        state_ref[modes + k : modes + k + 1, :] = pair_ref[r : r + 1, b * channels : (b + 1) * channels]
     used = modes + len(spots)
-    state_ref[used:ROWS, :] = jnp.zeros((ROWS - used, channels), jnp.float32)
+    state_ref[used : used + 2, :] = lead_ref[tail : tail + 2, :]
+    state_ref[used + 2 : ROWS, :] = jnp.zeros((ROWS - used - 2, channels), jnp.float32)
+    message = state_ref[...]
     for s in range(message_ref.shape[0]):
-        message_ref[s] = state_ref[...]
-
-
-def conv_kernel(length, drive_ref, h_ref, skip_ref, conv_ref, pad_ref, lag_ref):
+        message_ref[s] = message
+
+
+def conv_kernel(length, drive_ref, h_ref, skip_ref, lead_ref, taps_ref, conv_ref, first_ref, pad_ref, lag_ref):
     channels = drive_ref.shape[1]
     tiles = length // TILE
     pad_ref[0:TILE, :] = jnp.zeros((TILE, channels), jnp.float32)
     pad_ref[TILE:, :] = drive_ref[...]
     for j in range(TILE):
         lag_ref[j] = pad_ref[TILE - j : TILE - j + length, :]
+
+    for q in range(tiles):
+        at = (q + 1) * TILE
+        value = row_tile(taps_ref, 0) * lead_ref[at : at + TILE, :]
+        value = value + row_tile(taps_ref, 3) * lead_ref[at - 1 : at - 1 + TILE, :]
+        value = value + row_tile(taps_ref, 6) * lead_ref[at - 2 : at - 2 + TILE, :]
+        first_ref[q * TILE : (q + 1) * TILE, :] = value
 
     group = 8
     for g in range(tiles // group):
@@ -224,8 +243,9 @@
     far = lax.ppermute(near, "shard", across)
     near_up = lax.ppermute(near[:half], "shard", up)
     near_down = lax.ppermute(near[half:], "shard", down)
-    far_up = lax.ppermute(far[:half], "shard", up)
-    far_down = lax.ppermute(far[half:], "shard", down)
+    most = half + 1
+    far_up = lax.ppermute(far[:most], "shard", up)
+    far_down = lax.ppermute(far[most:], "shard", down)
     return near, near_up, near_down, far, far_up, far_down
 
 
@@ -248,17 +268,16 @@
     w_branch = in_proj.transpose(1, 0, 2)
     at = lax.axis_index("shard")
     taps = lax.dynamic_slice_in_dim(short_filter, at * channels, channels, 2).reshape(-1, channels)
-    step_rate = decay_rate / total
-    gain = residue * jnp.sqrt(jnp.expm1(-2.0 * step_rate) / jnp.expm1(-2.0 * decay_rate))
-    h, e = pl.pallas_call(
+    h, e, gain = pl.pallas_call(
         functools.partial(tables_kernel, modes, length, total),
         out_shape=(
             jax.ShapeDtypeStruct((length + TILE, channels), f32),
             jax.ShapeDtypeStruct((tiles * modes, channels), f32),
+            jax.ShapeDtypeStruct((modes, channels), f32),
         ),
         compiler_params=params(4),
         name="tables",
-    )(decay_rate, gain)
+    )(decay_rate, residue)
 
     place = jnp.stack([at // line, at % 2]).astype(jnp.int32)
     near, near_up, near_down, far, far_up, far_down = pieces
@@ -270,18 +289,17 @@
         compiler_params=params(12),
         name="early",
     )(place, near, near_up, near_down, far, w_branch)
-    first, drive, message = pl.pallas_call(
+    lead, drive, message = pl.pallas_call(
         functools.partial(project_kernel, modes, length, total),
         in_specs=[smem] + [vmem] * 7,
         out_specs=(vmem,) * 3,
         out_shape=(
-            jax.ShapeDtypeStruct((length, channels), f32),
+            jax.ShapeDtypeStruct((length + TILE, channels), f32),
             jax.ShapeDtypeStruct((length, channels), f32),
             jax.ShapeDtypeStruct((seq_count, ROWS, channels), f32),
         ),
         scratch_shapes=[
-            pltpu.VMEM((length + TILE, 3 * channels), f32),
-            pltpu.VMEM((2, length, channels), f32),
+            pltpu.VMEM((length + TILE, 2 * channels), f32),
             pltpu.VMEM((ROWS, channels), f32),
         ],
         compiler_params=params(12),
@@ -290,18 +308,18 @@
 
     everyone = lax.all_to_all(message, "seq", 0, 0).reshape(seq_count * ROWS, channels)
     skip = skip_gain.reshape(1, channels)
-    conv = pl.pallas_call(
+    conv, first = pl.pallas_call(
         functools.partial(conv_kernel, length),
-        in_specs=[vmem] * 3,
-        out_specs=vmem,
-        out_shape=jax.ShapeDtypeStruct((length, channels), f32),
+        in_specs=[vmem] * 5,
+        out_specs=(vmem,) * 2,
+        out_shape=(jax.ShapeDtypeStruct((length, channels), f32),) * 2,
         scratch_shapes=[
             pltpu.VMEM((length + TILE, channels), f32),
             pltpu.VMEM((TILE, length, channels), f32),
         ],
         compiler_params=params(6),
         name="conv",
-    )(drive, h, skip)
+    )(drive, h, skip, lead, taps)
 
     me = lax.axis_index("seq").astype(jnp.int32).reshape(1)
     return pl.pallas_call(

time: 83.6 us -> 90.4 us (1.081)
  starting transfers between devices: 26.8 us -> 30.1 us
  waiting for transfers between devices: 12.4 us -> 15.7 us
  local copies, waits for them, and re-layouts: 3.39 us -> 4.39 us
    ppermute x1, waiting for transfers between devices: 1.3 us -> 6.71 us  [gather_features(): far = lax.ppermute(near, 'shard', across)]
    ppermute x2, waiting for transfers between devices: 3.61 us -> 0.01 us  [the longest x1 0.01 us: gather_features(): far_down = lax.ppermute(far[most:], 'shard', down)]
    all_to_all x1, starting transfers between devices: 13.1 us -> 16.3 us  [shards(): lax.all_to_all(message, 'seq', 0, 0).reshape(seq_count * ROWS, channels)]
    ppermute x1, waiting for transfers between devices: 0.01 us -> 1.51 us  [gather_features(): near_down = lax.ppermute(near[half:], 'shard', down)]
    ppermute x1, starting transfers between devices: 3.28 us -> 2.25 us  [gather_features(): near_up = lax.ppermute(near[:half], 'shard', up)]
    ppermute x1, starting transfers between devices: 2 us -> 3.02 us  [gather_features(): near_down = lax.ppermute(near[half:], 'shard', down)]
    unnamed x12 -> x14, local copies, waits for them, and re-layouts: 2.6 us -> 3.61 us
  transfers between devices with their start and end apart: 6 -> 6, of which waited for: 3 -> 3; matrix products, arithmetic and copies ran while one was open for 2% -> 1% of each run, Pallas kernels for 4% -> 3%
where the time goes in v5:
time: 90.4 us; the launch traced here: 89.9 us
  blocking collectives  33.4 us (37%)
  starting transfers between devices  30.1 us (33%)
  waiting for transfers between devices  15.7 us (17%)
  Pallas kernels  6.05 us (7%)
  local copies, waits for them, and re-layouts  4.39 us (5%)
    all_gather x1, blocking collectives, gather_features(): near = lax.all_gather(features, 'shard', axis=0, axis_index_groups=groups)  33.4 us
    all_to_all x1, starting transfers between devices, shards(): lax.all_to_all(message, 'seq', 0, 0).reshape(seq_count * ROWS, channels)  16.3 us
    all_to_all x1, waiting for transfers between devices, shards(): lax.all_to_all(message, 'seq', 0, 0).reshape(seq_count * ROWS, channels)  7.5 us
    ppermute x1, waiting for transfers between devices, gather_features(): far = lax.ppermute(near, 'shard', across)  6.71 us
    unnamed x14, local copies, waits for them, and re-layouts  3.61 us
    ppermute x1, starting transfers between devices, gather_features(): far_up = lax.ppermute(far[:most], 'shard', up)  3.28 us
    ppermute x1, starting transfers between devices, gather_features(): far = lax.ppermute(near, 'shard', across)  3.19 us
    ppermute x1, starting transfers between devices, gather_features(): near_down = lax.ppermute(near[half:], 'shard', down)  3.02 us
  transfers between devices with their start and end apart: 6, of which 3 were waited for; matrix products, arithmetic and copies ran while one was open for 1% of the time, Pallas kernels for 3%

profile of v5, /device:TPU:1, one launch (start us, length us, event | category | flops | bytes accessed | tf_op | source)
XLA Modules:
  0.0 89.9 jit_solution(15437957597615258336)
XLA Ops:
  0.0 0.0 copy-start
  0.0 33.4 %all-gather = bf16[2048,128]{1,0:T(8,128)(2,1)S(1)} all-gather(bf16[256,128]{1,0:T(8,128)(2,1)} %param.6), channel_id=2, replica_groups={{0,2,4,6,8,10,12,14},{1,3,5,7,9,11,13,15},{16,18,20,22,24,26,28,30},{17..., dimensions={0}, use_global_device_ids=true | all-gather | bytes 589824 | tf_op jit(solution)/shard_map/all_gather | solution.py:242
  33.5 3.2 %collective-permute-start.2 = (bf16[8,256,128]{2,1,0:T(8,128)(2,1)S(1)}, bf16[8,256,128]{2,1,0:T(8,128)(2,1)S(1)}, u32[]{:S(2)}, u32[]{:S(2)}) collective-permute-start(bf16[8,256,128]{2,1,0:T(8,128)(2,1)S(1)} %bitcast.11), channel_id=1, source_target_pairs={{0,16},{1,17},{2,18},{3,19},{4,20},{5,21},{6,22},{7,23},{8,24},{9,... | collective-permute-start | bytes 1572872 | tf_op jit(solution)/shard_map/ppermute | solution.py:243
  36.7 6.7 %collective-permute-done.2.far_ref = bf16[8,256,128]{2,1,0:T(8,128)(2,1)S(1)} collective-permute-done((bf16[8,256,128]{2,1,0:T(8,128)(2,1)S(1)}, bf16[8,256,128]{2,1,0:T(8,128)(2,1)S(1)}, u32[]{:S(2)}, u32[]{:S(2)}) %collective-permute-start.2) | collective-permute-done | bytes 524320 | tf_op jit(solution)/shard_map/ppermute | solution.py:243
  43.4 0.0 copy-start.4
  43.4 3.3 %collective-permute-start.3 = (bf16[5,256,128]{2,1,0:T(8,128)(2,1)S(1)}, bf16[5,256,128]{2,1,0:T(8,128)(2,1)S(1)}, u32[]{:S(2)}, u32[]{:S(2)}) collective-permute-start(bf16[5,256,128]{2,1,0:T(8,128)(2,1)S(1)} %slice.20), channel_id=1, source_target_pairs={{0,15},{1,0},{2,1},{3,2},{4,3},{5,4},{6,5},{7,6},{8,7},{9,8},{10,9... | collective-permute-start | bytes 983048 | tf_op jit(solution)/shard_map/ppermute | solution.py:247
  46.7 0.7 fusion
  47.4 2.3 %collective-permute-start = (bf16[4,256,128]{2,1,0:T(8,128)(2,1)}, bf16[4,256,128]{2,1,0:T(8,128)(2,1)S(1)}, u32[]{:S(2)}, u32[]{:S(2)}) collective-permute-start(bf16[4,256,128]{2,1,0:T(8,128)(2,1)} %bitcast.4), channel_id=1, source_target_pairs={{0,15},{1,0},{2,1},{3,2},{4,3},{5,4},{6,5},{7,6},{8,7},{9,8},{10,9... | collective-permute-start | bytes 786440 | tf_op jit(solution)/shard_map/ppermute | solution.py:244
  49.7 3.0 %collective-permute-start.1 = (bf16[4,256,128]{2,1,0:T(8,128)(2,1)S(1)}, bf16[4,256,128]{2,1,0:T(8,128)(2,1)S(1)}, u32[]{:S(2)}, u32[]{:S(2)}) collective-permute-start(bf16[4,256,128]{2,1,0:T(8,128)(2,1)S(1)} %bitcast.16), channel_id=1, source_target_pairs={{0,1},{1,2},{2,3},{3,4},{4,5},{5,6},{6,7},{7,8},{8,9},{9,10},{10,1... | collective-permute-start | bytes 786440 | tf_op jit(solution)/shard_map/ppermute | solution.py:245
  52.7 2.0 %collective-permute-start.4 = (bf16[3,256,128]{2,1,0:T(8,128)(2,1)S(1)}, bf16[3,256,128]{2,1,0:T(8,128)(2,1)S(1)}, u32[]{:S(2)}, u32[]{:S(2)}) collective-permute-start(bf16[3,256,128]{2,1,0:T(8,128)(2,1)S(1)} %slice.21), channel_id=1, source_target_pairs={{0,1},{1,2},{2,3},{3,4},{4,5},{5,6},{6,7},{7,8},{8,9},{9,10},{10,1... | collective-permute-start | bytes 589832 | tf_op jit(solution)/shard_map/ppermute | solution.py:248
  54.8 0.0 copy-done
  54.8 0.0 copy-start.3
  54.8 0.7 copy-done.3
  55.5 0.0 copy-start.5
  55.5 0.7 copy-done.5
  56.2 0.2 tables.1
  56.4 0.1 pad_add_fusion.place_ref
  56.5 0.0 collective-permute-done.near_up_ref
  56.5 1.5 %collective-permute-done.1.near_down_ref = bf16[4,256,128]{2,1,0:T(8,128)(2,1)S(1)} collective-permute-done((bf16[4,256,128]{2,1,0:T(8,128)(2,1)S(1)}, bf16[4,256,128]{2,1,0:T(8,128)(2,1)S(1)}, u32[]{:S(2)}, u32[]{:S(2)}) %collective-permute-start.1) | collective-permute-done | bytes 262176 | tf_op jit(solution)/shard_map/ppermute | solution.py:245
  58.0 1.9 %copy-done.1 = bf16[4096,3,128]{2,0,1:T(8,128)(2,1)S(1)} copy-done((bf16[4096,3,128]{2,0,1:T(8,128)(2,1)S(1)}, bf16[4096,3,128]{2,0,1:T(8,128)(2,1)}, u32[]{:S(2)}) %copy-start.1) | copy-done | bytes 3145752
  59.9 1.5 %early.1.early_ref = f32[256,384]{1,0:T(8,128)S(1)} custom-call(s32[2]{0:T(128)S(1)} %pad_add_fusion.place_ref, bf16[8,256,128]{2,1,0:T(8,128)(2,1)S(1)} %bitcast.12, bf16[4,256,128]{2,1,0:T(8,128)(2,1)S(1)} %collective-permute-done.near_up_ref, bf16[4,256,128]{2,1,0:T(8,128)(2,1)S(1)} %collective-permute-done.1.near_down_ref, ...), custom_call_target="tpu_custom_call" | custom-call | tf_op jit(solution)/shard_map/early/pallas_call | solution.py:284
  61.4 0.0 copy-start.6
  61.4 0.0 collective-permute-done.4.far_down_ref
  61.5 0.0 collective-permute-done.3.far_up_ref
  61.5 0.0 copy-done.4
  61.5 0.3 copy-done.2
  61.8 2.0 %project.1 = (f32[264,128]{1,0:T(8,128)S(1)}, f32[256,128]{1,0:T(8,128)S(1)}, f32[16,32,128]{2,1,0:T(8,128)}) custom-call(s32[2]{0:T(128)S(1)} %pad_add_fusion.place_ref, f32[256,384]{1,0:T(8,128)S(1)} %early.1.early_ref, bf16[5,256,128]{2,1,0:T(8,128)(2,1)S(1)} %collective-permute-done.3.far_up_ref, ...), custom_call_target="tpu_custom_call" | custom-call | tf_op jit(solution)/shard_map/project/pallas_call | solution.py:292
  63.8 16.3 %all-to-all-start = ((f32[16,32,128]{2,1,0:T(8,128)}), f32[16,32,128]{2,1,0:T(8,128)S(1)}, u32[]{:S(2)}, u32[]{:S(2)}) async-start(f32[16,32,128]{2,1,0:T(8,128)} %get-tuple-element.14), calls=%async_computation | async-start | bytes 524288 | tf_op jit(solution)/shard_map/all_to_all | solution.py:309
  80.1 0.0 copy-done.6
  80.1 1.4 %conv.1 = (f32[256,128]{1,0:T(8,128)S(1)}, f32[256,128]{1,0:T(8,128)S(1)}) custom-call(f32[256,128]{1,0:T(8,128)S(1)} %get-tuple-element.15.drive_ref, f32[264,128]{1,0:T(8,128)S(1)} %get-tuple-element.16.h_ref, f32[1,128]{1,0:T(1,128)S(1)} %bitcast.14, f32[264,128]{1,0:T(8,128)S(1)} %get-tuple-element.17.lead_ref, f32[9,128]{1,0:T(8,128)S(1)} %reshape.13.taps_ref), custom_call_target="tpu_custom_call" | custom-call | tf_op jit(solution)/shard_map/conv/pallas_call | solution.py:311
  81.5 7.5 %all-to-all-done = f32[16,32,128]{2,1,0:T(8,128)S(1)} async-done(((f32[16,32,128]{2,1,0:T(8,128)}), f32[16,32,128]{2,1,0:T(8,128)S(1)}, u32[]{:S(2)}, u32[]{:S(2)}) %all-to-all-start) | async-done | bytes 262176 | tf_op jit(solution)/shard_map/all_to_all | solution.py:309
  89.0 0.9 %finish.1 = bf16[256,128]{1,0:T(8,128)(2,1)} custom-call(s32[1]{0:T(128)} %bitcast.me_ref, f32[512,128]{1,0:T(8,128)S(1)} %bitcast.13, f32[256,128]{1,0:T(8,128)S(1)} %get-tuple-element.18.first_ref, f32[256,128]{1,0:T(8,128)S(1)} %get-tuple-element.19.conv_ref, f32[9,128]{1,0:T(8,128)S(1)} %reshape.13.taps_ref, f32[16,128]{1,0:T(8,128)S(1)} %copy-done.4, ...), custom_call_target="tpu_custom_call" | custom-call | tf_op jit(solution)/shard_map/finish/pallas_call | solution.py:325
  (6 shorter events, 0.1 us)
Async XLA Ops:
  0.0 54.8 %copy-start = (f32[3,3,4096]{2,1,0:T(4,128)S(1)}, f32[3,3,4096]{2,1,0:T(4,128)}, u32[]{:S(2)}) copy-start(f32[3,3,4096]{2,1,0:T(4,128)} %param.8) | copy-start | bytes 442372
  33.5 9.9 %collective-permute-start.2 = (bf16[8,256,128]{2,1,0:T(8,128)(2,1)S(1)}, bf16[8,256,128]{2,1,0:T(8,128)(2,1)S(1)}, u32[]{:S(2)}, u32[]{:S(2)}) collective-permute-start(bf16[8,256,128]{2,1,0:T(8,128)(2,1)S(1)} %bitcast.11), channel_id=1, source_target_pairs={{0,16},{1,17},{2,18},{3,19},{4,20},{5,21},{6,22},{7,23},{8,24},{9,... | collective-permute-start | bytes 1572872 | tf_op jit(solution)/shard_map/ppermute | solution.py:243
  43.4 18.1 %copy-start.4 = (f32[16,128]{1,0:T(8,128)S(1)}, f32[16,128]{1,0:T(8,128)}, u32[]{:S(2)}) copy-start(f32[16,128]{1,0:T(8,128)} %rate_ref.5) | copy-start | bytes 24580
  43.4 18.1 %collective-permute-start.3 = (bf16[5,256,128]{2,1,0:T(8,128)(2,1)S(1)}, bf16[5,256,128]{2,1,0:T(8,128)(2,1)S(1)}, u32[]{:S(2)}, u32[]{:S(2)}) collective-permute-start(bf16[5,256,128]{2,1,0:T(8,128)(2,1)S(1)} %slice.20), channel_id=1, source_target_pairs={{0,15},{1,0},{2,1},{3,2},{4,3},{5,4},{6,5},{7,6},{8,7},{9,8},{10,9... | collective-permute-start | bytes 983048 | tf_op jit(solution)/shard_map/ppermute | solution.py:247
  47.4 9.1 %collective-permute-start = (bf16[4,256,128]{2,1,0:T(8,128)(2,1)}, bf16[4,256,128]{2,1,0:T(8,128)(2,1)S(1)}, u32[]{:S(2)}, u32[]{:S(2)}) collective-permute-start(bf16[4,256,128]{2,1,0:T(8,128)(2,1)} %bitcast.4), channel_id=1, source_target_pairs={{0,15},{1,0},{2,1},{3,2},{4,3},{5,4},{6,5},{7,6},{8,7},{9,8},{10,9... | collective-permute-start | bytes 786440 | tf_op jit(solution)/shard_map/ppermute | solution.py:244
  49.7 8.3 %collective-permute-start.1 = (bf16[4,256,128]{2,1,0:T(8,128)(2,1)S(1)}, bf16[4,256,128]{2,1,0:T(8,128)(2,1)S(1)}, u32[]{:S(2)}, u32[]{:S(2)}) collective-permute-start(bf16[4,256,128]{2,1,0:T(8,128)(2,1)S(1)} %bitcast.16), channel_id=1, source_target_pairs={{0,1},{1,2},{2,3},{3,4},{4,5},{5,6},{6,7},{7,8},{8,9},{9,10},{10,1... | collective-permute-start | bytes 786440 | tf_op jit(solution)/shard_map/ppermute | solution.py:245
  52.7 8.7 %collective-permute-start.4 = (bf16[3,256,128]{2,1,0:T(8,128)(2,1)S(1)}, bf16[3,256,128]{2,1,0:T(8,128)(2,1)S(1)}, u32[]{:S(2)}, u32[]{:S(2)}) collective-permute-start(bf16[3,256,128]{2,1,0:T(8,128)(2,1)S(1)} %slice.21), channel_id=1, source_target_pairs={{0,1},{1,2},{2,3},{3,4},{4,5},{5,6},{6,7},{7,8},{8,9},{9,10},{10,1... | collective-permute-start | bytes 589832 | tf_op jit(solution)/shard_map/ppermute | solution.py:248
  54.8 0.7 copy-start.3
  55.5 0.7 copy-start.5
  58.0 1.9 %copy-start.1 = (bf16[4096,3,128]{2,0,1:T(8,128)(2,1)S(1)}, bf16[4096,3,128]{2,0,1:T(8,128)(2,1)}, u32[]{:S(2)}) copy-start(bf16[4096,3,128]{2,0,1:T(8,128)(2,1)} %param.7) | copy-start | bytes 9437188
  59.9 1.9 %copy-start.2 = (bf16[4096,3,128]{2,0,1:T(8,128)(2,1)S(1)}, bf16[4096,3,128]{2,0,1:T(8,128)(2,1)}, u32[]{:S(2)}) copy-start(bf16[4096,3,128]{2,0,1:T(8,128)(2,1)} %param.7) | copy-start | bytes 9437188
  61.4 18.7 %copy-start.6 = (f32[128]{0:T(128)S(1)}, f32[128]{0:T(128)}, u32[]{:S(2)}) copy-start(f32[128]{0:T(128)} %param.11) | copy-start | bytes 1540
  63.8 25.2 %all-to-all-start = ((f32[16,32,128]{2,1,0:T(8,128)}), f32[16,32,128]{2,1,0:T(8,128)S(1)}, u32[]{:S(2)}, u32[]{:S(2)}) async-start(f32[16,32,128]{2,1,0:T(8,128)} %get-tuple-element.14), calls=%async_computation | async-start | bytes 524288 | tf_op jit(solution)/shard_map/all_to_all | solution.py:309

commit v6 on v5

--- a/solution.py
+++ b/solution.py
@@ -47,15 +47,13 @@
     return jnp.concatenate(rows, axis=0)
 
 
-def early_kernel(place_ref, near_ref, near_up_ref, near_down_ref, far_ref, w_ref, acc_ref):
+def early_kernel(place_ref, near_ref, odd_ref, far_ref, w_ref, acc_ref):
     line, parity = place_ref[0], place_ref[1]
     pairs, _, block = near_ref.shape
-    split = near_up_ref.shape[0]
     for k in range(0, pairs, 2):
         lefts, owners = [], []
         for i in (k, k + 1):
-            odd = near_up_ref[i] if i < split else near_down_ref[i - split]
-            lefts += [near_ref[i], odd, far_ref[i]]
+            lefts += [near_ref[i], odd_ref[i], far_ref[i]]
             own, other = 2 * pairs * line + 2 * i, 2 * pairs * (1 - line) + 2 * i
             owners += [own + parity, own + 1 - parity, other + parity]
         part = jnp.dot(
@@ -237,16 +235,14 @@
     across = [(i, (i + line) % shard_count) for i in range(shard_count)]
     up = [(l * line + z, l * line + (z - 1) % line) for l in range(2) for z in range(line)]
     down = [(l * line + z, l * line + (z + 1) % line) for l in range(2) for z in range(line)]
-    half = pairs // 2
+    few = 3 * pairs // 8
 
     near = lax.all_gather(features, "shard", axis=0, axis_index_groups=groups)
     far = lax.ppermute(near, "shard", across)
-    near_up = lax.ppermute(near[:half], "shard", up)
-    near_down = lax.ppermute(near[half:], "shard", down)
-    most = half + 1
-    far_up = lax.ppermute(far[:most], "shard", up)
-    far_down = lax.ppermute(far[most:], "shard", down)
-    return near, near_up, near_down, far, far_up, far_down
+    odd = lax.ppermute(near, "shard", up)
+    far_up = lax.ppermute(far[:few], "shard", up)
+    far_down = lax.ppermute(far[few:], "shard", down)
+    return near, odd, far, far_up, far_down
 
 
 def shards(features, in_proj, short_filter, residue, decay_rate, skip_gain):
@@ -280,15 +276,15 @@
     )(decay_rate, residue)
 
     place = jnp.stack([at // line, at % 2]).astype(jnp.int32)
-    near, near_up, near_down, far, far_up, far_down = pieces
+    near, odd, far, far_up, far_down = pieces
     early = pl.pallas_call(
         early_kernel,
-        in_specs=[smem] + [vmem] * 5,
+        in_specs=[smem] + [vmem] * 4,
         out_specs=vmem,
         out_shape=jax.ShapeDtypeStruct((length, 3 * channels), f32),
         compiler_params=params(12),
         name="early",
-    )(place, near, near_up, near_down, far, w_branch)
+    )(place, near, odd, far, w_branch)
     lead, drive, message = pl.pallas_call(
         functools.partial(project_kernel, modes, length, total),
         in_specs=[smem] + [vmem] * 7,

time: 90.4 us -> 82.1 us (0.908)
  waiting for transfers between devices: 15.7 us -> 10.9 us
  starting transfers between devices: 30.1 us -> 27.3 us
    ppermute x1, waiting for transfers between devices: 6.71 us -> 3.42 us  [gather_features(): far = lax.ppermute(near, 'shard', across)]
    all_to_all x1, starting transfers between devices: 16.3 us -> 14.2 us  [shards(): lax.all_to_all(message, 'seq', 0, 0).reshape(seq_count * ROWS, channels)]
    ppermute x4 -> x3, waiting for transfers between devices: 1.52 us -> 0.01 us  [the longest x1 0.01 us: gather_features(): odd = lax.ppermute(near, 'shard', up)]
    ppermute x4 -> x3, starting transfers between devices: 10.6 us -> 9.77 us  [the longest x1 4.43 us: gather_features(): far_up = lax.ppermute(far[:few], 'shard', up)]
  transfers between devices with their start and end apart: 6 -> 5, of which waited for: 3 -> 2; matrix products, arithmetic and copies ran while one was open for 1% -> 0% of each run, Pallas kernels for 3% -> 4%
where the time goes in v6:
time: 82.1 us; the launch traced here: 81.6 us
  blocking collectives  33.4 us (41%)
  starting transfers between devices  27.3 us (33%)
  waiting for transfers between devices  10.9 us (13%)
  Pallas kernels  6.04 us (7%)
  local copies, waits for them, and re-layouts  3.67 us (4%)
    all_gather x1, blocking collectives, gather_features(): near = lax.all_gather(features, 'shard', axis=0, axis_index_groups=groups)  33.4 us
    all_to_all x1, starting transfers between devices, shards(): lax.all_to_all(message, 'seq', 0, 0).reshape(seq_count * ROWS, channels)  14.2 us
    all_to_all x1, waiting for transfers between devices, shards(): lax.all_to_all(message, 'seq', 0, 0).reshape(seq_count * ROWS, channels)  7.5 us
    ppermute x1, starting transfers between devices, gather_features(): far_up = lax.ppermute(far[:few], 'shard', up)  4.43 us
    unnamed x14, local copies, waits for them, and re-layouts  3.61 us
    ppermute x1, waiting for transfers between devices, gather_features(): far = lax.ppermute(near, 'shard', across)  3.42 us
    ppermute x1, starting transfers between devices, gather_features(): far = lax.ppermute(near, 'shard', across)  3.33 us
    ppermute x1, starting transfers between devices, gather_features(): odd = lax.ppermute(near, 'shard', up)  3.28 us
  transfers between devices with their start and end apart: 5, of which 2 were waited for; matrix products, arithmetic and copies ran while one was open for 0% of the time, Pallas kernels for 4%

profile of v6, /device:TPU:1, one launch (start us, length us, event | category | flops | bytes accessed | tf_op | source)
XLA Modules:
  0.0 81.6 jit_solution(4554308414101408839)
XLA Ops:
  0.0 0.0 copy-start
  0.0 33.4 %all-gather = bf16[2048,128]{1,0:T(8,128)(2,1)S(1)} all-gather(bf16[256,128]{1,0:T(8,128)(2,1)} %param.6), channel_id=2, replica_groups={{0,2,4,6,8,10,12,14},{1,3,5,7,9,11,13,15},{16,18,20,22,24,26,28,30},{17..., dimensions={0}, use_global_device_ids=true | all-gather | bytes 589824 | tf_op jit(solution)/shard_map/all_gather | solution.py:240
  33.5 0.0 copy-start.4
  33.5 3.3 %collective-permute-start.1 = (bf16[8,256,128]{2,1,0:T(8,128)(2,1)S(1)}, bf16[8,256,128]{2,1,0:T(8,128)(2,1)S(1)}, u32[]{:S(2)}, u32[]{:S(2)}) collective-permute-start(bf16[8,256,128]{2,1,0:T(8,128)(2,1)S(1)} %bitcast.9), channel_id=1, source_target_pairs={{0,16},{1,17},{2,18},{3,19},{4,20},{5,21},{6,22},{7,23},{8,24},{9,... | collective-permute-start | bytes 1572872 | tf_op jit(solution)/shard_map/ppermute | solution.py:241
  36.8 3.3 %collective-permute-start = (bf16[8,256,128]{2,1,0:T(8,128)(2,1)S(1)}, bf16[8,256,128]{2,1,0:T(8,128)(2,1)S(1)}, u32[]{:S(2)}, u32[]{:S(2)}) collective-permute-start(bf16[8,256,128]{2,1,0:T(8,128)(2,1)S(1)} %bitcast.10), channel_id=1, source_target_pairs={{0,15},{1,0},{2,1},{3,2},{4,3},{5,4},{6,5},{7,6},{8,7},{9,8},{10,9... | collective-permute-start | bytes 1572872 | tf_op jit(solution)/shard_map/ppermute | solution.py:242
  40.1 3.4 %collective-permute-done.1.far_ref = bf16[8,256,128]{2,1,0:T(8,128)(2,1)S(1)} collective-permute-done((bf16[8,256,128]{2,1,0:T(8,128)(2,1)S(1)}, bf16[8,256,128]{2,1,0:T(8,128)(2,1)S(1)}, u32[]{:S(2)}, u32[]{:S(2)}) %collective-permute-start.1) | collective-permute-done | bytes 524320 | tf_op jit(solution)/shard_map/ppermute | solution.py:241
  43.5 2.1 %collective-permute-start.3 = (bf16[5,256,128]{2,1,0:T(8,128)(2,1)S(1)}, bf16[5,256,128]{2,1,0:T(8,128)(2,1)S(1)}, u32[]{:S(2)}, u32[]{:S(2)}) collective-permute-start(bf16[5,256,128]{2,1,0:T(8,128)(2,1)S(1)} %slice.9), channel_id=1, source_target_pairs={{0,1},{1,2},{2,3},{3,4},{4,5},{5,6},{6,7},{7,8},{8,9},{9,10},{10,1... | collective-permute-start | bytes 983048 | tf_op jit(solution)/shard_map/ppermute | solution.py:244
  45.6 4.4 %collective-permute-start.2 = (bf16[3,256,128]{2,1,0:T(8,128)(2,1)S(1)}, bf16[3,256,128]{2,1,0:T(8,128)(2,1)S(1)}, u32[]{:S(2)}, u32[]{:S(2)}) collective-permute-start(bf16[3,256,128]{2,1,0:T(8,128)(2,1)S(1)} %slice.8), channel_id=1, source_target_pairs={{0,15},{1,0},{2,1},{3,2},{4,3},{5,4},{6,5},{7,6},{8,7},{9,8},{10,9... | collective-permute-start | bytes 589832 | tf_op jit(solution)/shard_map/ppermute | solution.py:243
  50.1 0.0 copy-done
  50.1 0.0 copy-start.3
  50.1 0.7 copy-done.3
  50.8 0.0 copy-start.5
  50.8 0.7 copy-done.5
  51.5 0.2 tables.1
  51.7 0.1 pad_add_fusion.place_ref
  51.8 0.0 collective-permute-done.odd_ref
  51.8 0.0 copy-start.1
  51.8 1.9 %copy-done.1 = bf16[4096,3,128]{2,0,1:T(8,128)(2,1)S(1)} copy-done((bf16[4096,3,128]{2,0,1:T(8,128)(2,1)S(1)}, bf16[4096,3,128]{2,0,1:T(8,128)(2,1)}, u32[]{:S(2)}) %copy-start.1) | copy-done | bytes 3145752
  53.7 0.0 copy-start.2
  53.7 1.5 %early.1.early_ref = f32[256,384]{1,0:T(8,128)S(1)} custom-call(s32[2]{0:T(128)S(1)} %pad_add_fusion.place_ref, bf16[8,256,128]{2,1,0:T(8,128)(2,1)S(1)} %bitcast.11, bf16[8,256,128]{2,1,0:T(8,128)(2,1)S(1)} %collective-permute-done.odd_ref, bf16[8,256,128]{2,1,0:T(8,128)(2,1)S(1)} %collective-permute-done.1.far_ref, bf16[3,4096,128]{2,1,0:T(8,128)(2,1)S(1)} %bitcast.7), custom_call_target="tpu_custom_call" | custom-call | tf_op jit(solution)/shard_map/early/pallas_call | solution.py:280
  55.2 0.0 copy-start.6
  55.3 0.0 collective-permute-done.2.far_up_ref
  55.3 0.0 collective-permute-done.3.far_down_ref
  55.3 0.0 copy-done.4
  55.3 0.3 copy-done.2
  55.6 2.0 %project.1 = (f32[264,128]{1,0:T(8,128)S(1)}, f32[256,128]{1,0:T(8,128)S(1)}, f32[16,32,128]{2,1,0:T(8,128)}) custom-call(s32[2]{0:T(128)S(1)} %pad_add_fusion.place_ref, f32[256,384]{1,0:T(8,128)S(1)} %early.1.early_ref, bf16[3,256,128]{2,1,0:T(8,128)(2,1)S(1)} %collective-permute-done.2.far_up_ref, ...), custom_call_target="tpu_custom_call" | custom-call | tf_op jit(solution)/shard_map/project/pallas_call | solution.py:288
  57.6 14.2 %all-to-all-start = ((f32[16,32,128]{2,1,0:T(8,128)}), f32[16,32,128]{2,1,0:T(8,128)S(1)}, u32[]{:S(2)}, u32[]{:S(2)}) async-start(f32[16,32,128]{2,1,0:T(8,128)} %get-tuple-element.14), calls=%async_computation | async-start | bytes 524288 | tf_op jit(solution)/shard_map/all_to_all | solution.py:305
  71.8 0.0 copy-done.6
  71.8 1.4 %conv.1 = (f32[256,128]{1,0:T(8,128)S(1)}, f32[256,128]{1,0:T(8,128)S(1)}) custom-call(f32[256,128]{1,0:T(8,128)S(1)} %get-tuple-element.15.drive_ref, f32[264,128]{1,0:T(8,128)S(1)} %get-tuple-element.16.h_ref, f32[1,128]{1,0:T(1,128)S(1)} %bitcast.13, f32[264,128]{1,0:T(8,128)S(1)} %get-tuple-element.17.lead_ref, f32[9,128]{1,0:T(8,128)S(1)} %reshape.13.taps_ref), custom_call_target="tpu_custom_call" | custom-call | tf_op jit(solution)/shard_map/conv/pallas_call | solution.py:307
  73.2 7.5 %all-to-all-done = f32[16,32,128]{2,1,0:T(8,128)S(1)} async-done(((f32[16,32,128]{2,1,0:T(8,128)}), f32[16,32,128]{2,1,0:T(8,128)S(1)}, u32[]{:S(2)}, u32[]{:S(2)}) %all-to-all-start) | async-done | bytes 262176 | tf_op jit(solution)/shard_map/all_to_all | solution.py:305
  80.7 0.9 %finish.1 = bf16[256,128]{1,0:T(8,128)(2,1)} custom-call(s32[1]{0:T(128)} %bitcast.me_ref, f32[512,128]{1,0:T(8,128)S(1)} %bitcast.12, f32[256,128]{1,0:T(8,128)S(1)} %get-tuple-element.18.first_ref, f32[256,128]{1,0:T(8,128)S(1)} %get-tuple-element.19.conv_ref, f32[9,128]{1,0:T(8,128)S(1)} %reshape.13.taps_ref, f32[16,128]{1,0:T(8,128)S(1)} %copy-done.4, ...), custom_call_target="tpu_custom_call" | custom-call | tf_op jit(solution)/shard_map/finish/pallas_call | solution.py:321
  (4 shorter events, 0.1 us)
Async XLA Ops:
  0.0 50.1 %copy-start = (f32[3,3,4096]{2,1,0:T(4,128)S(1)}, f32[3,3,4096]{2,1,0:T(4,128)}, u32[]{:S(2)}) copy-start(f32[3,3,4096]{2,1,0:T(4,128)} %param.8) | copy-start | bytes 442372
  33.5 21.8 %copy-start.4 = (f32[16,128]{1,0:T(8,128)S(1)}, f32[16,128]{1,0:T(8,128)}, u32[]{:S(2)}) copy-start(f32[16,128]{1,0:T(8,128)} %rate_ref.5) | copy-start | bytes 24580
  33.5 10.0 %collective-permute-start.1 = (bf16[8,256,128]{2,1,0:T(8,128)(2,1)S(1)}, bf16[8,256,128]{2,1,0:T(8,128)(2,1)S(1)}, u32[]{:S(2)}, u32[]{:S(2)}) collective-permute-start(bf16[8,256,128]{2,1,0:T(8,128)(2,1)S(1)} %bitcast.9), channel_id=1, source_target_pairs={{0,16},{1,17},{2,18},{3,19},{4,20},{5,21},{6,22},{7,23},{8,24},{9,... | collective-permute-start | bytes 1572872 | tf_op jit(solution)/shard_map/ppermute | solution.py:241
  36.8 15.0 %collective-permute-start = (bf16[8,256,128]{2,1,0:T(8,128)(2,1)S(1)}, bf16[8,256,128]{2,1,0:T(8,128)(2,1)S(1)}, u32[]{:S(2)}, u32[]{:S(2)}) collective-permute-start(bf16[8,256,128]{2,1,0:T(8,128)(2,1)S(1)} %bitcast.10), channel_id=1, source_target_pairs={{0,15},{1,0},{2,1},{3,2},{4,3},{5,4},{6,5},{7,6},{8,7},{9,8},{10,9... | collective-permute-start | bytes 1572872 | tf_op jit(solution)/shard_map/ppermute | solution.py:242
  43.5 11.7 %collective-permute-start.3 = (bf16[5,256,128]{2,1,0:T(8,128)(2,1)S(1)}, bf16[5,256,128]{2,1,0:T(8,128)(2,1)S(1)}, u32[]{:S(2)}, u32[]{:S(2)}) collective-permute-start(bf16[5,256,128]{2,1,0:T(8,128)(2,1)S(1)} %slice.9), channel_id=1, source_target_pairs={{0,1},{1,2},{2,3},{3,4},{4,5},{5,6},{6,7},{7,8},{8,9},{9,10},{10,1... | collective-permute-start | bytes 983048 | tf_op jit(solution)/shard_map/ppermute | solution.py:244
  45.6 9.6 %collective-permute-start.2 = (bf16[3,256,128]{2,1,0:T(8,128)(2,1)S(1)}, bf16[3,256,128]{2,1,0:T(8,128)(2,1)S(1)}, u32[]{:S(2)}, u32[]{:S(2)}) collective-permute-start(bf16[3,256,128]{2,1,0:T(8,128)(2,1)S(1)} %slice.8), channel_id=1, source_target_pairs={{0,15},{1,0},{2,1},{3,2},{4,3},{5,4},{6,5},{7,6},{8,7},{9,8},{10,9... | collective-permute-start | bytes 589832 | tf_op jit(solution)/shard_map/ppermute | solution.py:243
  50.1 0.7 copy-start.3
  50.8 0.7 copy-start.5
  51.8 1.9 %copy-start.1 = (bf16[4096,3,128]{2,0,1:T(8,128)(2,1)S(1)}, bf16[4096,3,128]{2,0,1:T(8,128)(2,1)}, u32[]{:S(2)}) copy-start(bf16[4096,3,128]{2,0,1:T(8,128)(2,1)} %param.7) | copy-start | bytes 9437188
  53.7 1.9 %copy-start.2 = (bf16[4096,3,128]{2,0,1:T(8,128)(2,1)S(1)}, bf16[4096,3,128]{2,0,1:T(8,128)(2,1)}, u32[]{:S(2)}) copy-start(bf16[4096,3,128]{2,0,1:T(8,128)(2,1)} %param.7) | copy-start | bytes 9437188
  55.2 16.6 %copy-start.6 = (f32[128]{0:T(128)S(1)}, f32[128]{0:T(128)}, u32[]{:S(2)}) copy-start(f32[128]{0:T(128)} %param.11) | copy-start | bytes 1540
  57.6 23.1 %all-to-all-start = ((f32[16,32,128]{2,1,0:T(8,128)}), f32[16,32,128]{2,1,0:T(8,128)S(1)}, u32[]{:S(2)}, u32[]{:S(2)}) async-start(f32[16,32,128]{2,1,0:T(8,128)} %get-tuple-element.14), calls=%async_computation | async-start | bytes 524288 | tf_op jit(solution)/shard_map/all_to_all | solution.py:305

commit v7 on v6

--- a/solution.py
+++ b/solution.py
@@ -47,37 +47,45 @@
     return jnp.concatenate(rows, axis=0)
 
 
-def early_kernel(place_ref, near_ref, odd_ref, far_ref, w_ref, acc_ref):
+def early_kernel(place_ref, near_ref, odd_ref, far_ref, w_ref, acc_ref, rest_ref, held_ref, sems):
     line, parity = place_ref[0], place_ref[1]
     pairs, _, block = near_ref.shape
-    for k in range(0, pairs, 2):
+    steps = sems.shape[0]
+    per_step = pairs // steps
+    depth = 2 * per_step * block
+
+    def copy(step, half):
+        rows = pl.ds(half * 2 * pairs * block + step * depth, depth)
+        return pltpu.make_async_copy(w_ref.at[:, rows, :], held_ref.at[:, rows, :], sems.at[step, half])
+
+    for step in range(steps):
+        for half in range(2):
+            copy(step, half).start()
+    for step in range(steps):
+        for half in range(2):
+            copy(step, half).wait()
         lefts, owners = [], []
-        for i in (k, k + 1):
+        for i in range(step * per_step, (step + 1) * per_step):
             lefts += [near_ref[i], odd_ref[i], far_ref[i]]
             own, other = 2 * pairs * line + 2 * i, 2 * pairs * (1 - line) + 2 * i
             owners += [own + parity, own + 1 - parity, other + parity]
+            rest_ref[i * block : (i + 1) * block, :] = weight_rows(held_ref, [other + 1 - parity], block)
         part = jnp.dot(
             jnp.concatenate(lefts, axis=1),
-            weight_rows(w_ref, owners, block),
+            weight_rows(held_ref, owners, block),
             preferred_element_type=jnp.float32,
         )
-        acc_ref[...] = part if k == 0 else acc_ref[...] + part
+        acc_ref[...] = part if step == 0 else acc_ref[...] + part
 
 
 def project_kernel(
-    modes, length, total, place_ref, early_ref, far_up_ref, far_down_ref, w_ref, taps_ref, rate_ref,
+    modes, length, total, early_ref, rest_ref, far_up_ref, far_down_ref, taps_ref, rate_ref,
     e_ref, lead_ref, drive_ref, message_ref, pair_ref, state_ref,
 ):
-    line, parity = place_ref[0], place_ref[1]
-    split, _, block = far_up_ref.shape
-    pairs = split + far_down_ref.shape[0]
     channels = drive_ref.shape[1]
-    owners = [2 * pairs * (1 - line) + 2 * k + 1 - parity for k in range(pairs)]
-    left = [far_up_ref[k] if k < split else far_down_ref[k - split] for k in range(pairs)]
+    left = [ref[k] for ref in (far_up_ref, far_down_ref) for k in range(ref.shape[0])]
     acc = early_ref[...] + jnp.dot(
-        jnp.concatenate(left, axis=1),
-        weight_rows(w_ref, owners, block),
-        preferred_element_type=jnp.float32,
+        jnp.concatenate(left, axis=1), rest_ref[...], preferred_element_type=jnp.float32
     )
     proj = acc.astype(jnp.bfloat16).astype(jnp.float32)
     pad = TILE
@@ -227,7 +235,7 @@
     out_ref[...] = value_ref[...].astype(out_ref.dtype)
 
 
-def gather_features(features):
+def gather_features(features, *ready):
     shard_count = lax.axis_size("shard")
     line = shard_count // 2
     pairs = line // 2
@@ -240,9 +248,10 @@
     near = lax.all_gather(features, "shard", axis=0, axis_index_groups=groups)
     far = lax.ppermute(near, "shard", across)
     odd = lax.ppermute(near, "shard", up)
+    far, *ready = lax.optimization_barrier((far, *ready))
     far_up = lax.ppermute(far[:few], "shard", up)
     far_down = lax.ppermute(far[few:], "shard", down)
-    return near, odd, far, far_up, far_down
+    return (near, odd, far, far_up, far_down), ready
 
 
 def shards(features, in_proj, short_filter, residue, decay_rate, skip_gain):
@@ -260,11 +269,10 @@
     def params(mebibytes):
         return pltpu.CompilerParams(vmem_limit_bytes=mebibytes << 20)
 
-    pieces = gather_features(features)
     w_branch = in_proj.transpose(1, 0, 2)
     at = lax.axis_index("shard")
     taps = lax.dynamic_slice_in_dim(short_filter, at * channels, channels, 2).reshape(-1, channels)
-    h, e, gain = pl.pallas_call(
+    tables = pl.pallas_call(
         functools.partial(tables_kernel, modes, length, total),
         out_shape=(
             jax.ShapeDtypeStruct((length + TILE, channels), f32),
@@ -275,19 +283,29 @@
         name="tables",
     )(decay_rate, residue)
 
+    pieces, (h, e, gain) = gather_features(features, *tables)
     place = jnp.stack([at // line, at % 2]).astype(jnp.int32)
     near, odd, far, far_up, far_down = pieces
-    early = pl.pallas_call(
+    hbm = pl.BlockSpec(memory_space=pltpu.HBM)
+    pairs, _, block = near.shape
+    early, rest = pl.pallas_call(
         early_kernel,
-        in_specs=[smem] + [vmem] * 4,
-        out_specs=vmem,
-        out_shape=jax.ShapeDtypeStruct((length, 3 * channels), f32),
-        compiler_params=params(12),
+        in_specs=[smem] + [vmem] * 3 + [hbm],
+        out_specs=(vmem,) * 2,
+        out_shape=(
+            jax.ShapeDtypeStruct((length, 3 * channels), f32),
+            jax.ShapeDtypeStruct((pairs * block, 3 * channels), w_branch.dtype),
+        ),
+        scratch_shapes=[
+            pltpu.VMEM(w_branch.shape, w_branch.dtype),
+            pltpu.SemaphoreType.DMA((pairs // 2, 2)),
+        ],
+        compiler_params=params(14),
         name="early",
-    )(place, near, odd, far, w_branch)
+    )(place, near, odd, far, pltpu.with_memory_space_constraint(w_branch, pltpu.HBM))
     lead, drive, message = pl.pallas_call(
         functools.partial(project_kernel, modes, length, total),
-        in_specs=[smem] + [vmem] * 7,
+        in_specs=[vmem] * 7,
         out_specs=(vmem,) * 3,
         out_shape=(
             jax.ShapeDtypeStruct((length + TILE, channels), f32),
@@ -300,7 +318,7 @@
         ],
         compiler_params=params(12),
         name="project",
-    )(place, early, far_up, far_down, w_branch, taps, decay_rate, e)
+    )(early, rest, far_up, far_down, taps, decay_rate, e)
 
     everyone = lax.all_to_all(message, "seq", 0, 0).reshape(seq_count * ROWS, channels)
     skip = skip_gain.reshape(1, channels)

time: 82.1 us -> 79.4 us (0.967)
  local copies, waits for them, and re-layouts: 3.67 us -> 1.46 us
  starting transfers between devices: 27.3 us -> 25.9 us
  Pallas kernels: 6.04 us -> 7.21 us
    unnamed x14 -> x10, local copies, waits for them, and re-layouts: 3.61 us -> 1.4 us
    pallas_call x1, Pallas kernels: 1.53 us -> 3.24 us  [shards(): pl.pallas_call(early_kernel, in_specs=[smem] + [vmem] * 3 + [hbm], out_sp...]
    ppermute x1, waiting for transfers between devices: 3.42 us -> 1.83 us  [gather_features(): far = lax.ppermute(near, 'shard', across)]
    ppermute x1, waiting for transfers between devices: 0.01 us -> 1.38 us  [gather_features(): far_up = lax.ppermute(far[:few], 'shard', up)]
    all_to_all x1, starting transfers between devices: 14.2 us -> 12.9 us  [shards(): lax.all_to_all(message, 'seq', 0, 0).reshape(seq_count * ROWS, channels)]
  transfers between devices with their start and end apart: 5 -> 5, of which waited for: 2 -> 3; matrix products, arithmetic and copies ran while one was open for 0% -> 0% of each run, Pallas kernels for 4% -> 6%
where the time goes in v7:
time: 79.4 us; the launch traced here: 78.9 us
  blocking collectives  33.4 us (42%)
  starting transfers between devices  25.9 us (33%)
  waiting for transfers between devices  10.7 us (13%)
  Pallas kernels  7.21 us (9%)
  local copies, waits for them, and re-layouts  1.46 us (2%)
    all_gather x1, blocking collectives, gather_features(): near = lax.all_gather(features, 'shard', axis=0, axis_index_groups=groups)  33.4 us
    all_to_all x1, starting transfers between devices, shards(): lax.all_to_all(message, 'seq', 0, 0).reshape(seq_count * ROWS, channels)  12.9 us
    all_to_all x1, waiting for transfers between devices, shards(): lax.all_to_all(message, 'seq', 0, 0).reshape(seq_count * ROWS, channels)  7.5 us
    ppermute x1, starting transfers between devices, gather_features(): far_up = lax.ppermute(far[:few], 'shard', up)  4.43 us
    ppermute x1, starting transfers between devices, gather_features(): odd = lax.ppermute(near, 'shard', up)  3.28 us
    pallas_call x1, Pallas kernels, shards(): pl.pallas_call(early_kernel, in_specs=[smem] + [vmem] * 3 + [hbm], out_sp...  3.24 us
    ppermute x1, starting transfers between devices, gather_features(): far = lax.ppermute(near, 'shard', across)  3.19 us
    ppermute x1, starting transfers between devices, gather_features(): far_down = lax.ppermute(far[few:], 'shard', down)  2.07 us
  transfers between devices with their start and end apart: 5, of which 3 were waited for; matrix products, arithmetic and copies ran while one was open for 0% of the time, Pallas kernels for 6%

profile of v7, /device:TPU:1, one launch (start us, length us, event | category | flops | bytes accessed | tf_op | source)
XLA Modules:
  0.0 78.9 jit_solution(18395975949646948509)
XLA Ops:
  0.0 0.0 copy-start
  0.0 0.0 copy-start.2
  0.0 33.4 %all-gather = bf16[2048,128]{1,0:T(8,128)(2,1)S(1)} all-gather(bf16[256,128]{1,0:T(8,128)(2,1)} %param.6), channel_id=2, replica_groups={{0,2,4,6,8,10,12,14},{1,3,5,7,9,11,13,15},{16,18,20,22,24,26,28,30},{17..., dimensions={0}, use_global_device_ids=true | all-gather | bytes 589824 | tf_op jit(solution)/shard_map/all_gather | solution.py:248
  33.5 3.2 %collective-permute-start.1 = (bf16[8,256,128]{2,1,0:T(8,128)(2,1)S(1)}, bf16[8,256,128]{2,1,0:T(8,128)(2,1)S(1)}, u32[]{:S(2)}, u32[]{:S(2)}) collective-permute-start(bf16[8,256,128]{2,1,0:T(8,128)(2,1)S(1)} %bitcast.7), channel_id=1, source_target_pairs={{0,16},{1,17},{2,18},{3,19},{4,20},{5,21},{6,22},{7,23},{8,24},{9,... | collective-permute-start | bytes 1572872 | tf_op jit(solution)/shard_map/ppermute | solution.py:249
  36.7 3.3 %collective-permute-start = (bf16[8,256,128]{2,1,0:T(8,128)(2,1)S(1)}, bf16[8,256,128]{2,1,0:T(8,128)(2,1)S(1)}, u32[]{:S(2)}, u32[]{:S(2)}) collective-permute-start(bf16[8,256,128]{2,1,0:T(8,128)(2,1)S(1)} %bitcast.8), channel_id=1, source_target_pairs={{0,15},{1,0},{2,1},{3,2},{4,3},{5,4},{6,5},{7,6},{8,7},{9,8},{10,9... | collective-permute-start | bytes 1572872 | tf_op jit(solution)/shard_map/ppermute | solution.py:250
  39.9 0.0 copy-start.1
  40.0 0.7 copy-done.1
  40.6 0.0 copy-start.3
  40.6 0.7 copy-done.3
  41.3 0.2 tables.1
  41.5 1.8 %collective-permute-done.1.far_ref = bf16[8,256,128]{2,1,0:T(8,128)(2,1)S(1)} collective-permute-done((bf16[8,256,128]{2,1,0:T(8,128)(2,1)S(1)}, bf16[8,256,128]{2,1,0:T(8,128)(2,1)S(1)}, u32[]{:S(2)}, u32[]{:S(2)}) %collective-permute-start.1) | collective-permute-done | bytes 524320 | tf_op jit(solution)/shard_map/ppermute | solution.py:249
  43.4 2.1 %collective-permute-start.3 = (bf16[5,256,128]{2,1,0:T(8,128)(2,1)S(1)}, bf16[5,256,128]{2,1,0:T(8,128)(2,1)S(1)}, u32[]{:S(2)}, u32[]{:S(2)}) collective-permute-start(bf16[5,256,128]{2,1,0:T(8,128)(2,1)S(1)} %slice.7), channel_id=1, source_target_pairs={{0,1},{1,2},{2,3},{3,4},{4,5},{5,6},{6,7},{7,8},{8,9},{9,10},{10,1... | collective-permute-start | bytes 983048 | tf_op jit(solution)/shard_map/ppermute | solution.py:253
  45.5 4.4 %collective-permute-start.2 = (bf16[3,256,128]{2,1,0:T(8,128)(2,1)S(1)}, bf16[3,256,128]{2,1,0:T(8,128)(2,1)S(1)}, u32[]{:S(2)}, u32[]{:S(2)}) collective-permute-start(bf16[3,256,128]{2,1,0:T(8,128)(2,1)S(1)} %slice.6), channel_id=1, source_target_pairs={{0,15},{1,0},{2,1},{3,2},{4,3},{5,4},{6,5},{7,6},{8,7},{9,8},{10,9... | collective-permute-start | bytes 589832 | tf_op jit(solution)/shard_map/ppermute | solution.py:252
  49.9 0.0 copy-done
  50.0 0.1 pad_add_fusion.place_ref
  50.1 0.0 collective-permute-done.odd_ref
  50.1 0.0 copy-start.4
  50.1 3.2 %early.1 = (f32[256,384]{1,0:T(8,128)S(1)}, bf16[1024,384]{1,0:T(8,128)(2,1)S(1)}) custom-call(s32[2]{0:T(128)S(1)} %pad_add_fusion.place_ref, bf16[8,256,128]{2,1,0:T(8,128)(2,1)S(1)} %bitcast.9, bf16[8,256,128]{2,1,0:T(8,128)(2,1)S(1)} %collective-permute-done.odd_ref, bf16[8,256,128]{2,1,0:T(8,128)(2,1)S(1)} %collective-permute-done.1.far_ref, ...), custom_call_target="tpu_custom_call" | custom-call | tf_op jit(solution)/shard_map/early/pallas_call | solution.py:291
  53.3 1.4 %collective-permute-done.2.far_up_ref = bf16[3,256,128]{2,1,0:T(8,128)(2,1)S(1)} collective-permute-done((bf16[3,256,128]{2,1,0:T(8,128)(2,1)S(1)}, bf16[3,256,128]{2,1,0:T(8,128)(2,1)S(1)}, u32[]{:S(2)}, u32[]{:S(2)}) %collective-permute-start.2) | collective-permute-done | bytes 196640 | tf_op jit(solution)/shard_map/ppermute | solution.py:252
  54.7 0.0 collective-permute-done.3.far_down_ref
  54.7 0.0 copy-done.2
  54.7 1.5 %project.1 = (f32[264,128]{1,0:T(8,128)S(1)}, f32[256,128]{1,0:T(8,128)S(1)}, f32[16,32,128]{2,1,0:T(8,128)}) custom-call(f32[256,384]{1,0:T(8,128)S(1)} %get-tuple-element.23.early_ref, bf16[1024,384]{1,0:T(8,128)(2,1)S(1)} %get-tuple-element.24.rest_ref, bf16[3,256,128]{2,1,0:T(8,128)(2,1)S(1)} %collective-permute-done.2.far_up_ref, ...), custom_call_target="tpu_custom_call" | custom-call | tf_op jit(solution)/shard_map/project/pallas_call | solution.py:306
  56.2 12.9 %all-to-all-start = ((f32[16,32,128]{2,1,0:T(8,128)}), f32[16,32,128]{2,1,0:T(8,128)S(1)}, u32[]{:S(2)}, u32[]{:S(2)}) async-start(f32[16,32,128]{2,1,0:T(8,128)} %get-tuple-element.26), calls=%async_computation | async-start | bytes 524288 | tf_op jit(solution)/shard_map/all_to_all | solution.py:323
  69.1 0.0 copy-done.4
  69.1 1.4 %conv.1 = (f32[256,128]{1,0:T(8,128)S(1)}, f32[256,128]{1,0:T(8,128)S(1)}) custom-call(f32[256,128]{1,0:T(8,128)S(1)} %get-tuple-element.27.drive_ref, f32[264,128]{1,0:T(8,128)S(1)} %get-tuple-element.28.h_ref, f32[1,128]{1,0:T(1,128)S(1)} %bitcast.11, f32[264,128]{1,0:T(8,128)S(1)} %get-tuple-element.29.lead_ref, f32[9,128]{1,0:T(8,128)S(1)} %reshape.13.taps_ref), custom_call_target="tpu_custom_call" | custom-call | tf_op jit(solution)/shard_map/conv/pallas_call | solution.py:325
  70.5 7.5 %all-to-all-done = f32[16,32,128]{2,1,0:T(8,128)S(1)} async-done(((f32[16,32,128]{2,1,0:T(8,128)}), f32[16,32,128]{2,1,0:T(8,128)S(1)}, u32[]{:S(2)}, u32[]{:S(2)}) %all-to-all-start) | async-done | bytes 262176 | tf_op jit(solution)/shard_map/all_to_all | solution.py:323
  78.0 0.9 %finish.1 = bf16[256,128]{1,0:T(8,128)(2,1)} custom-call(s32[1]{0:T(128)} %bitcast.me_ref, f32[512,128]{1,0:T(8,128)S(1)} %bitcast.10, f32[256,128]{1,0:T(8,128)S(1)} %get-tuple-element.30.first_ref, f32[256,128]{1,0:T(8,128)S(1)} %get-tuple-element.31.conv_ref, f32[9,128]{1,0:T(8,128)S(1)} %reshape.13.taps_ref, f32[16,128]{1,0:T(8,128)S(1)} %copy-done.2, ...), custom_call_target="tpu_custom_call" | custom-call | tf_op jit(solution)/shard_map/finish/pallas_call | solution.py:339
  (4 shorter events, 0.1 us)
Async XLA Ops:
  0.0 49.9 %copy-start = (f32[3,3,4096]{2,1,0:T(4,128)S(1)}, f32[3,3,4096]{2,1,0:T(4,128)}, u32[]{:S(2)}) copy-start(f32[3,3,4096]{2,1,0:T(4,128)} %param.8) | copy-start | bytes 442372
  0.0 54.7 %copy-start.2 = (f32[16,128]{1,0:T(8,128)S(1)}, f32[16,128]{1,0:T(8,128)}, u32[]{:S(2)}) copy-start(f32[16,128]{1,0:T(8,128)} %rate_ref.5) | copy-start | bytes 24580
  33.5 9.9 %collective-permute-start.1 = (bf16[8,256,128]{2,1,0:T(8,128)(2,1)S(1)}, bf16[8,256,128]{2,1,0:T(8,128)(2,1)S(1)}, u32[]{:S(2)}, u32[]{:S(2)}) collective-permute-start(bf16[8,256,128]{2,1,0:T(8,128)(2,1)S(1)} %bitcast.7), channel_id=1, source_target_pairs={{0,16},{1,17},{2,18},{3,19},{4,20},{5,21},{6,22},{7,23},{8,24},{9,... | collective-permute-start | bytes 1572872 | tf_op jit(solution)/shard_map/ppermute | solution.py:249
  36.7 13.4 %collective-permute-start = (bf16[8,256,128]{2,1,0:T(8,128)(2,1)S(1)}, bf16[8,256,128]{2,1,0:T(8,128)(2,1)S(1)}, u32[]{:S(2)}, u32[]{:S(2)}) collective-permute-start(bf16[8,256,128]{2,1,0:T(8,128)(2,1)S(1)} %bitcast.8), channel_id=1, source_target_pairs={{0,15},{1,0},{2,1},{3,2},{4,3},{5,4},{6,5},{7,6},{8,7},{9,8},{10,9... | collective-permute-start | bytes 1572872 | tf_op jit(solution)/shard_map/ppermute | solution.py:250
  39.9 0.7 copy-start.1
  40.6 0.7 copy-start.3
  43.4 11.3 %collective-permute-start.3 = (bf16[5,256,128]{2,1,0:T(8,128)(2,1)S(1)}, bf16[5,256,128]{2,1,0:T(8,128)(2,1)S(1)}, u32[]{:S(2)}, u32[]{:S(2)}) collective-permute-start(bf16[5,256,128]{2,1,0:T(8,128)(2,1)S(1)} %slice.7), channel_id=1, source_target_pairs={{0,1},{1,2},{2,3},{3,4},{4,5},{5,6},{6,7},{7,8},{8,9},{9,10},{10,1... | collective-permute-start | bytes 983048 | tf_op jit(solution)/shard_map/ppermute | solution.py:253
  45.5 9.2 %collective-permute-start.2 = (bf16[3,256,128]{2,1,0:T(8,128)(2,1)S(1)}, bf16[3,256,128]{2,1,0:T(8,128)(2,1)S(1)}, u32[]{:S(2)}, u32[]{:S(2)}) collective-permute-start(bf16[3,256,128]{2,1,0:T(8,128)(2,1)S(1)} %slice.6), channel_id=1, source_target_pairs={{0,15},{1,0},{2,1},{3,2},{4,3},{5,4},{6,5},{7,6},{8,7},{9,8},{10,9... | collective-permute-start | bytes 589832 | tf_op jit(solution)/shard_map/ppermute | solution.py:252
  50.1 19.0 %copy-start.4 = (f32[128]{0:T(128)S(1)}, f32[128]{0:T(128)}, u32[]{:S(2)}) copy-start(f32[128]{0:T(128)} %param.11) | copy-start | bytes 1540
  56.2 21.8 %all-to-all-start = ((f32[16,32,128]{2,1,0:T(8,128)}), f32[16,32,128]{2,1,0:T(8,128)S(1)}, u32[]{:S(2)}, u32[]{:S(2)}) async-start(f32[16,32,128]{2,1,0:T(8,128)} %get-tuple-element.26), calls=%async_computation | async-start | bytes 524288 | tf_op jit(solution)/shard_map/all_to_all | solution.py:323

commit v8 on v7

--- a/solution.py
+++ b/solution.py
@@ -39,43 +39,73 @@
         h_ref[(q + 1) * TILE : (q + 2) * TILE, :] = total_tile
 
 
-def weight_rows(w_ref, owners, block):
+def side_by_side(held_ref, starts, block):
     rows = []
-    for owner in owners:
-        at = pl.ds(pl.multiple_of(owner * block, block), block)
-        rows.append(jnp.concatenate([w_ref[b, at, :] for b in range(3)], axis=1))
+    for start in starts:
+        at = pl.ds(start, block)
+        rows.append(jnp.concatenate([held_ref[b, at, :] for b in range(3)], axis=1))
     return jnp.concatenate(rows, axis=0)
 
 
-def early_kernel(place_ref, near_ref, odd_ref, far_ref, w_ref, acc_ref, rest_ref, held_ref, sems):
+def first_kernel(place_ref, near_ref, w_ref, acc_ref, held_ref, sems):
     line, parity = place_ref[0], place_ref[1]
     pairs, _, block = near_ref.shape
-    steps = sems.shape[0]
-    per_step = pairs // steps
-    depth = 2 * per_step * block
-
-    def copy(step, half):
-        rows = pl.ds(half * 2 * pairs * block + step * depth, depth)
-        return pltpu.make_async_copy(w_ref.at[:, rows, :], held_ref.at[:, rows, :], sems.at[step, half])
-
-    for step in range(steps):
-        for half in range(2):
-            copy(step, half).start()
-    for step in range(steps):
-        for half in range(2):
-            copy(step, half).wait()
-        lefts, owners = [], []
-        for i in range(step * per_step, (step + 1) * per_step):
-            lefts += [near_ref[i], odd_ref[i], far_ref[i]]
-            own, other = 2 * pairs * line + 2 * i, 2 * pairs * (1 - line) + 2 * i
-            owners += [own + parity, own + 1 - parity, other + parity]
-            rest_ref[i * block : (i + 1) * block, :] = weight_rows(held_ref, [other + 1 - parity], block)
+
+    def copy(i):
+        owner = 2 * pairs * line + 2 * i + parity
+        rows = pl.ds(pl.multiple_of(owner * block, block), block)
+        return pltpu.make_async_copy(w_ref.at[:, rows, :], held_ref.at[:, pl.ds(i * block, block), :], sems.at[i])
+
+    for i in range(pairs):
+        copy(i).start()
+    for i in range(0, pairs, 4):
+        for k in range(i, i + 4):
+            copy(k).wait()
+        part = jnp.dot(
+            jnp.concatenate([near_ref[k] for k in range(i, i + 4)], axis=1),
+            side_by_side(held_ref, [k * block for k in range(i, i + 4)], block),
+            preferred_element_type=jnp.float32,
+        )
+        acc_ref[...] = part if i == 0 else acc_ref[...] + part
+
+
+def early_kernel(place_ref, first_ref, odd_ref, far_ref, w_ref, acc_ref, rest_ref, held_ref, sems):
+    line, parity = place_ref[0], place_ref[1]
+    pairs, _, block = odd_ref.shape
+
+    def copies(i):
+        own = 2 * pairs * line + 2 * i + 1 - parity
+        other = 2 * pairs * (1 - line) + 2 * i
+        one = pl.ds(pl.multiple_of(own * block, block), block)
+        two = pl.ds(pl.multiple_of(other * block, block), 2 * block)
+        at = 3 * i * block
+        return (
+            pltpu.make_async_copy(w_ref.at[:, one, :], held_ref.at[:, pl.ds(at, block), :], sems.at[i, 0]),
+            pltpu.make_async_copy(
+                w_ref.at[:, two, :], held_ref.at[:, pl.ds(at + block, 2 * block), :], sems.at[i, 1]
+            ),
+        )
+
+    for i in range(pairs):
+        for copy in copies(i):
+            copy.start()
+    for i in range(0, pairs, 2):
+        lefts, starts = [], []
+        for k in (i, i + 1):
+            for copy in copies(k):
+                copy.wait()
+            at = 3 * k * block
+            same = pl.multiple_of(at + block + parity * block, block)
+            cross = pl.multiple_of(at + 2 * block - parity * block, block)
+            lefts += [odd_ref[k], far_ref[k]]
+            starts += [at, same]
+            rest_ref[k * block : (k + 1) * block, :] = side_by_side(held_ref, [cross], block)
         part = jnp.dot(
             jnp.concatenate(lefts, axis=1),
-            weight_rows(held_ref, owners, block),
+            side_by_side(held_ref, starts, block),
             preferred_element_type=jnp.float32,
         )
-        acc_ref[...] = part if step == 0 else acc_ref[...] + part
+        acc_ref[...] = (first_ref[...] if i == 0 else acc_ref[...]) + part
 
 
 def project_kernel(
@@ -235,7 +265,7 @@
     out_ref[...] = value_ref[...].astype(out_ref.dtype)
 
 
-def gather_features(features, *ready):
+def gather_features(features, prepare):
     shard_count = lax.axis_size("shard")
     line = shard_count // 2
     pairs = line // 2
@@ -246,12 +276,13 @@
     few = 3 * pairs // 8
 
     near = lax.all_gather(features, "shard", axis=0, axis_index_groups=groups)
+    ready = prepare(near)
     far = lax.ppermute(near, "shard", across)
     odd = lax.ppermute(near, "shard", up)
     far, *ready = lax.optimization_barrier((far, *ready))
     far_up = lax.ppermute(far[:few], "shard", up)
     far_down = lax.ppermute(far[few:], "shard", down)
-    return (near, odd, far, far_up, far_down), ready
+    return (odd, far, far_up, far_down), ready
 
 
 def shards(features, in_proj, short_filter, residue, decay_rate, skip_gain):
@@ -283,26 +314,44 @@
         name="tables",
     )(decay_rate, residue)
 
-    pieces, (h, e, gain) = gather_features(features, *tables)
     place = jnp.stack([at // line, at % 2]).astype(jnp.int32)
-    near, odd, far, far_up, far_down = pieces
     hbm = pl.BlockSpec(memory_space=pltpu.HBM)
-    pairs, _, block = near.shape
+    pairs, block = line // 2, features.shape[1]
+    total_shape = jax.ShapeDtypeStruct((length, 3 * channels), f32)
+    w_far = pltpu.with_memory_space_constraint(w_branch, pltpu.HBM)
+
+    def prepare(near):
+        begun = pl.pallas_call(
+            first_kernel,
+            in_specs=[smem, vmem, hbm],
+            out_specs=vmem,
+            out_shape=total_shape,
+            scratch_shapes=[
+                pltpu.VMEM((3, pairs * block, channels), w_branch.dtype),
+                pltpu.SemaphoreType.DMA((pairs,)),
+            ],
+            compiler_params=params(8),
+            name="begin",
+        )(place, near, w_far)
+        return (begun, *tables)
+
+    pieces, (begun, h, e, gain) = gather_features(features, prepare)
+    odd, far, far_up, far_down = pieces
     early, rest = pl.pallas_call(
         early_kernel,
         in_specs=[smem] + [vmem] * 3 + [hbm],
         out_specs=(vmem,) * 2,
         out_shape=(
-            jax.ShapeDtypeStruct((length, 3 * channels), f32),
+            total_shape,
             jax.ShapeDtypeStruct((pairs * block, 3 * channels), w_branch.dtype),
         ),
         scratch_shapes=[
-            pltpu.VMEM(w_branch.shape, w_branch.dtype),
-            pltpu.SemaphoreType.DMA((pairs // 2, 2)),
+            pltpu.VMEM((3, 3 * pairs * block, channels), w_branch.dtype),
+            pltpu.SemaphoreType.DMA((pairs, 2)),
         ],
-        compiler_params=params(14),
+        compiler_params=params(12),
         name="early",
-    )(place, near, odd, far, pltpu.with_memory_space_constraint(w_branch, pltpu.HBM))
+    )(place, begun, odd, far, w_far)
     lead, drive, message = pl.pallas_call(
         functools.partial(project_kernel, modes, length, total),
         in_specs=[vmem] * 7,

time: 79.4 us -> 80.1 us (level)
  Pallas kernels: 7.21 us -> 9.3 us
  waiting for transfers between devices: 10.7 us -> 9.84 us
    pallas_call x0 -> x1, Pallas kernels: none -> 2.23 us  [prepare(): pl.pallas_call(first_kernel, in_specs=[smem, vmem, hbm], out_specs=vmem,...]
    unnamed x10 -> x8, local copies, waits for them, and re-layouts: 1.4 us -> 0.02 us
    ppermute x1, waiting for transfers between devices: 1.83 us -> 0.87 us  [gather_features(): far = lax.ppermute(near, 'shard', across)]
  transfers between devices with their start and end apart: 5 -> 5, of which waited for: 3 -> 3; matrix products, arithmetic and copies ran while one was open for 0% -> 1% of each run, Pallas kernels for 6% -> 9%
where the time goes in v8:
time: 80.1 us; the launch traced here: 79.8 us
  blocking collectives  33.5 us (42%)
  starting transfers between devices  26.2 us (33%)
  waiting for transfers between devices  9.84 us (12%)
  Pallas kernels  9.3 us (12%)
    all_gather x1, blocking collectives, gather_features(): near = lax.all_gather(features, 'shard', axis=0, axis_index_groups=groups)  33.5 us
    all_to_all x1, starting transfers between devices, shards(): lax.all_to_all(message, 'seq', 0, 0).reshape(seq_count * ROWS, channels)  13.3 us
    all_to_all x1, waiting for transfers between devices, shards(): lax.all_to_all(message, 'seq', 0, 0).reshape(seq_count * ROWS, channels)  7.5 us
    ppermute x1, starting transfers between devices, gather_features(): far_up = lax.ppermute(far[:few], 'shard', up)  4.42 us
    ppermute x1, starting transfers between devices, gather_features(): odd = lax.ppermute(near, 'shard', up)  3.28 us
    ppermute x1, starting transfers between devices, gather_features(): far = lax.ppermute(near, 'shard', across)  3.19 us
    pallas_call x1, Pallas kernels, shards(): pl.pallas_call(early_kernel, in_specs=[smem] + [vmem] * 3 + [hbm], out_sp...  3.1 us
    pallas_call x1, Pallas kernels, prepare(): pl.pallas_call(first_kernel, in_specs=[smem, vmem, hbm], out_specs=vmem,...  2.23 us
  transfers between devices with their start and end apart: 5, of which 3 were waited for; matrix products, arithmetic and copies ran while one was open for 1% of the time, Pallas kernels for 9%

profile of v8, /device:TPU:1, one launch (start us, length us, event | category | flops | bytes accessed | tf_op | source)
XLA Modules:
  0.0 79.8 jit_solution(16994492650455398455)
XLA Ops:
  0.0 0.0 copy-start
  0.0 0.0 copy-start.1
  0.0 0.0 copy-start.2
  0.0 33.5 %all-gather = bf16[2048,128]{1,0:T(8,128)(2,1)S(1)} all-gather(bf16[256,128]{1,0:T(8,128)(2,1)} %param.6), channel_id=2, replica_groups={{0,2,4,6,8,10,12,14},{1,3,5,7,9,11,13,15},{16,18,20,22,24,26,28,30},{17..., dimensions={0}, use_global_device_ids=true | all-gather | bytes 589824 | tf_op jit(solution)/shard_map/all_gather | solution.py:278
  33.5 3.2 %collective-permute-start = (bf16[8,256,128]{2,1,0:T(8,128)(2,1)S(1)}, bf16[8,256,128]{2,1,0:T(8,128)(2,1)S(1)}, u32[]{:S(2)}, u32[]{:S(2)}) collective-permute-start(bf16[8,256,128]{2,1,0:T(8,128)(2,1)S(1)} %bitcast.7), channel_id=1, source_target_pairs={{0,16},{1,17},{2,18},{3,19},{4,20},{5,21},{6,22},{7,23},{8,24},{9,... | collective-permute-start | bytes 1572872 | tf_op jit(solution)/shard_map/ppermute | solution.py:280
  36.7 3.3 %collective-permute-start.1 = (bf16[8,256,128]{2,1,0:T(8,128)(2,1)S(1)}, bf16[8,256,128]{2,1,0:T(8,128)(2,1)S(1)}, u32[]{:S(2)}, u32[]{:S(2)}) collective-permute-start(bf16[8,256,128]{2,1,0:T(8,128)(2,1)S(1)} %bitcast.8), channel_id=1, source_target_pairs={{0,15},{1,0},{2,1},{3,2},{4,3},{5,4},{6,5},{7,6},{8,7},{9,8},{10,9... | collective-permute-start | bytes 1572872 | tf_op jit(solution)/shard_map/ppermute | solution.py:281
  40.0 0.1 pad_add_fusion.place_ref
  40.1 2.2 %begin.1.first_ref = f32[256,384]{1,0:T(8,128)S(1)} custom-call(s32[2]{0:T(128)S(1)} %pad_add_fusion.place_ref, bf16[8,256,128]{2,1,0:T(8,128)(2,1)S(1)} %bitcast.9, bf16[3,4096,128]{2,1,0:T(8,128)(2,1)} %bitcast.13), custom_call_target="tpu_custom_call" | custom-call | tf_op jit(solution)/shard_map/begin/pallas_call | solution.py:324
  42.3 0.0 copy-done.1
  42.3 0.0 copy-done.2
  42.3 0.2 tables.1
  42.5 0.9 %collective-permute-done.far_ref = bf16[8,256,128]{2,1,0:T(8,128)(2,1)S(1)} collective-permute-done((bf16[8,256,128]{2,1,0:T(8,128)(2,1)S(1)}, bf16[8,256,128]{2,1,0:T(8,128)(2,1)S(1)}, u32[]{:S(2)}, u32[]{:S(2)}) %collective-permute-start) | collective-permute-done | bytes 524320 | tf_op jit(solution)/shard_map/ppermute | solution.py:280
  43.4 2.1 %collective-permute-start.3 = (bf16[5,256,128]{2,1,0:T(8,128)(2,1)S(1)}, bf16[5,256,128]{2,1,0:T(8,128)(2,1)S(1)}, u32[]{:S(2)}, u32[]{:S(2)}) collective-permute-start(bf16[5,256,128]{2,1,0:T(8,128)(2,1)S(1)} %slice.7), channel_id=1, source_target_pairs={{0,1},{1,2},{2,3},{3,4},{4,5},{5,6},{6,7},{7,8},{8,9},{9,10},{10,1... | collective-permute-start | bytes 983048 | tf_op jit(solution)/shard_map/ppermute | solution.py:284
  45.5 0.7 slice.6
  46.2 4.4 %collective-permute-start.2 = (bf16[3,256,128]{2,1,0:T(8,128)(2,1)}, bf16[3,256,128]{2,1,0:T(8,128)(2,1)S(1)}, u32[]{:S(2)}, u32[]{:S(2)}) collective-permute-start(bf16[3,256,128]{2,1,0:T(8,128)(2,1)} %slice.6), channel_id=1, source_target_pairs={{0,15},{1,0},{2,1},{3,2},{4,3},{5,4},{6,5},{7,6},{8,7},{9,8},{10,9... | collective-permute-start | bytes 589832 | tf_op jit(solution)/shard_map/ppermute | solution.py:283
  50.6 0.0 copy-done
  50.6 0.0 copy-start.3
  50.7 0.0 collective-permute-done.1.odd_ref
  50.7 3.1 %early.1 = (f32[256,384]{1,0:T(8,128)S(1)}, bf16[1024,384]{1,0:T(8,128)(2,1)S(1)}) custom-call(s32[2]{0:T(128)S(1)} %pad_add_fusion.place_ref, f32[256,384]{1,0:T(8,128)S(1)} %begin.1.first_ref, bf16[8,256,128]{2,1,0:T(8,128)(2,1)S(1)} %collective-permute-done.1.odd_ref, bf16[8,256,128]{2,1,0:T(8,128)(2,1)S(1)} %collective-permute-done.far_ref, ...), custom_call_target="tpu_custom_call" | custom-call | tf_op jit(solution)/shard_map/early/pallas_call | solution.py:340
  53.8 1.5 %collective-permute-done.2.far_up_ref = bf16[3,256,128]{2,1,0:T(8,128)(2,1)S(1)} collective-permute-done((bf16[3,256,128]{2,1,0:T(8,128)(2,1)}, bf16[3,256,128]{2,1,0:T(8,128)(2,1)S(1)}, u32[]{:S(2)}, u32[]{:S(2)}) %collective-permute-start.2) | collective-permute-done | bytes 196640 | tf_op jit(solution)/shard_map/ppermute | solution.py:283
  55.3 0.0 collective-permute-done.3.far_down_ref
  55.3 1.4 %project.1 = (f32[264,128]{1,0:T(8,128)S(1)}, f32[256,128]{1,0:T(8,128)S(1)}, f32[16,32,128]{2,1,0:T(8,128)}) custom-call(f32[256,384]{1,0:T(8,128)S(1)} %get-tuple-element.25.early_ref, bf16[1024,384]{1,0:T(8,128)(2,1)S(1)} %get-tuple-element.26.rest_ref, bf16[3,256,128]{2,1,0:T(8,128)(2,1)S(1)} %collective-permute-done.2.far_up_ref, ...), custom_call_target="tpu_custom_call" | custom-call | tf_op jit(solution)/shard_map/project/pallas_call | solution.py:355
  56.7 13.3 %all-to-all-start = ((f32[16,32,128]{2,1,0:T(8,128)}), f32[16,32,128]{2,1,0:T(8,128)S(1)}, u32[]{:S(2)}, u32[]{:S(2)}) async-start(f32[16,32,128]{2,1,0:T(8,128)} %get-tuple-element.28), calls=%async_computation | async-start | bytes 524288 | tf_op jit(solution)/shard_map/all_to_all | solution.py:372
  70.0 0.0 copy-done.3
  70.0 1.4 %conv.1 = (f32[256,128]{1,0:T(8,128)S(1)}, f32[256,128]{1,0:T(8,128)S(1)}) custom-call(f32[256,128]{1,0:T(8,128)S(1)} %get-tuple-element.29.drive_ref, f32[264,128]{1,0:T(8,128)S(1)} %get-tuple-element.30.h_ref, f32[1,128]{1,0:T(1,128)S(1)} %bitcast.11, f32[264,128]{1,0:T(8,128)S(1)} %get-tuple-element.31.lead_ref, f32[9,128]{1,0:T(8,128)S(1)} %reshape.13.taps_ref), custom_call_target="tpu_custom_call" | custom-call | tf_op jit(solution)/shard_map/conv/pallas_call | solution.py:374
  71.4 7.5 %all-to-all-done = f32[16,32,128]{2,1,0:T(8,128)S(1)} async-done(((f32[16,32,128]{2,1,0:T(8,128)}), f32[16,32,128]{2,1,0:T(8,128)S(1)}, u32[]{:S(2)}, u32[]{:S(2)}) %all-to-all-start) | async-done | bytes 262176 | tf_op jit(solution)/shard_map/all_to_all | solution.py:372
  78.9 0.9 %finish.1 = bf16[256,128]{1,0:T(8,128)(2,1)} custom-call(s32[1]{0:T(128)} %bitcast.me_ref, f32[512,128]{1,0:T(8,128)S(1)} %bitcast.10, f32[256,128]{1,0:T(8,128)S(1)} %get-tuple-element.32.first_ref, f32[256,128]{1,0:T(8,128)S(1)} %get-tuple-element.33.conv_ref, f32[9,128]{1,0:T(8,128)S(1)} %reshape.13.taps_ref, f32[16,128]{1,0:T(8,128)S(1)} %copy-done.1, ...), custom_call_target="tpu_custom_call" | custom-call | tf_op jit(solution)/shard_map/finish/pallas_call | solution.py:388
  (3 shorter events, 0.0 us)
Async XLA Ops:
  0.0 50.6 %copy-start = (f32[3,3,4096]{2,1,0:T(4,128)S(1)}, f32[3,3,4096]{2,1,0:T(4,128)}, u32[]{:S(2)}) copy-start(f32[3,3,4096]{2,1,0:T(4,128)} %param.8) | copy-start | bytes 442372
  0.0 42.3 %copy-start.1 = (f32[16,128]{1,0:T(8,128)S(1)}, f32[16,128]{1,0:T(8,128)}, u32[]{:S(2)}) copy-start(f32[16,128]{1,0:T(8,128)} %rate_ref.5) | copy-start | bytes 24580
  0.0 42.3 %copy-start.2 = (f32[16,128]{1,0:T(8,128)S(1)}, f32[16,128]{1,0:T(8,128)}, u32[]{:S(2)}) copy-start(f32[16,128]{1,0:T(8,128)} %residue_ref.1) | copy-start | bytes 24580
  33.5 9.9 %collective-permute-start = (bf16[8,256,128]{2,1,0:T(8,128)(2,1)S(1)}, bf16[8,256,128]{2,1,0:T(8,128)(2,1)S(1)}, u32[]{:S(2)}, u32[]{:S(2)}) collective-permute-start(bf16[8,256,128]{2,1,0:T(8,128)(2,1)S(1)} %bitcast.7), channel_id=1, source_target_pairs={{0,16},{1,17},{2,18},{3,19},{4,20},{5,21},{6,22},{7,23},{8,24},{9,... | collective-permute-start | bytes 1572872 | tf_op jit(solution)/shard_map/ppermute | solution.py:280
  36.7 14.0 %collective-permute-start.1 = (bf16[8,256,128]{2,1,0:T(8,128)(2,1)S(1)}, bf16[8,256,128]{2,1,0:T(8,128)(2,1)S(1)}, u32[]{:S(2)}, u32[]{:S(2)}) collective-permute-start(bf16[8,256,128]{2,1,0:T(8,128)(2,1)S(1)} %bitcast.8), channel_id=1, source_target_pairs={{0,15},{1,0},{2,1},{3,2},{4,3},{5,4},{6,5},{7,6},{8,7},{9,8},{10,9... | collective-permute-start | bytes 1572872 | tf_op jit(solution)/shard_map/ppermute | solution.py:281
  43.4 11.8 %collective-permute-start.3 = (bf16[5,256,128]{2,1,0:T(8,128)(2,1)S(1)}, bf16[5,256,128]{2,1,0:T(8,128)(2,1)S(1)}, u32[]{:S(2)}, u32[]{:S(2)}) collective-permute-start(bf16[5,256,128]{2,1,0:T(8,128)(2,1)S(1)} %slice.7), channel_id=1, source_target_pairs={{0,1},{1,2},{2,3},{3,4},{4,5},{5,6},{6,7},{7,8},{8,9},{9,10},{10,1... | collective-permute-start | bytes 983048 | tf_op jit(solution)/shard_map/ppermute | solution.py:284
  46.2 9.1 %collective-permute-start.2 = (bf16[3,256,128]{2,1,0:T(8,128)(2,1)}, bf16[3,256,128]{2,1,0:T(8,128)(2,1)S(1)}, u32[]{:S(2)}, u32[]{:S(2)}) collective-permute-start(bf16[3,256,128]{2,1,0:T(8,128)(2,1)} %slice.6), channel_id=1, source_target_pairs={{0,15},{1,0},{2,1},{3,2},{4,3},{5,4},{6,5},{7,6},{8,7},{9,8},{10,9... | collective-permute-start | bytes 589832 | tf_op jit(solution)/shard_map/ppermute | solution.py:283
  50.6 19.3 %copy-start.3 = (f32[128]{0:T(128)S(1)}, f32[128]{0:T(128)}, u32[]{:S(2)}) copy-start(f32[128]{0:T(128)} %param.11) | copy-start | bytes 1540
  56.7 22.2 %all-to-all-start = ((f32[16,32,128]{2,1,0:T(8,128)}), f32[16,32,128]{2,1,0:T(8,128)S(1)}, u32[]{:S(2)}, u32[]{:S(2)}) async-start(f32[16,32,128]{2,1,0:T(8,128)} %get-tuple-element.28), calls=%async_computation | async-start | bytes 524288 | tf_op jit(solution)/shard_map/all_to_all | solution.py:372

commit v9 on v7

--- a/solution.py
+++ b/solution.py
@@ -22,7 +22,7 @@
     return z * (1.0 - z * value)
 
 
-def tables_kernel(modes, length, total, rate_ref, residue_ref, h_ref, e_ref, gain_ref):
+def tables(modes, length, total, rate_ref, residue_ref, h_ref, e_ref, gain_ref):
     tiles = length // TILE
     rate = rate_ref[...]
     step = rate * (1.0 / total)
@@ -47,9 +47,13 @@
     return jnp.concatenate(rows, axis=0)
 
 
-def early_kernel(place_ref, near_ref, odd_ref, far_ref, w_ref, acc_ref, rest_ref, held_ref, sems):
+def early_kernel(
+    modes, length, total, place_ref, near_ref, odd_ref, far_low_ref, far_high_ref, rate_ref, residue_ref,
+    w_ref, acc_ref, rest_ref, h_ref, e_ref, gain_ref, held_ref, modes_ref, sems, mode_sems,
+):
     line, parity = place_ref[0], place_ref[1]
     pairs, _, block = near_ref.shape
+    few = far_low_ref.shape[0]
     steps = sems.shape[0]
     per_step = pairs // steps
     depth = 2 * per_step * block
@@ -58,15 +62,24 @@
         rows = pl.ds(half * 2 * pairs * block + step * depth, depth)
         return pltpu.make_async_copy(w_ref.at[:, rows, :], held_ref.at[:, rows, :], sems.at[step, half])
 
+    small = [
+        pltpu.make_async_copy(ref, modes_ref.at[k], mode_sems.at[k])
+        for k, ref in enumerate((rate_ref, residue_ref))
+    ]
+    for each in small:
+        each.start()
     for step in range(steps):
         for half in range(2):
             copy(step, half).start()
+    for each in small:
+        each.wait()
+    tables(modes, length, total, modes_ref.at[0], modes_ref.at[1], h_ref, e_ref, gain_ref)
     for step in range(steps):
         for half in range(2):
             copy(step, half).wait()
         lefts, owners = [], []
         for i in range(step * per_step, (step + 1) * per_step):
-            lefts += [near_ref[i], odd_ref[i], far_ref[i]]
+            lefts += [near_ref[i], odd_ref[i], far_low_ref[i] if i < few else far_high_ref[i - few]]
             own, other = 2 * pairs * line + 2 * i, 2 * pairs * (1 - line) + 2 * i
             owners += [own + parity, own + 1 - parity, other + parity]
             rest_ref[i * block : (i + 1) * block, :] = weight_rows(held_ref, [other + 1 - parity], block)
@@ -235,7 +248,7 @@
     out_ref[...] = value_ref[...].astype(out_ref.dtype)
 
 
-def gather_features(features, *ready):
+def gather_features(features):
     shard_count = lax.axis_size("shard")
     line = shard_count // 2
     pairs = line // 2
@@ -246,12 +259,12 @@
     few = 3 * pairs // 8
 
     near = lax.all_gather(features, "shard", axis=0, axis_index_groups=groups)
-    far = lax.ppermute(near, "shard", across)
+    far_high = lax.ppermute(near[few:], "shard", across)
     odd = lax.ppermute(near, "shard", up)
-    far, *ready = lax.optimization_barrier((far, *ready))
-    far_up = lax.ppermute(far[:few], "shard", up)
-    far_down = lax.ppermute(far[few:], "shard", down)
-    return (near, odd, far, far_up, far_down), ready
+    far_low = lax.ppermute(near[:few], "shard", across)
+    far_down = lax.ppermute(far_high, "shard", down)
+    far_up = lax.ppermute(far_low, "shard", up)
+    return near, odd, far_low, far_high, far_up, far_down
 
 
 def shards(features, in_proj, short_filter, residue, decay_rate, skip_gain):
@@ -272,37 +285,30 @@
     w_branch = in_proj.transpose(1, 0, 2)
     at = lax.axis_index("shard")
     taps = lax.dynamic_slice_in_dim(short_filter, at * channels, channels, 2).reshape(-1, channels)
-    tables = pl.pallas_call(
-        functools.partial(tables_kernel, modes, length, total),
+    place = jnp.stack([at // line, at % 2]).astype(jnp.int32)
+    near, odd, far_low, far_high, far_up, far_down = gather_features(features)
+    hbm = pl.BlockSpec(memory_space=pltpu.HBM)
+    pairs, _, block = near.shape
+    early, rest, h, e, gain = pl.pallas_call(
+        functools.partial(early_kernel, modes, length, total),
+        in_specs=[smem] + [vmem] * 4 + [hbm] * 3,
+        out_specs=(vmem,) * 5,
         out_shape=(
+            jax.ShapeDtypeStruct((length, 3 * channels), f32),
+            jax.ShapeDtypeStruct((pairs * block, 3 * channels), w_branch.dtype),
             jax.ShapeDtypeStruct((length + TILE, channels), f32),
             jax.ShapeDtypeStruct((tiles * modes, channels), f32),
             jax.ShapeDtypeStruct((modes, channels), f32),
         ),
-        compiler_params=params(4),
-        name="tables",
-    )(decay_rate, residue)
-
-    pieces, (h, e, gain) = gather_features(features, *tables)
-    place = jnp.stack([at // line, at % 2]).astype(jnp.int32)
-    near, odd, far, far_up, far_down = pieces
-    hbm = pl.BlockSpec(memory_space=pltpu.HBM)
-    pairs, _, block = near.shape
-    early, rest = pl.pallas_call(
-        early_kernel,
-        in_specs=[smem] + [vmem] * 3 + [hbm],
-        out_specs=(vmem,) * 2,
-        out_shape=(
-            jax.ShapeDtypeStruct((length, 3 * channels), f32),
-            jax.ShapeDtypeStruct((pairs * block, 3 * channels), w_branch.dtype),
-        ),
         scratch_shapes=[
             pltpu.VMEM(w_branch.shape, w_branch.dtype),
+            pltpu.VMEM((2, modes, channels), f32),
             pltpu.SemaphoreType.DMA((pairs // 2, 2)),
+            pltpu.SemaphoreType.DMA((2,)),
         ],
         compiler_params=params(14),
         name="early",
-    )(place, near, odd, far, pltpu.with_memory_space_constraint(w_branch, pltpu.HBM))
+    )(place, near, odd, far_low, far_high, *(pltpu.with_memory_space_constraint(a, pltpu.HBM) for a in (decay_rate, residue, w_branch)))
     lead, drive, message = pl.pallas_call(
         functools.partial(project_kernel, modes, length, total),
         in_specs=[vmem] * 7,

time: 79.4 us -> 80 us (level)
  waiting for transfers between devices: 10.7 us -> 12.6 us
  local copies, waits for them, and re-layouts: 1.46 us -> 0.07 us
    ppermute x3 -> x4, waiting for transfers between devices: 3.2 us -> 5.08 us  [the longest x1 4.62 us: gather_features(): far_low = lax.ppermute(near[:few], 'shard', across)]
    unnamed x10 -> x6, local copies, waits for them, and re-layouts: 1.4 us -> 0.01 us
    ppermute x3 -> x4, starting transfers between devices: 9.69 us -> 9.19 us  [the longest x1 3.2 us: gather_features(): far_high = lax.ppermute(near[few:], 'shard', across)]
    pallas_call x2 -> x1, Pallas kernels: 3.44 us -> 3.88 us  [shards(): pl.pallas_call(functools.partial(early_kernel, modes, length, total), in_...]
  transfers between devices with their start and end apart: 5 -> 6, of which waited for: 3 -> 3; matrix products, arithmetic and copies ran while one was open for 0% -> 0% of each run, Pallas kernels for 6% -> 7%
where the time goes in v9:
time: 80 us; the launch traced here: 79.7 us
  blocking collectives  33.4 us (42%)
  starting transfers between devices  25.7 us (32%)
  waiting for transfers between devices  12.6 us (16%)
  Pallas kernels  7.66 us (10%)
    all_gather x1, blocking collectives, gather_features(): near = lax.all_gather(features, 'shard', axis=0, axis_index_groups=groups)  33.4 us
    all_to_all x1, starting transfers between devices, shards(): lax.all_to_all(message, 'seq', 0, 0).reshape(seq_count * ROWS, channels)  13.2 us
    all_to_all x1, waiting for transfers between devices, shards(): lax.all_to_all(message, 'seq', 0, 0).reshape(seq_count * ROWS, channels)  7.5 us
    ppermute x1, waiting for transfers between devices, gather_features(): far_low = lax.ppermute(near[:few], 'shard', across)  4.62 us
    pallas_call x1, Pallas kernels, shards(): pl.pallas_call(functools.partial(early_kernel, modes, length, total), in_...  3.88 us
    ppermute x1, starting transfers between devices, gather_features(): odd = lax.ppermute(near, 'shard', up)  3.28 us
    ppermute x1, starting transfers between devices, gather_features(): far_high = lax.ppermute(near[few:], 'shard', across)  3.2 us
    ppermute x1, starting transfers between devices, gather_features(): far_low = lax.ppermute(near[:few], 'shard', across)  2.08 us
  transfers between devices with their start and end apart: 6, of which 3 were waited for; matrix products, arithmetic and copies ran while one was open for 0% of the time, Pallas kernels for 7%

profile of v9, /device:TPU:1, one launch (start us, length us, event | category | flops | bytes accessed | tf_op | source)
XLA Modules:
  0.0 79.7 jit_solution(4351428378323732442)
XLA Ops:
  0.0 0.0 copy-start
  0.0 0.0 copy-start.1
  0.0 33.4 %all-gather = bf16[2048,128]{1,0:T(8,128)(2,1)S(1)} all-gather(bf16[256,128]{1,0:T(8,128)(2,1)} %param.6), channel_id=2, replica_groups={{0,2,4,6,8,10,12,14},{1,3,5,7,9,11,13,15},{16,18,20,22,24,26,28,30},{17..., dimensions={0}, use_global_device_ids=true | all-gather | bytes 589824 | tf_op jit(solution)/shard_map/all_gather | solution.py:261
  33.5 3.2 %collective-permute-start.2 = (bf16[5,256,128]{2,1,0:T(8,128)(2,1)S(1)}, bf16[5,256,128]{2,1,0:T(8,128)(2,1)S(1)}, u32[]{:S(2)}, u32[]{:S(2)}) collective-permute-start(bf16[5,256,128]{2,1,0:T(8,128)(2,1)S(1)} %bitcast.15), channel_id=1, source_target_pairs={{0,16},{1,17},{2,18},{3,19},{4,20},{5,21},{6,22},{7,23},{8,24},{9,... | collective-permute-start | bytes 983048 | tf_op jit(solution)/shard_map/ppermute | solution.py:262
  36.7 3.3 %collective-permute-start = (bf16[8,256,128]{2,1,0:T(8,128)(2,1)S(1)}, bf16[8,256,128]{2,1,0:T(8,128)(2,1)S(1)}, u32[]{:S(2)}, u32[]{:S(2)}) collective-permute-start(bf16[8,256,128]{2,1,0:T(8,128)(2,1)S(1)} %bitcast.9), channel_id=1, source_target_pairs={{0,15},{1,0},{2,1},{3,2},{4,3},{5,4},{6,5},{7,6},{8,7},{9,8},{10,9... | collective-permute-start | bytes 1572872 | tf_op jit(solution)/shard_map/ppermute | solution.py:263
  40.0 2.1 %collective-permute-start.1 = (bf16[3,256,128]{2,1,0:T(8,128)(2,1)S(1)}, bf16[3,256,128]{2,1,0:T(8,128)(2,1)S(1)}, u32[]{:S(2)}, u32[]{:S(2)}) collective-permute-start(bf16[3,256,128]{2,1,0:T(8,128)(2,1)S(1)} %bitcast.16), channel_id=1, source_target_pairs={{0,16},{1,17},{2,18},{3,19},{4,20},{5,21},{6,22},{7,23},{8,24},{9,... | collective-permute-start | bytes 589832 | tf_op jit(solution)/shard_map/ppermute | solution.py:264
  42.1 0.0 collective-permute-done.2.far_high_ref
  42.1 2.0 %collective-permute-start.4 = (bf16[5,256,128]{2,1,0:T(8,128)(2,1)S(1)}, bf16[5,256,128]{2,1,0:T(8,128)(2,1)S(1)}, u32[]{:S(2)}, u32[]{:S(2)}) collective-permute-start(bf16[5,256,128]{2,1,0:T(8,128)(2,1)S(1)} %collective-permute-done.2.far_high_ref), channel_id=1, source_target_pairs={{0,1},{1,2},{2,3},{3,4},{4,5},{5,6},{6,7},{7,8},{8,9},{9,10},{10,1... | collective-permute-start | bytes 983048 | tf_op jit(solution)/shard_map/ppermute | solution.py:265
  44.1 4.6 %collective-permute-done.1.far_low_ref = bf16[3,256,128]{2,1,0:T(8,128)(2,1)S(1)} collective-permute-done((bf16[3,256,128]{2,1,0:T(8,128)(2,1)S(1)}, bf16[3,256,128]{2,1,0:T(8,128)(2,1)S(1)}, u32[]{:S(2)}, u32[]{:S(2)}) %collective-permute-start.1) | collective-permute-done | bytes 196640 | tf_op jit(solution)/shard_map/ppermute | solution.py:264
  48.7 1.9 %collective-permute-start.3 = (bf16[3,256,128]{2,1,0:T(8,128)(2,1)S(1)}, bf16[3,256,128]{2,1,0:T(8,128)(2,1)S(1)}, u32[]{:S(2)}, u32[]{:S(2)}) collective-permute-start(bf16[3,256,128]{2,1,0:T(8,128)(2,1)S(1)} %collective-permute-done.1.far_low_ref), channel_id=1, source_target_pairs={{0,15},{1,0},{2,1},{3,2},{4,3},{5,4},{6,5},{7,6},{8,7},{9,8},{10,9... | collective-permute-start | bytes 589832 | tf_op jit(solution)/shard_map/ppermute | solution.py:266
  50.7 0.0 copy-done
  50.7 0.1 pad_add_fusion.place_ref
  50.8 0.0 collective-permute-done.odd_ref
  50.8 0.0 copy-start.2
  50.8 3.9 %early.1 = (f32[256,384]{1,0:T(8,128)S(1)}, bf16[1024,384]{1,0:T(8,128)(2,1)S(1)}, f32[264,128]{1,0:T(8,128)S(1)}, f32[512,128]{1,0:T(8,128)S(1)}, f32[16,128]{1,0:T(8,128)S(1)}) custom-call(s32[2]{0:T(128)S(1)} %pad_add_fusion.place_ref, bf16[8,256,128]{2,1,0:T(8,128)(2,1)S(1)} %bitcast.10, bf16[8,256,128]{2,1,0:T(8,128)(2,1)S(1)} %collective-permute-done.odd_ref, ...), custom_call_target="tpu_custom_call" | custom-call | tf_op jit(solution)/shard_map/early/pallas_call | solution.py:292
  54.7 0.5 collective-permute-done.3.far_up_ref
  55.1 0.0 collective-permute-done.4.far_down_ref
  55.2 0.0 copy-done.1
  55.2 1.5 %project.1 = (f32[264,128]{1,0:T(8,128)S(1)}, f32[256,128]{1,0:T(8,128)S(1)}, f32[16,32,128]{2,1,0:T(8,128)}) custom-call(f32[256,384]{1,0:T(8,128)S(1)} %get-tuple-element.15.early_ref, bf16[1024,384]{1,0:T(8,128)(2,1)S(1)} %get-tuple-element.16.rest_ref, bf16[3,256,128]{2,1,0:T(8,128)(2,1)S(1)} %collective-permute-done.3.far_up_ref, ...), custom_call_target="tpu_custom_call" | custom-call | tf_op jit(solution)/shard_map/project/pallas_call | solution.py:312
  56.6 13.2 %all-to-all-start = ((f32[16,32,128]{2,1,0:T(8,128)}), f32[16,32,128]{2,1,0:T(8,128)S(1)}, u32[]{:S(2)}, u32[]{:S(2)}) async-start(f32[16,32,128]{2,1,0:T(8,128)} %get-tuple-element.18), calls=%async_computation | async-start | bytes 524288 | tf_op jit(solution)/shard_map/all_to_all | solution.py:329
  69.8 0.0 copy-done.2
  69.8 1.4 %conv.1 = (f32[256,128]{1,0:T(8,128)S(1)}, f32[256,128]{1,0:T(8,128)S(1)}) custom-call(f32[256,128]{1,0:T(8,128)S(1)} %get-tuple-element.19.drive_ref, f32[264,128]{1,0:T(8,128)S(1)} %get-tuple-element.20.h_ref, f32[1,128]{1,0:T(1,128)S(1)} %bitcast.12, f32[264,128]{1,0:T(8,128)S(1)} %get-tuple-element.21.lead_ref, f32[9,128]{1,0:T(8,128)S(1)} %reshape.13.taps_ref), custom_call_target="tpu_custom_call" | custom-call | tf_op jit(solution)/shard_map/conv/pallas_call | solution.py:331
  71.2 7.5 %all-to-all-done = f32[16,32,128]{2,1,0:T(8,128)S(1)} async-done(((f32[16,32,128]{2,1,0:T(8,128)}), f32[16,32,128]{2,1,0:T(8,128)S(1)}, u32[]{:S(2)}, u32[]{:S(2)}) %all-to-all-start) | async-done | bytes 262176 | tf_op jit(solution)/shard_map/all_to_all | solution.py:329
  78.7 0.9 %finish.1 = bf16[256,128]{1,0:T(8,128)(2,1)} custom-call(s32[1]{0:T(128)} %bitcast.me_ref, f32[512,128]{1,0:T(8,128)S(1)} %bitcast.11, f32[256,128]{1,0:T(8,128)S(1)} %get-tuple-element.22.first_ref, f32[256,128]{1,0:T(8,128)S(1)} %get-tuple-element.23.conv_ref, f32[9,128]{1,0:T(8,128)S(1)} %reshape.13.taps_ref, f32[16,128]{1,0:T(8,128)S(1)} %copy-done.1, ...), custom_call_target="tpu_custom_call" | custom-call | tf_op jit(solution)/shard_map/finish/pallas_call | solution.py:345
  (4 shorter events, 0.1 us)
Async XLA Ops:
  0.0 50.7 %copy-start = (f32[3,3,4096]{2,1,0:T(4,128)S(1)}, f32[3,3,4096]{2,1,0:T(4,128)}, u32[]{:S(2)}) copy-start(f32[3,3,4096]{2,1,0:T(4,128)} %param.8) | copy-start | bytes 442372
  0.0 55.2 %copy-start.1 = (f32[16,128]{1,0:T(8,128)S(1)}, f32[16,128]{1,0:T(8,128)}, u32[]{:S(2)}) copy-start(f32[16,128]{1,0:T(8,128)} %rate_ref.5) | copy-start | bytes 24580
  33.5 8.6 %collective-permute-start.2 = (bf16[5,256,128]{2,1,0:T(8,128)(2,1)S(1)}, bf16[5,256,128]{2,1,0:T(8,128)(2,1)S(1)}, u32[]{:S(2)}, u32[]{:S(2)}) collective-permute-start(bf16[5,256,128]{2,1,0:T(8,128)(2,1)S(1)} %bitcast.15), channel_id=1, source_target_pairs={{0,16},{1,17},{2,18},{3,19},{4,20},{5,21},{6,22},{7,23},{8,24},{9,... | collective-permute-start | bytes 983048 | tf_op jit(solution)/shard_map/ppermute | solution.py:262
  36.7 14.1 %collective-permute-start = (bf16[8,256,128]{2,1,0:T(8,128)(2,1)S(1)}, bf16[8,256,128]{2,1,0:T(8,128)(2,1)S(1)}, u32[]{:S(2)}, u32[]{:S(2)}) collective-permute-start(bf16[8,256,128]{2,1,0:T(8,128)(2,1)S(1)} %bitcast.9), channel_id=1, source_target_pairs={{0,15},{1,0},{2,1},{3,2},{4,3},{5,4},{6,5},{7,6},{8,7},{9,8},{10,9... | collective-permute-start | bytes 1572872 | tf_op jit(solution)/shard_map/ppermute | solution.py:263
  40.0 8.7 %collective-permute-start.1 = (bf16[3,256,128]{2,1,0:T(8,128)(2,1)S(1)}, bf16[3,256,128]{2,1,0:T(8,128)(2,1)S(1)}, u32[]{:S(2)}, u32[]{:S(2)}) collective-permute-start(bf16[3,256,128]{2,1,0:T(8,128)(2,1)S(1)} %bitcast.16), channel_id=1, source_target_pairs={{0,16},{1,17},{2,18},{3,19},{4,20},{5,21},{6,22},{7,23},{8,24},{9,... | collective-permute-start | bytes 589832 | tf_op jit(solution)/shard_map/ppermute | solution.py:264
  42.1 13.1 %collective-permute-start.4 = (bf16[5,256,128]{2,1,0:T(8,128)(2,1)S(1)}, bf16[5,256,128]{2,1,0:T(8,128)(2,1)S(1)}, u32[]{:S(2)}, u32[]{:S(2)}) collective-permute-start(bf16[5,256,128]{2,1,0:T(8,128)(2,1)S(1)} %collective-permute-done.2.far_high_ref), channel_id=1, source_target_pairs={{0,1},{1,2},{2,3},{3,4},{4,5},{5,6},{6,7},{7,8},{8,9},{9,10},{10,1... | collective-permute-start | bytes 983048 | tf_op jit(solution)/shard_map/ppermute | solution.py:265
  48.7 6.4 %collective-permute-start.3 = (bf16[3,256,128]{2,1,0:T(8,128)(2,1)S(1)}, bf16[3,256,128]{2,1,0:T(8,128)(2,1)S(1)}, u32[]{:S(2)}, u32[]{:S(2)}) collective-permute-start(bf16[3,256,128]{2,1,0:T(8,128)(2,1)S(1)} %collective-permute-done.1.far_low_ref), channel_id=1, source_target_pairs={{0,15},{1,0},{2,1},{3,2},{4,3},{5,4},{6,5},{7,6},{8,7},{9,8},{10,9... | collective-permute-start | bytes 589832 | tf_op jit(solution)/shard_map/ppermute | solution.py:266
  50.8 19.0 %copy-start.2 = (f32[128]{0:T(128)S(1)}, f32[128]{0:T(128)}, u32[]{:S(2)}) copy-start(f32[128]{0:T(128)} %param.11) | copy-start | bytes 1540
  56.6 22.1 %all-to-all-start = ((f32[16,32,128]{2,1,0:T(8,128)}), f32[16,32,128]{2,1,0:T(8,128)S(1)}, u32[]{:S(2)}, u32[]{:S(2)}) async-start(f32[16,32,128]{2,1,0:T(8,128)} %get-tuple-element.18), calls=%async_computation | async-start | bytes 524288 | tf_op jit(solution)/shard_map/all_to_all | solution.py:329

commit v10 on v7

--- a/solution.py
+++ b/solution.py
@@ -298,7 +298,7 @@
         ),
         scratch_shapes=[
             pltpu.VMEM(w_branch.shape, w_branch.dtype),
-            pltpu.SemaphoreType.DMA((pairs // 2, 2)),
+            pltpu.SemaphoreType.DMA((pairs, 2)),
         ],
         compiler_params=params(14),
         name="early",

time: 79.4 us -> 79.8 us (level)
  transfers between devices with their start and end apart: 5 -> 5, of which waited for: 3 -> 3; matrix products, arithmetic and copies ran while one was open for 0% -> 0% of each run, Pallas kernels for 6% -> 7%
where the time goes in v10:
time: 79.8 us; the launch traced here: 79.3 us
  blocking collectives  33.4 us (42%)
  starting transfers between devices  26.3 us (33%)
  waiting for transfers between devices  10.3 us (13%)
  Pallas kernels  7.63 us (10%)
  local copies, waits for them, and re-layouts  1.46 us (2%)
    all_gather x1, blocking collectives, gather_features(): near = lax.all_gather(features, 'shard', axis=0, axis_index_groups=groups)  33.4 us
    all_to_all x1, starting transfers between devices, shards(): lax.all_to_all(message, 'seq', 0, 0).reshape(seq_count * ROWS, channels)  13.3 us
    all_to_all x1, waiting for transfers between devices, shards(): lax.all_to_all(message, 'seq', 0, 0).reshape(seq_count * ROWS, channels)  7.5 us
    ppermute x1, starting transfers between devices, gather_features(): far_up = lax.ppermute(far[:few], 'shard', up)  4.43 us
    pallas_call x1, Pallas kernels, shards(): pl.pallas_call(early_kernel, in_specs=[smem] + [vmem] * 3 + [hbm], out_sp...  3.66 us
    ppermute x1, starting transfers between devices, gather_features(): odd = lax.ppermute(near, 'shard', up)  3.28 us
    ppermute x1, starting transfers between devices, gather_features(): far = lax.ppermute(near, 'shard', across)  3.19 us
    ppermute x1, starting transfers between devices, gather_features(): far_down = lax.ppermute(far[few:], 'shard', down)  2.07 us
  transfers between devices with their start and end apart: 5, of which 3 were waited for; matrix products, arithmetic and copies ran while one was open for 0% of the time, Pallas kernels for 7%

profile of v10, /device:TPU:1, one launch (start us, length us, event | category | flops | bytes accessed | tf_op | source)
XLA Modules:
  0.0 79.3 jit_solution(7551455961334996890)
XLA Ops:
  0.0 0.0 copy-start
  0.0 0.0 copy-start.2
  0.0 33.4 %all-gather = bf16[2048,128]{1,0:T(8,128)(2,1)S(1)} all-gather(bf16[256,128]{1,0:T(8,128)(2,1)} %param.6), channel_id=2, replica_groups={{0,2,4,6,8,10,12,14},{1,3,5,7,9,11,13,15},{16,18,20,22,24,26,28,30},{17..., dimensions={0}, use_global_device_ids=true | all-gather | bytes 589824 | tf_op jit(solution)/shard_map/all_gather | solution.py:248
  33.5 3.2 %collective-permute-start.1 = (bf16[8,256,128]{2,1,0:T(8,128)(2,1)S(1)}, bf16[8,256,128]{2,1,0:T(8,128)(2,1)S(1)}, u32[]{:S(2)}, u32[]{:S(2)}) collective-permute-start(bf16[8,256,128]{2,1,0:T(8,128)(2,1)S(1)} %bitcast.7), channel_id=1, source_target_pairs={{0,16},{1,17},{2,18},{3,19},{4,20},{5,21},{6,22},{7,23},{8,24},{9,... | collective-permute-start | bytes 1572872 | tf_op jit(solution)/shard_map/ppermute | solution.py:249
  36.7 3.3 %collective-permute-start = (bf16[8,256,128]{2,1,0:T(8,128)(2,1)S(1)}, bf16[8,256,128]{2,1,0:T(8,128)(2,1)S(1)}, u32[]{:S(2)}, u32[]{:S(2)}) collective-permute-start(bf16[8,256,128]{2,1,0:T(8,128)(2,1)S(1)} %bitcast.8), channel_id=1, source_target_pairs={{0,15},{1,0},{2,1},{3,2},{4,3},{5,4},{6,5},{7,6},{8,7},{9,8},{10,9... | collective-permute-start | bytes 1572872 | tf_op jit(solution)/shard_map/ppermute | solution.py:250
  39.9 0.0 copy-start.1
  40.0 0.7 copy-done.1
  40.6 0.0 copy-start.3
  40.6 0.7 copy-done.3
  41.3 0.2 tables.1
  41.5 1.8 %collective-permute-done.1.far_ref = bf16[8,256,128]{2,1,0:T(8,128)(2,1)S(1)} collective-permute-done((bf16[8,256,128]{2,1,0:T(8,128)(2,1)S(1)}, bf16[8,256,128]{2,1,0:T(8,128)(2,1)S(1)}, u32[]{:S(2)}, u32[]{:S(2)}) %collective-permute-start.1) | collective-permute-done | bytes 524320 | tf_op jit(solution)/shard_map/ppermute | solution.py:249
  43.4 2.1 %collective-permute-start.3 = (bf16[5,256,128]{2,1,0:T(8,128)(2,1)S(1)}, bf16[5,256,128]{2,1,0:T(8,128)(2,1)S(1)}, u32[]{:S(2)}, u32[]{:S(2)}) collective-permute-start(bf16[5,256,128]{2,1,0:T(8,128)(2,1)S(1)} %slice.7), channel_id=1, source_target_pairs={{0,1},{1,2},{2,3},{3,4},{4,5},{5,6},{6,7},{7,8},{8,9},{9,10},{10,1... | collective-permute-start | bytes 983048 | tf_op jit(solution)/shard_map/ppermute | solution.py:253
  45.5 4.4 %collective-permute-start.2 = (bf16[3,256,128]{2,1,0:T(8,128)(2,1)S(1)}, bf16[3,256,128]{2,1,0:T(8,128)(2,1)S(1)}, u32[]{:S(2)}, u32[]{:S(2)}) collective-permute-start(bf16[3,256,128]{2,1,0:T(8,128)(2,1)S(1)} %slice.6), channel_id=1, source_target_pairs={{0,15},{1,0},{2,1},{3,2},{4,3},{5,4},{6,5},{7,6},{8,7},{9,8},{10,9... | collective-permute-start | bytes 589832 | tf_op jit(solution)/shard_map/ppermute | solution.py:252
  49.9 0.0 copy-done
  50.0 0.1 pad_add_fusion.place_ref
  50.1 0.0 collective-permute-done.odd_ref
  50.1 0.0 copy-start.4
  50.1 3.7 %early.1 = (f32[256,384]{1,0:T(8,128)S(1)}, bf16[1024,384]{1,0:T(8,128)(2,1)S(1)}) custom-call(s32[2]{0:T(128)S(1)} %pad_add_fusion.place_ref, bf16[8,256,128]{2,1,0:T(8,128)(2,1)S(1)} %bitcast.9, bf16[8,256,128]{2,1,0:T(8,128)(2,1)S(1)} %collective-permute-done.odd_ref, bf16[8,256,128]{2,1,0:T(8,128)(2,1)S(1)} %collective-permute-done.1.far_ref, ...), custom_call_target="tpu_custom_call" | custom-call | tf_op jit(solution)/shard_map/early/pallas_call | solution.py:291
  53.8 0.9 %collective-permute-done.2.far_up_ref = bf16[3,256,128]{2,1,0:T(8,128)(2,1)S(1)} collective-permute-done((bf16[3,256,128]{2,1,0:T(8,128)(2,1)S(1)}, bf16[3,256,128]{2,1,0:T(8,128)(2,1)S(1)}, u32[]{:S(2)}, u32[]{:S(2)}) %collective-permute-start.2) | collective-permute-done | bytes 196640 | tf_op jit(solution)/shard_map/ppermute | solution.py:252
  54.7 0.0 collective-permute-done.3.far_down_ref
  54.7 0.0 copy-done.2
  54.7 1.5 %project.1 = (f32[264,128]{1,0:T(8,128)S(1)}, f32[256,128]{1,0:T(8,128)S(1)}, f32[16,32,128]{2,1,0:T(8,128)}) custom-call(f32[256,384]{1,0:T(8,128)S(1)} %get-tuple-element.23.early_ref, bf16[1024,384]{1,0:T(8,128)(2,1)S(1)} %get-tuple-element.24.rest_ref, bf16[3,256,128]{2,1,0:T(8,128)(2,1)S(1)} %collective-permute-done.2.far_up_ref, ...), custom_call_target="tpu_custom_call" | custom-call | tf_op jit(solution)/shard_map/project/pallas_call | solution.py:306
  56.2 13.3 %all-to-all-start = ((f32[16,32,128]{2,1,0:T(8,128)}), f32[16,32,128]{2,1,0:T(8,128)S(1)}, u32[]{:S(2)}, u32[]{:S(2)}) async-start(f32[16,32,128]{2,1,0:T(8,128)} %get-tuple-element.26), calls=%async_computation | async-start | bytes 524288 | tf_op jit(solution)/shard_map/all_to_all | solution.py:323
  69.5 0.0 copy-done.4
  69.5 1.4 %conv.1 = (f32[256,128]{1,0:T(8,128)S(1)}, f32[256,128]{1,0:T(8,128)S(1)}) custom-call(f32[256,128]{1,0:T(8,128)S(1)} %get-tuple-element.27.drive_ref, f32[264,128]{1,0:T(8,128)S(1)} %get-tuple-element.28.h_ref, f32[1,128]{1,0:T(1,128)S(1)} %bitcast.11, f32[264,128]{1,0:T(8,128)S(1)} %get-tuple-element.29.lead_ref, f32[9,128]{1,0:T(8,128)S(1)} %reshape.13.taps_ref), custom_call_target="tpu_custom_call" | custom-call | tf_op jit(solution)/shard_map/conv/pallas_call | solution.py:325
  70.9 7.5 %all-to-all-done = f32[16,32,128]{2,1,0:T(8,128)S(1)} async-done(((f32[16,32,128]{2,1,0:T(8,128)}), f32[16,32,128]{2,1,0:T(8,128)S(1)}, u32[]{:S(2)}, u32[]{:S(2)}) %all-to-all-start) | async-done | bytes 262176 | tf_op jit(solution)/shard_map/all_to_all | solution.py:323
  78.4 0.9 %finish.1 = bf16[256,128]{1,0:T(8,128)(2,1)} custom-call(s32[1]{0:T(128)} %bitcast.me_ref, f32[512,128]{1,0:T(8,128)S(1)} %bitcast.10, f32[256,128]{1,0:T(8,128)S(1)} %get-tuple-element.30.first_ref, f32[256,128]{1,0:T(8,128)S(1)} %get-tuple-element.31.conv_ref, f32[9,128]{1,0:T(8,128)S(1)} %reshape.13.taps_ref, f32[16,128]{1,0:T(8,128)S(1)} %copy-done.2, ...), custom_call_target="tpu_custom_call" | custom-call | tf_op jit(solution)/shard_map/finish/pallas_call | solution.py:339
  (4 shorter events, 0.1 us)
Async XLA Ops:
  0.0 49.9 %copy-start = (f32[3,3,4096]{2,1,0:T(4,128)S(1)}, f32[3,3,4096]{2,1,0:T(4,128)}, u32[]{:S(2)}) copy-start(f32[3,3,4096]{2,1,0:T(4,128)} %param.8) | copy-start | bytes 442372
  0.0 54.7 %copy-start.2 = (f32[16,128]{1,0:T(8,128)S(1)}, f32[16,128]{1,0:T(8,128)}, u32[]{:S(2)}) copy-start(f32[16,128]{1,0:T(8,128)} %rate_ref.5) | copy-start | bytes 24580
  33.5 9.9 %collective-permute-start.1 = (bf16[8,256,128]{2,1,0:T(8,128)(2,1)S(1)}, bf16[8,256,128]{2,1,0:T(8,128)(2,1)S(1)}, u32[]{:S(2)}, u32[]{:S(2)}) collective-permute-start(bf16[8,256,128]{2,1,0:T(8,128)(2,1)S(1)} %bitcast.7), channel_id=1, source_target_pairs={{0,16},{1,17},{2,18},{3,19},{4,20},{5,21},{6,22},{7,23},{8,24},{9,... | collective-permute-start | bytes 1572872 | tf_op jit(solution)/shard_map/ppermute | solution.py:249
  36.7 13.4 %collective-permute-start = (bf16[8,256,128]{2,1,0:T(8,128)(2,1)S(1)}, bf16[8,256,128]{2,1,0:T(8,128)(2,1)S(1)}, u32[]{:S(2)}, u32[]{:S(2)}) collective-permute-start(bf16[8,256,128]{2,1,0:T(8,128)(2,1)S(1)} %bitcast.8), channel_id=1, source_target_pairs={{0,15},{1,0},{2,1},{3,2},{4,3},{5,4},{6,5},{7,6},{8,7},{9,8},{10,9... | collective-permute-start | bytes 1572872 | tf_op jit(solution)/shard_map/ppermute | solution.py:250
  39.9 0.7 copy-start.1
  40.6 0.7 copy-start.3
  43.4 11.3 %collective-permute-start.3 = (bf16[5,256,128]{2,1,0:T(8,128)(2,1)S(1)}, bf16[5,256,128]{2,1,0:T(8,128)(2,1)S(1)}, u32[]{:S(2)}, u32[]{:S(2)}) collective-permute-start(bf16[5,256,128]{2,1,0:T(8,128)(2,1)S(1)} %slice.7), channel_id=1, source_target_pairs={{0,1},{1,2},{2,3},{3,4},{4,5},{5,6},{6,7},{7,8},{8,9},{9,10},{10,1... | collective-permute-start | bytes 983048 | tf_op jit(solution)/shard_map/ppermute | solution.py:253
  45.5 9.2 %collective-permute-start.2 = (bf16[3,256,128]{2,1,0:T(8,128)(2,1)S(1)}, bf16[3,256,128]{2,1,0:T(8,128)(2,1)S(1)}, u32[]{:S(2)}, u32[]{:S(2)}) collective-permute-start(bf16[3,256,128]{2,1,0:T(8,128)(2,1)S(1)} %slice.6), channel_id=1, source_target_pairs={{0,15},{1,0},{2,1},{3,2},{4,3},{5,4},{6,5},{7,6},{8,7},{9,8},{10,9... | collective-permute-start | bytes 589832 | tf_op jit(solution)/shard_map/ppermute | solution.py:252
  50.1 19.4 %copy-start.4 = (f32[128]{0:T(128)S(1)}, f32[128]{0:T(128)}, u32[]{:S(2)}) copy-start(f32[128]{0:T(128)} %param.11) | copy-start | bytes 1540
  56.2 22.2 %all-to-all-start = ((f32[16,32,128]{2,1,0:T(8,128)}), f32[16,32,128]{2,1,0:T(8,128)S(1)}, u32[]{:S(2)}, u32[]{:S(2)}) async-start(f32[16,32,128]{2,1,0:T(8,128)} %get-tuple-element.26), calls=%async_computation | async-start | bytes 524288 | tf_op jit(solution)/shard_map/all_to_all | solution.py:323
